TPU v7x, 512 devices: a whole 4x4x16 slice. The times are simulated.
512 devices in a mesh: dp: 16 (over z), expert: 32 (over x, y, core).
Axes of the slice: x: 4, y: 4, z: 16, core: 2. Of those that a mesh axis runs over, the one named last changes fastest.
Arguments:
- first_out: bfloat16 [65536, 1024], P(('dp', 'expert')), may hold values from -6 to 6
- second_out: bfloat16 [65536, 1024], P(('dp', 'expert')), may hold values from -6 to 6
- first_grad: bfloat16 [65536, 1024], P(('dp', 'expert')), may hold values from -6 to 6
- second_grad: bfloat16 [65536, 1024], P(('dp', 'expert')), may hold values from -6 to 6
- routes: int32 [65536, 2], P(('dp', 'expert')), may hold values from 0 to 31, all different within a row; in each aligned block of 128 rows (0 to 127, 128 to 255, ...) at most 16 rows name the same one
- gate_values: float32 [65536, 2], P(('dp', 'expert')), may hold values from 0.1 to 1
- w_gate: bfloat16 [32, 1024, 768], P('expert', 'dp'), may hold values from -0.1875 to 0.1875
- w_up: bfloat16 [32, 1024, 768], P('expert', 'dp'), may hold values from -0.1875 to 0.1875
- w_down: bfloat16 [32, 1024, 768], P('expert', 'dp'), may hold values from -0.21875 to 0.21875
Outputs:
- second_in: bfloat16 [65536, 1024], P(('dp', 'expert'))
- first_total: bfloat16 [65536, 1024], P(('dp', 'expert'))
- gate_grad: float32 [65536, 2], P(('dp', 'expert'))
- w_down_grad: float32 [32, 1024, 768], P('expert', 'dp')
Inputs may be any that keep to these rules, and one draw needn't show every extreme that they name: `routes`: each row names 2 different experts. Among the 128 rows of one device no expert is named more than 16 times, and in every draw some device names some expert exactly 16 times.
All inputs are finite; a program needn't handle non-finite values.
Results may differ from a plain program's by a relative error of at most 0.0051.
Values may be sent and summed in bfloat16 or wider, within the bound.
No kernel may reach another device: no remote copies, remote signals or barrier semaphores. Data moves between devices by JAX's collectives and lax.ppermute only.
A program may use at most 64 MiB of HBM per device.

v0:
```python
import math

import jax
import jax.numpy as jnp
from jax import lax
from jax.sharding import PartitionSpec as P


def expert_rows(rows_in, rows_cot, gate_mat, up_mat, down_mat):
    pre_gate = jnp.dot(rows_in, gate_mat, preferred_element_type=jnp.float32)
    pre_up = jnp.dot(rows_in, up_mat, preferred_element_type=jnp.float32)
    squashed = jax.nn.sigmoid(pre_gate)
    activated = pre_gate * squashed
    hidden = (activated * pre_up).astype(jnp.bfloat16)
    out_rows = lax.dot_general(
        hidden, down_mat, (((1,), (1,)), ((), ())), preferred_element_type=jnp.float32
    ).astype(jnp.bfloat16)
    hidden_cot = jnp.dot(rows_cot, down_mat, preferred_element_type=jnp.float32)
    gate_cot = (hidden_cot * pre_up * squashed * (1.0 + pre_gate * (1.0 - squashed))).astype(
        jnp.bfloat16
    )
    up_cot = (hidden_cot * activated).astype(jnp.bfloat16)
    input_cot = lax.dot_general(
        gate_cot, gate_mat, (((1,), (1,)), ((), ())), preferred_element_type=jnp.float32
    )
    input_cot = input_cot + lax.dot_general(
        up_cot, up_mat, (((1,), (1,)), ((), ())), preferred_element_type=jnp.float32
    )
    return (out_rows, input_cot.astype(jnp.bfloat16), hidden)


def to_slots(placing, assigned_rows):
    return lax.dot_general(
        placing, assigned_rows, (((0,), (0,)), ((), ())), preferred_element_type=jnp.float32
    ).astype(jnp.bfloat16)


def per_device(
    first_out, second_out, first_grad, second_grad, routes, gate_values, w_gate, w_up, w_down
):
    count_here = first_out.shape[0]
    feature_count = first_out.shape[1]
    top_count = routes.shape[1]
    owners = lax.axis_size("expert")
    groups = lax.axis_size("dp")
    capacity = min(count_here, 2 * count_here * top_count // owners)
    assigned = count_here * top_count
    slots_all = owners * capacity
    expert_ids = routes.reshape(assigned)
    onehot = (expert_ids[:, None] == jnp.arange(owners, dtype=jnp.int32)[None, :]).astype(jnp.int32)
    before = jnp.cumsum(onehot, axis=0) - onehot
    rank_in = jnp.sum(before * onehot, axis=1)
    slot_index = expert_ids * capacity + rank_in
    placing = (slot_index[:, None] == jnp.arange(slots_all, dtype=jnp.int32)[None, :]).astype(
        jnp.bfloat16
    )
    repeated = jnp.broadcast_to(
        first_out[:, None, :], (count_here, top_count, feature_count)
    ).reshape(assigned, feature_count)
    grad_repeated = jnp.broadcast_to(
        second_grad[:, None, :], (count_here, top_count, feature_count)
    ).reshape(assigned, feature_count)
    cot_rows = (gate_values.reshape(assigned)[:, None] * grad_repeated.astype(jnp.float32)).astype(
        jnp.bfloat16
    )
    send_input = to_slots(placing, repeated).reshape(owners, capacity, feature_count)
    send_cot = to_slots(placing, cot_rows).reshape(owners, capacity, feature_count)
    arrived_input, arrived_cot = (
        lax.all_to_all(send_input, "expert", split_axis=0, concat_axis=0, tiled=True),
        lax.all_to_all(send_cot, "expert", split_axis=0, concat_axis=0, tiled=True),
    )
    rows_in = arrived_input.reshape(slots_all, feature_count)
    rows_cot = arrived_cot.reshape(slots_all, feature_count)
    gate_full, up_full, down_full = (
        lax.all_gather(w_gate, "dp", axis=1, tiled=True),
        lax.all_gather(w_up, "dp", axis=1, tiled=True),
        lax.all_gather(w_down, "dp", axis=1, tiled=True),
    )
    down_mat = down_full[0]
    out_rows, input_cot, hidden = expert_rows(rows_in, rows_cot, gate_full[0], up_full[0], down_mat)
    grad_scale = 1.0 / math.sqrt(count_here * groups)
    partial_grad = lax.dot_general(
        rows_cot, hidden, (((0,), (0,)), ((), ())), preferred_element_type=jnp.float32
    )
    reduced = lax.psum_scatter(partial_grad, "dp", scatter_dimension=0, tiled=True)
    w_down_grad = (reduced * grad_scale)[None]
    back_out, back_cot = (
        lax.all_to_all(
            out_rows.reshape(owners, capacity, feature_count),
            "expert",
            split_axis=0,
            concat_axis=0,
            tiled=True,
        ),
        lax.all_to_all(
            input_cot.reshape(owners, capacity, feature_count),
            "expert",
            split_axis=0,
            concat_axis=0,
            tiled=True,
        ),
    )
    out_assigned = jnp.dot(
        placing, back_out.reshape(slots_all, feature_count), preferred_element_type=jnp.float32
    )
    cot_assigned = jnp.dot(
        placing, back_cot.reshape(slots_all, feature_count), preferred_element_type=jnp.float32
    )
    expert_out = out_assigned.reshape(count_here, top_count, feature_count)
    combined = jnp.sum(gate_values[:, :, None] * expert_out, axis=1)
    second_in = (second_out.astype(jnp.float32) - combined).astype(jnp.bfloat16)
    gate_grad = jnp.sum(second_grad.astype(jnp.float32)[:, None, :] * expert_out, axis=2)
    first_total = (
        first_grad.astype(jnp.float32)
        + jnp.sum(cot_assigned.reshape(count_here, top_count, feature_count), axis=1)
    ).astype(jnp.bfloat16)
    return (second_in, first_total, gate_grad, w_down_grad)


def solution(mesh):
    placed = (
        P(("dp", "expert"), None),
        P(("dp", "expert"), None),
        P(("dp", "expert"), None),
        P(("dp", "expert"), None),
        P(("dp", "expert"), None),
        P(("dp", "expert"), None),
        P("expert", "dp", None),
        P("expert", "dp", None),
        P("expert", "dp", None),
    )
    return jax.shard_map(
        per_device,
        mesh=mesh,
        in_specs=placed,
        out_specs=(
            P(("dp", "expert"), None),
            P(("dp", "expert"), None),
            P(("dp", "expert"), None),
            P("expert", "dp", None),
        ),
        check_vma=False,
    )
```

profile of v0, /device:TPU:4, one launch (start us, length us, event | category | flops | bytes accessed | tf_op | source)
XLA Modules:
  0.0 313.4 jit_solution(8915855435524135631)
XLA Ops:
  7.2 0.0 all-gather.4.cloned.1.call-start
  7.2 0.7 all-gather.4.cloned.1.call-update
  7.9 0.0 all-gather.6.cloned.1.call-start
  7.9 0.7 all-gather.6.cloned.1.call-update
  8.6 0.0 all-gather.8.cloned.1.call-start
  8.7 0.7 all-gather.8.cloned.1.call-update
  9.4 0.8 copy.21
  10.2 0.1 eq.65
  10.3 0.1 eq.69
  10.5 1.2 broadcast_in_dim.6
  11.7 0.2 reshape.109
  11.9 0.6 reduce-window.6
  12.5 0.2 slice_reduce_fusion
  12.7 0.1 fusion.28
  12.9 1.6 convolution_convert_fusion.1
  14.4 9.5 %all-to-all-start = ((bf16[32,16,1024]{2,1,0:T(8,128)(2,1)}), bf16[32,16,1024]{2,1,0:T(8,128)(2,1)S(1)}, u32[]{:S(2)}, u32[]{:S(2)}) async-start(bf16[32,16,1024]{2,1,0:T(8,128)(2,1)} %bitcast.2), calls=%async_computation | async-start | bytes 2097152 | tf_op jit(solution)/shard_map/all_to_all | solution.py:69
  24.0 0.3 broadcast_in_dim.7.clone
  24.3 0.7 convert_element_type.61
  25.0 0.1 copy.25
  25.1 0.1 mul.78
  25.3 1.5 convolution_convert_fusion
  26.8 11.9 %all-to-all-done = bf16[32,16,1024]{2,1,0:T(8,128)(2,1)S(1)} async-done(((bf16[32,16,1024]{2,1,0:T(8,128)(2,1)}), bf16[32,16,1024]{2,1,0:T(8,128)(2,1)S(1)}, u32[]{:S(2)}, u32[]{:S(2)}) %all-to-all-start) | async-done | bytes 1048608 | tf_op jit(solution)/shard_map/all_to_all | solution.py:69
  38.8 6.0 %all-to-all-start.2 = ((bf16[32,16,1024]{2,1,0:T(8,128)(2,1)}), bf16[32,16,1024]{2,1,0:T(8,128)(2,1)S(1)}, u32[]{:S(2)}, u32[]{:S(2)}) async-start(bf16[32,16,1024]{2,1,0:T(8,128)(2,1)} %bitcast.10), calls=%async_computation.2 | async-start | bytes 2097152 | tf_op jit(solution)/shard_map/all_to_all | solution.py:70
  44.8 0.0 reduce-scatter.2.cloned.1.call-start
  44.9 41.4 %all-gather.4.cloned.1.call-done = bf16[1,1024,768]{2,1,0:T(8,128)(2,1)} async-done(((bf16[1,64,768]{2,1,0:T(8,128)(2,1)}), bf16[1,1024,768]{2,1,0:T(8,128)(2,1)}) %all-gather.4.cloned.1.call-update) | async-done | bytes 1572880 | tf_op jit(solution)/shard_map/all_gather | solution.py:75
  86.2 3.6 %fusion.9 = f32[512,768]{1,0:T(8,128)} fusion(bf16[512,1024]{1,0:T(8,128)(2,1)S(1)} %bitcast.69, bf16[1,1024,768]{2,1,0:T(8,128)(2,1)} %all-gather.4.cloned.1.call-done), kind=kOutput, calls=%fused_computation.10 | convolution fusion | flops 805306368 | bytes 4194304 | tf_op jit(solution)/shard_map/dot_general | solution.py:10
  89.8 67.4 %all-gather.6.cloned.1.call-done = bf16[1,1024,768]{2,1,0:T(8,128)(2,1)} async-done(((bf16[1,64,768]{2,1,0:T(8,128)(2,1)}), bf16[1,1024,768]{2,1,0:T(8,128)(2,1)}) %all-gather.6.cloned.1.call-update) | async-done | bytes 1572880 | tf_op jit(solution)/shard_map/all_gather | solution.py:76
  157.2 4.0 %multiply_convert_fusion.2 = (bf16[512,768]{1,0:T(8,128)(2,1)S(1)}, f32[512,768]{1,0:T(8,128)}) fusion(f32[512,768]{1,0:T(8,128)} %fusion.9, bf16[512,1024]{1,0:T(8,128)(2,1)S(1)} %bitcast.70, bf16[1,1024,768]{2,1,0:T(8,128)(2,1)} %all-gather.6.cloned.1.call-done), kind=kOutput, calls=%fused_computation.14 | convolution fusion | flops 807665664 | bytes 6553600 | tf_op jit(solution)/shard_map/dot_general | solution.py:11
  161.3 2.7 fusion.32
  163.9 0.0 reduce-scatter.2.cloned.1.call-update
  164.0 64.3 %all-gather.8.cloned.1.call-done = bf16[1,1024,768]{2,1,0:T(8,128)(2,1)} async-done(((bf16[1,64,768]{2,1,0:T(8,128)(2,1)}), bf16[1,1024,768]{2,1,0:T(8,128)(2,1)}) %all-gather.8.cloned.1.call-update) | async-done | bytes 1572880 | tf_op jit(solution)/shard_map/all_gather | solution.py:77
  228.3 2.5 fusion
  230.9 0.3 copy-done.8
  231.1 1.4 fusion.7
  232.6 2.0 add_convert_fusion
  234.6 7.4 %all-to-all-start.3 = ((bf16[32,16,1024]{2,1,0:T(8,128)(2,1)}), bf16[32,16,1024]{2,1,0:T(8,128)(2,1)S(1)}, u32[]{:S(2)}, u32[]{:S(2)}) async-start(bf16[32,16,1024]{2,1,0:T(8,128)(2,1)} %bitcast.12), calls=%async_computation.3 | async-start | bytes 2097152 | tf_op jit(solution)/shard_map/all_to_all | solution.py:95
  242.0 3.4 %fusion.12 = bf16[512,1024]{1,0:T(8,128)(2,1)} fusion(bf16[512,768]{1,0:T(8,128)(2,1)S(1)} %get-tuple-element.6, bf16[1,1024,768]{2,1,0:T(8,128)(2,1)} %all-gather.8.cloned.1.call-done), kind=kOutput, calls=%fused_computation.17 | convolution fusion | flops 805830656 | bytes 3407872 | tf_op jit(solution)/shard_map/dot_general | solution.py:15
  245.5 11.4 %all-to-all-done.3 = bf16[32,16,1024]{2,1,0:T(8,128)(2,1)S(1)} async-done(((bf16[32,16,1024]{2,1,0:T(8,128)(2,1)}), bf16[32,16,1024]{2,1,0:T(8,128)(2,1)S(1)}, u32[]{:S(2)}, u32[]{:S(2)}) %all-to-all-start.3) | async-done | bytes 1048608 | tf_op jit(solution)/shard_map/all_to_all | solution.py:95
  256.9 6.0 %all-to-all-start.1 = ((bf16[32,16,1024]{2,1,0:T(8,128)(2,1)}), bf16[32,16,1024]{2,1,0:T(8,128)(2,1)S(1)}, u32[]{:S(2)}, u32[]{:S(2)}) async-start(bf16[32,16,1024]{2,1,0:T(8,128)(2,1)} %bitcast.7), calls=%async_computation.1 | async-start | bytes 2097152 | tf_op jit(solution)/shard_map/all_to_all | solution.py:88
  262.9 0.1 reduce_sum.39
  263.1 0.1 copy.24
  263.1 0.5 convolution_reduce_fusion
  263.7 14.1 %all-to-all-done.1 = bf16[32,16,1024]{2,1,0:T(8,128)(2,1)S(1)} async-done(((bf16[32,16,1024]{2,1,0:T(8,128)(2,1)}), bf16[32,16,1024]{2,1,0:T(8,128)(2,1)S(1)}, u32[]{:S(2)}, u32[]{:S(2)}) %all-to-all-start.1) | async-done | bytes 1048608 | tf_op jit(solution)/shard_map/all_to_all | solution.py:88
  277.7 1.1 multiply_reduce_fusion
  278.9 0.8 subtract_convert_fusion
  279.7 0.8 add_convert_fusion.1
  280.4 24.8 %reduce-scatter.2.cloned.1.call-done = f32[64,768]{1,0:T(8,128)} async-done(((f32[1024,768]{1,0:T(8,128)}), f32[64,768]{1,0:T(8,128)}) %reduce-scatter.2.cloned.1.call-update) | async-done | bytes 196624 | tf_op jit(solution)/shard_map/reduce_scatter | solution.py:85
  305.2 1.6 multiply_bitcast_fusion
  (24 shorter events, 0.1 us)
Async XLA Ops:
  7.2 79.1 %all-gather.4.cloned.1.call-start = ((), (), s32[]{:S(2)}) async-start(), calls=%async_computation.5 | async-start | bytes 1671168 | tf_op jit(solution)/shard_map/all_gather | solution.py:75
  7.9 149.3 %all-gather.6.cloned.1.call-start = ((), (), s32[]{:S(2)}) async-start(), calls=%async_computation.6 | async-start | bytes 1671168 | tf_op jit(solution)/shard_map/all_gather | solution.py:76
  8.6 219.7 %all-gather.8.cloned.1.call-start = ((), (), s32[]{:S(2)}) async-start(), calls=%async_computation.7 | async-start | bytes 1671168 | tf_op jit(solution)/shard_map/all_gather | solution.py:77
  12.8 11.1 %copy-start = (bf16[128,1024]{1,0:T(8,128)(2,1)S(1)}, bf16[128,1024]{1,0:T(8,128)(2,1)}, u32[]{:S(2)}) copy-start(bf16[128,1024]{1,0:T(8,128)(2,1)} %param.12) | copy-start | bytes 786436
  14.4 24.3 %all-to-all-start = ((bf16[32,16,1024]{2,1,0:T(8,128)(2,1)}), bf16[32,16,1024]{2,1,0:T(8,128)(2,1)S(1)}, u32[]{:S(2)}, u32[]{:S(2)}) async-start(bf16[32,16,1024]{2,1,0:T(8,128)(2,1)} %bitcast.2), calls=%async_computation | async-start | bytes 2097152 | tf_op jit(solution)/shard_map/all_to_all | solution.py:69
  24.0 1.0 copy-start.4
  38.8 122.5 %all-to-all-start.2 = ((bf16[32,16,1024]{2,1,0:T(8,128)(2,1)}), bf16[32,16,1024]{2,1,0:T(8,128)(2,1)S(1)}, u32[]{:S(2)}, u32[]{:S(2)}) async-start(bf16[32,16,1024]{2,1,0:T(8,128)(2,1)} %bitcast.10), calls=%async_computation.2 | async-start | bytes 2097152 | tf_op jit(solution)/shard_map/all_to_all | solution.py:70
  44.8 260.4 %reduce-scatter.2.cloned.1.call-start = ((), (), s32[]{:S(2)}) async-start(), calls=%async_computation.8 | async-start | bytes 3342336 | tf_op jit(solution)/shard_map/reduce_scatter | solution.py:85
  228.3 2.5 copy-start.5
  228.3 2.6 copy-start.7
  228.3 2.8 copy-start.8
  231.1 1.4 copy-start.6
  234.6 22.3 %all-to-all-start.3 = ((bf16[32,16,1024]{2,1,0:T(8,128)(2,1)}), bf16[32,16,1024]{2,1,0:T(8,128)(2,1)S(1)}, u32[]{:S(2)}, u32[]{:S(2)}) async-start(bf16[32,16,1024]{2,1,0:T(8,128)(2,1)} %bitcast.12), calls=%async_computation.3 | async-start | bytes 2097152 | tf_op jit(solution)/shard_map/all_to_all | solution.py:95
  245.5 17.7 %copy-start.3 = (s32[128,2]{0,1:T(2,128)S(1)}, s32[128,2]{0,1:T(2,128)}, u32[]{:S(2)}) copy-start(s32[128,2]{0,1:T(2,128)} %param.13) | copy-start | bytes 3076
  256.9 20.8 %all-to-all-start.1 = ((bf16[32,16,1024]{2,1,0:T(8,128)(2,1)}), bf16[32,16,1024]{2,1,0:T(8,128)(2,1)S(1)}, u32[]{:S(2)}, u32[]{:S(2)}) async-start(bf16[32,16,1024]{2,1,0:T(8,128)(2,1)} %bitcast.7), calls=%async_computation.1 | async-start | bytes 2097152 | tf_op jit(solution)/shard_map/all_to_all | solution.py:88
  263.7 15.2 %copy-start.1 = (bf16[128,1024]{1,0:T(8,128)(2,1)S(1)}, bf16[128,1024]{1,0:T(8,128)(2,1)}, u32[]{:S(2)}) copy-start(bf16[128,1024]{1,0:T(8,128)(2,1)} %param.10) | copy-start | bytes 786436
  277.7 1.9 copy-start.2
Sparse Core Ops, SparseCore 0:
  10.1 76.1 all-gather.3
  88.3 68.8 all-gather.5
  159.3 68.9 all-gather.7
  231.0 74.1 reduce-scatter.1
where the time goes:
time: 314 us; the launch traced here: 313 us
  waiting for transfers between devices  237 us (75%)
  starting transfers between devices  29.1 us (9%)
  matrix products  24.5 us (8%)
  between operations  14 us (4%)
  local copies, waits for them, and re-layouts  4.42 us (1%)
  other arithmetic  3.92 us (1%)
    all_gather x1, waiting for transfers between devices, per_device(): lax.all_gather(w_up, 'dp', axis=1, tiled=True)  67.4 us
    all_gather x1, waiting for transfers between devices, per_device(): lax.all_gather(w_down, 'dp', axis=1, tiled=True)  64.3 us
    all_gather x1, waiting for transfers between devices, per_device(): lax.all_gather(w_gate, 'dp', axis=1, tiled=True)  41.4 us
    reduce_scatter x1, waiting for transfers between devices, per_device(): lax.psum_scatter(partial_grad, 'dp', scatter_dimension=0, tiled=True)  24.8 us
    all_to_all x1, waiting for transfers between devices, per_device(): lax.all_to_all(out_rows.reshape(owners, capacity, feature_count), 'expert...  14.1 us
    all_to_all x1, waiting for transfers between devices, per_device(): lax.all_to_all(send_input, 'expert', split_axis=0, concat_axis=0, tiled=T...  11.9 us
    all_to_all x1, waiting for transfers between devices, per_device(): lax.all_to_all(input_cot.reshape(owners, capacity, feature_count), 'exper...  11.4 us
    all_to_all x1, starting transfers between devices, per_device(): lax.all_to_all(send_input, 'expert', split_axis=0, concat_axis=0, tiled=T...  9.53 us
  transfers between devices with their start and end apart: 8, of which 7 were waited for; matrix products, arithmetic and copies ran while one was open for 10% of the time, Pallas kernels for 0%

commit v1 on v0

--- a/solution.py
+++ b/solution.py
@@ -71,13 +71,13 @@
     )
     rows_in = arrived_input.reshape(slots_all, feature_count)
     rows_cot = arrived_cot.reshape(slots_all, feature_count)
-    gate_full, up_full, down_full = (
-        lax.all_gather(w_gate, "dp", axis=1, tiled=True),
-        lax.all_gather(w_up, "dp", axis=1, tiled=True),
-        lax.all_gather(w_down, "dp", axis=1, tiled=True),
-    )
-    down_mat = down_full[0]
-    out_rows, input_cot, hidden = expert_rows(rows_in, rows_cot, gate_full[0], up_full[0], down_mat)
+    hidden_count = w_gate.shape[2]
+    shards = jnp.concatenate([w_gate[0], w_up[0], w_down[0]], axis=1)
+    mats = lax.all_gather(shards, "dp", axis=0, tiled=True)
+    gate_mat = mats[:, :hidden_count]
+    up_mat = mats[:, hidden_count : 2 * hidden_count]
+    down_mat = mats[:, 2 * hidden_count :]
+    out_rows, input_cot, hidden = expert_rows(rows_in, rows_cot, gate_mat, up_mat, down_mat)
     grad_scale = 1.0 / math.sqrt(count_here * groups)
     partial_grad = lax.dot_general(
         rows_cot, hidden, (((0,), (0,)), ((), ())), preferred_element_type=jnp.float32

time: 314 us -> 186 us (0.59)
  the two profiles are of different devices: /device:TPU:4 before, /device:TPU:2 now
where the time goes in v1:
time: 186 us; the launch traced here: 185 us
  waiting for transfers between devices  104 us (56%)
  starting transfers between devices  30.1 us (16%)
  matrix products  25.9 us (14%)
  between operations  14.3 us (8%)
  other arithmetic  5.66 us (3%)
  local copies, waits for them, and re-layouts  5.32 us (3%)
    all_gather x1, waiting for transfers between devices, per_device(): mats = lax.all_gather(shards, 'dp', axis=0, tiled=True)  49 us
    reduce_scatter x1, waiting for transfers between devices, per_device(): lax.psum_scatter(partial_grad, 'dp', scatter_dimension=0, tiled=True)  18.7 us
    all_to_all x1, waiting for transfers between devices, per_device(): lax.all_to_all(out_rows.reshape(owners, capacity, feature_count), 'expert...  13.6 us
    all_to_all x1, waiting for transfers between devices, per_device(): lax.all_to_all(send_input, 'expert', split_axis=0, concat_axis=0, tiled=T...  11.6 us
    all_to_all x1, waiting for transfers between devices, per_device(): lax.all_to_all(input_cot.reshape(owners, capacity, feature_count), 'exper...  10.9 us
    all_to_all x1, starting transfers between devices, per_device(): lax.all_to_all(send_input, 'expert', split_axis=0, concat_axis=0, tiled=T...  9.51 us
    all_to_all x1, starting transfers between devices, per_device(): lax.all_to_all(input_cot.reshape(owners, capacity, feature_count), 'exper...  7.71 us
    all_to_all x1, starting transfers between devices, per_device(): lax.all_to_all(out_rows.reshape(owners, capacity, feature_count), 'expert...  6.42 us
  transfers between devices with their start and end apart: 6, of which 5 were waited for; matrix products, arithmetic and copies ran while one was open for 16% of the time, Pallas kernels for 0%

profile of v1, /device:TPU:2, one launch (start us, length us, event | category | flops | bytes accessed | tf_op | source)
XLA Modules:
  0.0 185.1 jit_solution(12592394571378709768)
XLA Ops:
  7.2 0.0 all-gather.2.cloned.1.call-start
  7.2 1.7 pad_maximum_fusion
  9.0 0.0 all-gather.2.cloned.1.call-update
  9.0 0.8 copy.21
  9.8 0.1 eq.69
  9.9 0.1 eq.65
  10.1 0.6 reduce-window.6
  10.7 0.2 slice_reduce_fusion
  10.9 1.2 broadcast_in_dim.6
  12.1 0.2 reshape.109
  12.3 0.1 fusion.23
  12.4 0.0 copy-start
  12.4 1.5 convolution_convert_fusion.2
  14.0 9.5 %all-to-all-start = ((bf16[32,16,1024]{2,1,0:T(8,128)(2,1)}), bf16[32,16,1024]{2,1,0:T(8,128)(2,1)S(1)}, u32[]{:S(2)}, u32[]{:S(2)}) async-start(bf16[32,16,1024]{2,1,0:T(8,128)(2,1)} %bitcast.2), calls=%async_computation | async-start | bytes 2097152 | tf_op jit(solution)/shard_map/all_to_all | solution.py:69
  23.5 0.0 copy-start.4
  23.5 0.3 broadcast_in_dim.7.clone
  23.8 0.7 convert_element_type.61
  24.5 0.1 copy.25
  24.7 0.1 mul.78
  24.8 1.6 convolution_convert_fusion.1
  26.4 11.6 %all-to-all-done = bf16[32,16,1024]{2,1,0:T(8,128)(2,1)S(1)} async-done(((bf16[32,16,1024]{2,1,0:T(8,128)(2,1)}), bf16[32,16,1024]{2,1,0:T(8,128)(2,1)S(1)}, u32[]{:S(2)}, u32[]{:S(2)}) %all-to-all-start) | async-done | bytes 1048608 | tf_op jit(solution)/shard_map/all_to_all | solution.py:69
  38.0 6.4 %all-to-all-start.2 = ((bf16[32,16,1024]{2,1,0:T(8,128)(2,1)}), bf16[32,16,1024]{2,1,0:T(8,128)(2,1)S(1)}, u32[]{:S(2)}, u32[]{:S(2)}) async-start(bf16[32,16,1024]{2,1,0:T(8,128)(2,1)} %bitcast.10), calls=%async_computation.2 | async-start | bytes 2097152 | tf_op jit(solution)/shard_map/all_to_all | solution.py:70
  44.4 0.0 reduce-scatter.2.cloned.1.call-start
  44.4 49.0 %all-gather.2.cloned.1.call-done = bf16[1024,2304]{1,0:T(8,128)(2,1)} async-done(((bf16[64,2304]{1,0:T(8,128)(2,1)}), bf16[1024,2304]{1,0:T(8,128)(2,1)}) %all-gather.2.cloned.1.call-update) | async-done | bytes 4718608 | tf_op jit(solution)/shard_map/all_gather | solution.py:76
  93.5 2.4 %fusion.9 = f32[512,768]{1,0:T(8,128)S(1)} fusion(bf16[512,1024]{1,0:T(8,128)(2,1)S(1)} %bitcast.53, bf16[1024,2304]{1,0:T(8,128)(2,1)} %all-gather.2.cloned.1.call-done), kind=kOutput, calls=%fused_computation.17 | convolution fusion | flops 805306368 | bytes 4194304 | tf_op jit(solution)/shard_map/dot_general | solution.py:10
  95.8 0.0 copy-start.5
  95.9 1.2 copy-done.5
  97.0 3.6 %multiply_convert_fusion.2 = (bf16[512,768]{1,0:T(8,128)(2,1)S(1)}, f32[512,768]{1,0:T(8,128)}) fusion(f32[512,768]{1,0:T(8,128)S(1)} %fusion.9, bf16[512,1024]{1,0:T(8,128)(2,1)S(1)} %bitcast.54, bf16[1024,2304]{1,0:T(8,128)(2,1)} %all-gather.2.cloned.1.call-done), kind=kOutput, calls=%fused_computation.3 | convolution fusion | flops 807665664 | bytes 6553600 | tf_op jit(solution)/shard_map/dot_general | solution.py:11
  100.7 0.0 all-to-all-done.2
  100.7 2.7 %fusion.27 = f32[1024,768]{1,0:T(8,128)} fusion(bf16[512,1024]{1,0:T(8,128)(2,1)S(1)} %bitcast.51, bf16[512,768]{1,0:T(8,128)(2,1)S(1)} %get-tuple-element.6), kind=kOutput, calls=%fused_computation.49 | convolution fusion | flops 805306368 | bytes 4980736 | tf_op jit(solution)/shard_map/dot_general | solution.py:82
  103.3 0.0 reduce-scatter.2.cloned.1.call-update
  103.4 2.5 %fusion.1 = f32[512,768]{1,0:T(8,128)S(1)} fusion(bf16[512,1024]{1,0:T(8,128)(2,1)S(1)} %bitcast.52, bf16[1024,2304]{1,0:T(8,128)(2,1)} %all-gather.2.cloned.1.call-done), kind=kOutput, calls=%fused_computation.9 | convolution fusion | flops 805306368 | bytes 4194304 | tf_op jit(solution)/shard_map/dot_general | solution.py:18
  106.0 2.9 %fusion.7 = f32[512,1024]{1,0:T(8,128)S(1)} fusion(bf16[1024,2304]{1,0:T(8,128)(2,1)} %all-gather.2.cloned.1.call-done, f32[512,768]{1,0:T(8,128)S(1)} %copy-done.6, f32[512,768]{1,0:T(8,128)S(1)} %fusion.1, f32[512,768]{1,0:T(8,128)S(1)} %copy-done.7), kind=kOutput, calls=%fused_computation.15 | convolution fusion | flops 809238528 | bytes 8388608 | tf_op jit(solution)/shard_map/dot_general | solution.py:23
  108.8 3.5 %add_convert_fusion = bf16[512,1024]{1,0:T(8,128)(2,1)} fusion(f32[512,1024]{1,0:T(8,128)S(1)} %fusion.7, bf16[1024,2304]{1,0:T(8,128)(2,1)} %all-gather.2.cloned.1.call-done, f32[512,768]{1,0:T(8,128)S(1)} %fusion.1, f32[512,768]{1,0:T(8,128)S(1)} %copy-done.6), kind=kOutput, calls=%fused_computation | convolution fusion | flops 808714240 | bytes 7864320 | tf_op jit(solution)/shard_map/dot_general | solution.py:26
  112.3 7.7 %all-to-all-start.3 = ((bf16[32,16,1024]{2,1,0:T(8,128)(2,1)}), bf16[32,16,1024]{2,1,0:T(8,128)(2,1)S(1)}, u32[]{:S(2)}, u32[]{:S(2)}) async-start(bf16[32,16,1024]{2,1,0:T(8,128)(2,1)} %bitcast.12), calls=%async_computation.3 | async-start | bytes 2097152 | tf_op jit(solution)/shard_map/all_to_all | solution.py:95
  120.1 3.5 %convolution_convert_fusion = bf16[512,1024]{1,0:T(8,128)(2,1)} fusion(bf16[512,768]{1,0:T(8,128)(2,1)S(1)} %get-tuple-element.6, bf16[1024,2304]{1,0:T(8,128)(2,1)} %all-gather.2.cloned.1.call-done), kind=kOutput, calls=%fused_computation.6 | convolution fusion | flops 805830656 | bytes 3407872 | tf_op jit(solution)/shard_map/dot_general | solution.py:15
  123.5 10.9 %all-to-all-done.3 = bf16[32,16,1024]{2,1,0:T(8,128)(2,1)S(1)} async-done(((bf16[32,16,1024]{2,1,0:T(8,128)(2,1)}), bf16[32,16,1024]{2,1,0:T(8,128)(2,1)S(1)}, u32[]{:S(2)}, u32[]{:S(2)}) %all-to-all-start.3) | async-done | bytes 1048608 | tf_op jit(solution)/shard_map/all_to_all | solution.py:95
  134.5 6.4 %all-to-all-start.1 = ((bf16[32,16,1024]{2,1,0:T(8,128)(2,1)}), bf16[32,16,1024]{2,1,0:T(8,128)(2,1)S(1)}, u32[]{:S(2)}, u32[]{:S(2)}) async-start(bf16[32,16,1024]{2,1,0:T(8,128)(2,1)} %bitcast.7), calls=%async_computation.1 | async-start | bytes 2097152 | tf_op jit(solution)/shard_map/all_to_all | solution.py:88
  140.9 0.1 reduce_sum.39
  141.1 0.1 copy.24
  141.2 0.5 convolution_reduce_fusion
  141.7 0.0 copy-start.1
  141.7 13.6 %all-to-all-done.1 = bf16[32,16,1024]{2,1,0:T(8,128)(2,1)S(1)} async-done(((bf16[32,16,1024]{2,1,0:T(8,128)(2,1)}), bf16[32,16,1024]{2,1,0:T(8,128)(2,1)S(1)}, u32[]{:S(2)}, u32[]{:S(2)}) %all-to-all-start.1) | async-done | bytes 1048608 | tf_op jit(solution)/shard_map/all_to_all | solution.py:88
  155.3 1.1 multiply_reduce_fusion
  156.5 0.8 add_convert_fusion.1
  157.2 0.8 subtract_convert_fusion
  158.0 18.7 %reduce-scatter.2.cloned.1.call-done = f32[64,768]{1,0:T(8,128)} async-done(((f32[1024,768]{1,0:T(8,128)}), f32[64,768]{1,0:T(8,128)}) %reduce-scatter.2.cloned.1.call-update) | async-done | bytes 196624 | tf_op jit(solution)/shard_map/reduce_scatter | solution.py:85
  176.7 1.6 multiply_bitcast_fusion
  (17 shorter events, 0.1 us)
Async XLA Ops:
  7.2 86.3 %all-gather.2.cloned.1.call-start = ((), (), s32[]{:S(2)}) async-start(), calls=%async_computation.5 | async-start | bytes 5013504 | tf_op jit(solution)/shard_map/all_gather | solution.py:76
  12.4 11.1 %copy-start = (bf16[128,1024]{1,0:T(8,128)(2,1)S(1)}, bf16[128,1024]{1,0:T(8,128)(2,1)}, u32[]{:S(2)}) copy-start(bf16[128,1024]{1,0:T(8,128)(2,1)} %param.12) | copy-start | bytes 786436
  14.0 24.0 %all-to-all-start = ((bf16[32,16,1024]{2,1,0:T(8,128)(2,1)}), bf16[32,16,1024]{2,1,0:T(8,128)(2,1)S(1)}, u32[]{:S(2)}, u32[]{:S(2)}) async-start(bf16[32,16,1024]{2,1,0:T(8,128)(2,1)} %bitcast.2), calls=%async_computation | async-start | bytes 2097152 | tf_op jit(solution)/shard_map/all_to_all | solution.py:69
  23.5 1.0 copy-start.4
  38.0 62.7 %all-to-all-start.2 = ((bf16[32,16,1024]{2,1,0:T(8,128)(2,1)}), bf16[32,16,1024]{2,1,0:T(8,128)(2,1)S(1)}, u32[]{:S(2)}, u32[]{:S(2)}) async-start(bf16[32,16,1024]{2,1,0:T(8,128)(2,1)} %bitcast.10), calls=%async_computation.2 | async-start | bytes 2097152 | tf_op jit(solution)/shard_map/all_to_all | solution.py:70
  44.4 132.3 %reduce-scatter.2.cloned.1.call-start = ((), (), s32[]{:S(2)}) async-start(), calls=%async_computation.6 | async-start | bytes 3342336 | tf_op jit(solution)/shard_map/reduce_scatter | solution.py:85
  95.8 1.2 copy-start.5
  103.4 2.6 %copy-start.6 = (f32[512,768]{1,0:T(8,128)S(1)}, f32[512,768]{1,0:T(8,128)}, u32[]{:S(2)}) copy-start(f32[512,768]{1,0:T(8,128)} %copy-done.5) | copy-start | bytes 4718596
  103.4 2.6 %copy-start.7 = (f32[512,768]{1,0:T(8,128)S(1)}, f32[512,768]{1,0:T(8,128)}, u32[]{:S(2)}) copy-start(f32[512,768]{1,0:T(8,128)} %get-tuple-element.7) | copy-start | bytes 4718596
  112.3 22.1 %all-to-all-start.3 = ((bf16[32,16,1024]{2,1,0:T(8,128)(2,1)}), bf16[32,16,1024]{2,1,0:T(8,128)(2,1)S(1)}, u32[]{:S(2)}, u32[]{:S(2)}) async-start(bf16[32,16,1024]{2,1,0:T(8,128)(2,1)} %bitcast.12), calls=%async_computation.3 | async-start | bytes 2097152 | tf_op jit(solution)/shard_map/all_to_all | solution.py:95
  123.5 17.6 %copy-start.3 = (s32[128,2]{0,1:T(2,128)S(1)}, s32[128,2]{0,1:T(2,128)}, u32[]{:S(2)}) copy-start(s32[128,2]{0,1:T(2,128)} %param.13) | copy-start | bytes 3076
  134.5 20.8 %all-to-all-start.1 = ((bf16[32,16,1024]{2,1,0:T(8,128)(2,1)}), bf16[32,16,1024]{2,1,0:T(8,128)(2,1)S(1)}, u32[]{:S(2)}, u32[]{:S(2)}) async-start(bf16[32,16,1024]{2,1,0:T(8,128)(2,1)} %bitcast.7), calls=%async_computation.1 | async-start | bytes 2097152 | tf_op jit(solution)/shard_map/all_to_all | solution.py:88
  141.7 14.8 %copy-start.1 = (bf16[128,1024]{1,0:T(8,128)(2,1)S(1)}, bf16[128,1024]{1,0:T(8,128)(2,1)}, u32[]{:S(2)}) copy-start(bf16[128,1024]{1,0:T(8,128)(2,1)} %param.11) | copy-start | bytes 786436
  155.3 1.9 %copy-start.2 = (bf16[128,1024]{1,0:T(8,128)(2,1)S(1)}, bf16[128,1024]{1,0:T(8,128)(2,1)}, u32[]{:S(2)}) copy-start(bf16[128,1024]{1,0:T(8,128)(2,1)} %param.10) | copy-start | bytes 786436
Sparse Core Ops, SparseCore 0:
  10.1 83.3 all-gather.1
  103.5 73.1 reduce-scatter.1

commit v2 on v1

--- a/solution.py
+++ b/solution.py
@@ -3,36 +3,154 @@
 import jax
 import jax.numpy as jnp
 from jax import lax
+from jax.experimental import pallas as pl
+from jax.experimental.pallas import tpu as pltpu
 from jax.sharding import PartitionSpec as P
 
 
-def expert_rows(rows_in, rows_cot, gate_mat, up_mat, down_mat):
-    pre_gate = jnp.dot(rows_in, gate_mat, preferred_element_type=jnp.float32)
-    pre_up = jnp.dot(rows_in, up_mat, preferred_element_type=jnp.float32)
+BLOCK = 256
+STRIDE = 4
+
+
+def _dot(a, b, over):
+    return lax.dot_general(a, b, ((over[:1], over[1:]), ((), ())), preferred_element_type=jnp.float32)
+
+
+def _hidden_kernel(
+    place, rows, cot, gate, up, hidden, slope, activated, send_two, send_one, own_three, own_zero, classes
+):
+    pre_gate = _dot(rows[...], gate[...], (1, 0))
+    pre_up = _dot(rows[...], up[...], (1, 0))
     squashed = jax.nn.sigmoid(pre_gate)
-    activated = pre_gate * squashed
-    hidden = (activated * pre_up).astype(jnp.bfloat16)
-    out_rows = lax.dot_general(
-        hidden, down_mat, (((1,), (1,)), ((), ())), preferred_element_type=jnp.float32
-    ).astype(jnp.bfloat16)
-    hidden_cot = jnp.dot(rows_cot, down_mat, preferred_element_type=jnp.float32)
-    gate_cot = (hidden_cot * pre_up * squashed * (1.0 + pre_gate * (1.0 - squashed))).astype(
-        jnp.bfloat16
-    )
-    up_cot = (hidden_cot * activated).astype(jnp.bfloat16)
-    input_cot = lax.dot_general(
-        gate_cot, gate_mat, (((1,), (1,)), ((), ())), preferred_element_type=jnp.float32
-    )
-    input_cot = input_cot + lax.dot_general(
-        up_cot, up_mat, (((1,), (1,)), ((), ())), preferred_element_type=jnp.float32
-    )
-    return (out_rows, input_cot.astype(jnp.bfloat16), hidden)
+    active = pre_gate * squashed
+    here = (active * pre_up).astype(jnp.bfloat16)
+    hidden[...] = here
+    activated[...] = active
+    slope[...] = pre_up * squashed * (1.0 + pre_gate * (1.0 - squashed))
+    partial = _dot(cot[...], here, (0, 0))
+    members, block = classes.shape[1], classes.shape[2]
+    for index in range(members * STRIDE):
+        classes[index % STRIDE, index // STRIDE] = partial[index * block : (index + 1) * block]
+    for shift, target in ((2, send_two), (1, send_one), (3, own_three), (0, own_zero)):
+        target[...] = classes[(place[0] + shift) % STRIDE].astype(target.dtype)
+
+
+def hidden_and_partial(place, rows, cot, mats, groups):
+    slots, features = rows.shape
+    width = mats.shape[1] // 3
+    steps = width // BLOCK
+    members, block = groups // STRIDE, features // groups
+    whole = pl.BlockSpec((slots, features), lambda j, place: (0, 0))
+    column = pl.BlockSpec((slots, BLOCK), lambda j, place: (0, j))
+    part = pl.BlockSpec((members, block, BLOCK), lambda j, place: (0, 0, j))
+    part_shape = (members, block, width)
+    return pl.pallas_call(
+        _hidden_kernel,
+        grid_spec=pltpu.PrefetchScalarGridSpec(
+            num_scalar_prefetch=1,
+            grid=(steps,),
+            in_specs=[
+                whole,
+                whole,
+                pl.BlockSpec((features, BLOCK), lambda j, place: (0, j)),
+                pl.BlockSpec((features, BLOCK), lambda j, place: (0, j + steps)),
+            ],
+            out_specs=[column, column, column, part, part, part, part],
+            scratch_shapes=[pltpu.VMEM((STRIDE, members, block, BLOCK), jnp.float32)],
+        ),
+        out_shape=[
+            jax.ShapeDtypeStruct((slots, width), jnp.bfloat16),
+            jax.ShapeDtypeStruct((slots, width), jnp.float32),
+            jax.ShapeDtypeStruct((slots, width), jnp.float32),
+            jax.ShapeDtypeStruct(part_shape, jnp.bfloat16),
+            jax.ShapeDtypeStruct(part_shape, jnp.bfloat16),
+            jax.ShapeDtypeStruct(part_shape, jnp.float32),
+            jax.ShapeDtypeStruct(part_shape, jnp.float32),
+        ],
+        name="hidden_and_partial",
+    )(place, rows, cot, mats, mats)
+
+
+def _back_kernel(hidden, cot, slope, activated, gate, up, down_mat, back, out_sum, cot_sum):
+    at = pl.program_id(0)
+    features = cot.shape[1]
+    down = down_mat[...]
+    hidden_cot = _dot(cot[...], down, (1, 0))
+    gate_cot = (hidden_cot * slope[...]).astype(jnp.bfloat16)
+    up_cot = (hidden_cot * activated[...]).astype(jnp.bfloat16)
+    out_part = _dot(hidden[...], down, (1, 1))
+    cot_part = _dot(gate_cot, gate[...], (1, 1)) + _dot(up_cot, up[...], (1, 1))
+
+    @pl.when(at == 0)
+    def _():
+        out_sum[...] = out_part
+        cot_sum[...] = cot_part
+
+    @pl.when(at > 0)
+    def _():
+        out_sum[...] += out_part
+        cot_sum[...] += cot_part
+
+    @pl.when(at == pl.num_programs(0) - 1)
+    def _():
+        back[:, :features] = out_sum[...].astype(jnp.bfloat16)
+        back[:, features:] = cot_sum[...].astype(jnp.bfloat16)
+
+
+def rows_back(hidden, cot, slope, activated, mats):
+    slots, features = cot.shape
+    steps = hidden.shape[1] // BLOCK
+    column = pl.BlockSpec((slots, BLOCK), lambda j: (0, j))
+    return pl.pallas_call(
+        _back_kernel,
+        grid=(steps,),
+        in_specs=[
+            column,
+            pl.BlockSpec((slots, features), lambda j: (0, 0)),
+            column,
+            column,
+            pl.BlockSpec((features, BLOCK), lambda j: (0, j)),
+            pl.BlockSpec((features, BLOCK), lambda j: (0, j + steps)),
+            pl.BlockSpec((features, BLOCK), lambda j: (0, j + 2 * steps)),
+        ],
+        out_specs=pl.BlockSpec((slots, 2 * features), lambda j: (0, 0)),
+        out_shape=jax.ShapeDtypeStruct((slots, 2 * features), jnp.bfloat16),
+        scratch_shapes=[
+            pltpu.VMEM((slots, features), jnp.float32),
+            pltpu.VMEM((slots, features), jnp.float32),
+        ],
+        name="rows_back",
+    )(hidden, cot, slope, activated, mats, mats, mats)
 
 
 def to_slots(placing, assigned_rows):
     return lax.dot_general(
         placing, assigned_rows, (((0,), (0,)), ((), ())), preferred_element_type=jnp.float32
     ).astype(jnp.bfloat16)
+
+
+def window_reduce(send_two, send_one, own_three, own_zero, groups):
+    members = groups // STRIDE
+    place = lax.axis_index("dp")
+
+    def moved(value, by):
+        return lax.ppermute(value, "dp", [(i, (i + by) % groups) for i in range(groups)])
+
+    from_second = moved(send_two, -1)
+    from_below = moved(send_one, 1)
+    passed_on = (from_second.astype(jnp.float32) + own_three).astype(jnp.bfloat16)
+    from_above = moved(passed_on, -1)
+    window = from_above.astype(jnp.float32) + (from_below.astype(jnp.float32) + own_zero)
+    rounded = window.astype(jnp.bfloat16)
+    member = place // STRIDE
+
+    def block_of(values, ahead):
+        return lax.dynamic_index_in_dim(values, (member + ahead) % members, 0, keepdims=False)
+
+    total = block_of(window, 0)
+    for ahead in range(1, members):
+        total = total + moved(block_of(rounded, ahead), ahead * STRIDE).astype(jnp.float32)
+    return total
 
 
 def per_device(
@@ -71,41 +189,22 @@
     )
     rows_in = arrived_input.reshape(slots_all, feature_count)
     rows_cot = arrived_cot.reshape(slots_all, feature_count)
-    hidden_count = w_gate.shape[2]
     shards = jnp.concatenate([w_gate[0], w_up[0], w_down[0]], axis=1)
     mats = lax.all_gather(shards, "dp", axis=0, tiled=True)
-    gate_mat = mats[:, :hidden_count]
-    up_mat = mats[:, hidden_count : 2 * hidden_count]
-    down_mat = mats[:, 2 * hidden_count :]
-    out_rows, input_cot, hidden = expert_rows(rows_in, rows_cot, gate_mat, up_mat, down_mat)
+    place = lax.axis_index("dp").astype(jnp.int32).reshape(1)
+    hidden, slope, activated, *parts = hidden_and_partial(place, rows_in, rows_cot, mats, groups)
+    back_rows = rows_back(hidden, rows_cot, slope, activated, mats)
+    back = lax.all_to_all(
+        back_rows.reshape(owners, capacity, 2 * feature_count),
+        "expert",
+        split_axis=0,
+        concat_axis=0,
+        tiled=True,
+    ).reshape(slots_all, 2 * feature_count)
     grad_scale = 1.0 / math.sqrt(count_here * groups)
-    partial_grad = lax.dot_general(
-        rows_cot, hidden, (((0,), (0,)), ((), ())), preferred_element_type=jnp.float32
-    )
-    reduced = lax.psum_scatter(partial_grad, "dp", scatter_dimension=0, tiled=True)
-    w_down_grad = (reduced * grad_scale)[None]
-    back_out, back_cot = (
-        lax.all_to_all(
-            out_rows.reshape(owners, capacity, feature_count),
-            "expert",
-            split_axis=0,
-            concat_axis=0,
-            tiled=True,
-        ),
-        lax.all_to_all(
-            input_cot.reshape(owners, capacity, feature_count),
-            "expert",
-            split_axis=0,
-            concat_axis=0,
-            tiled=True,
-        ),
-    )
-    out_assigned = jnp.dot(
-        placing, back_out.reshape(slots_all, feature_count), preferred_element_type=jnp.float32
-    )
-    cot_assigned = jnp.dot(
-        placing, back_cot.reshape(slots_all, feature_count), preferred_element_type=jnp.float32
-    )
+    w_down_grad = (window_reduce(*parts, groups) * grad_scale)[None]
+    out_assigned = jnp.dot(placing, back[:, :feature_count], preferred_element_type=jnp.float32)
+    cot_assigned = jnp.dot(placing, back[:, feature_count:], preferred_element_type=jnp.float32)
     expert_out = out_assigned.reshape(count_here, top_count, feature_count)
     combined = jnp.sum(gate_values[:, :, None] * expert_out, axis=1)
     second_in = (second_out.astype(jnp.float32) - combined).astype(jnp.bfloat16)

time: 186 us -> 199 us (1.070)
  the two profiles are of different devices: /device:TPU:2 before, /device:TPU:65 now
where the time goes in v2:
time: 199 us; the launch traced here: 198 us
  waiting for transfers between devices  90.4 us (45%)
  starting transfers between devices  51 us (26%)
  Pallas kernels  15.9 us (8%)
  between operations  14.4 us (7%)
  other arithmetic  12 us (6%)
  local copies, waits for them, and re-layouts  7.99 us (4%)
  matrix products  6.12 us (3%)
    ppermute x6, waiting for transfers between devices, moved(): lax.ppermute(value, 'dp', [(i, (i + by) % groups) for i in range(groups)])  35 us
    ppermute x6, starting transfers between devices, moved(): lax.ppermute(value, 'dp', [(i, (i + by) % groups) for i in range(groups)])  23.6 us
    all_gather x1, waiting for transfers between devices, per_device(): mats = lax.all_gather(shards, 'dp', axis=0, tiled=True)  23.6 us
    all_to_all x1, waiting for transfers between devices, per_device(): lax.all_to_all(send_input, 'expert', split_axis=0, concat_axis=0, tiled=T...  16.9 us
    all_to_all x1, starting transfers between devices, per_device(): lax.all_to_all(back_rows.reshape(owners, capacity, 2 * feature_count), 'e...  15.7 us
    all_to_all x1, waiting for transfers between devices, per_device(): lax.all_to_all(send_cot, 'expert', split_axis=0, concat_axis=0, tiled=True)  14.8 us
    pallas_call x1, Pallas kernels, rows_back(): pl.pallas_call(_back_kernel, grid=(steps,), in_specs=[column, pl.BlockSpe...  9.06 us
    all_to_all x1, starting transfers between devices, per_device(): lax.all_to_all(send_cot, 'expert', split_axis=0, concat_axis=0, tiled=True)  7.76 us
  transfers between devices with their start and end apart: 10, of which 7 were waited for; matrix products, arithmetic and copies ran while one was open for 7% of the time, Pallas kernels for 0%

profile of v2, /device:TPU:65, one launch (start us, length us, event | category | flops | bytes accessed | tf_op | source)
XLA Modules:
  0.0 197.8 jit_solution(11388303047904676876)
XLA Ops:
  7.2 0.0 all-gather.2.cloned.1.call-start
  7.2 1.7 pad_maximum_fusion
  8.9 0.0 all-gather.2.cloned.1.call-update
  9.0 0.8 copy.15
  9.8 0.1 eq.44
  9.9 0.1 reshape.75
  10.1 0.6 reduce-window.6
  10.6 0.2 slice_reduce_fusion
  10.9 1.2 broadcast_in_dim.7
  12.1 0.7 convert_element_type.66
  12.9 0.1 copy.14
  13.0 0.1 mul.48
  13.1 0.1 fusion.15
  13.2 1.6 convolution_convert_fusion
  14.8 7.8 %all-to-all-start.1 = ((bf16[32,16,1024]{2,1,0:T(8,128)(2,1)}), bf16[32,16,1024]{2,1,0:T(8,128)(2,1)S(1)}, u32[]{:S(2)}, u32[]{:S(2)}) async-start(bf16[32,16,1024]{2,1,0:T(8,128)(2,1)} %bitcast.4), calls=%async_computation.1 | async-start | bytes 2097152 | tf_op jit(solution)/shard_map/all_to_all | solution.py:188
  22.6 0.3 broadcast_in_dim.6
  22.8 0.2 reshape.78
  23.0 1.6 convolution_convert_fusion.1
  24.6 14.8 %all-to-all-done.1 = bf16[32,16,1024]{2,1,0:T(8,128)(2,1)S(1)} async-done(((bf16[32,16,1024]{2,1,0:T(8,128)(2,1)}), bf16[32,16,1024]{2,1,0:T(8,128)(2,1)S(1)}, u32[]{:S(2)}, u32[]{:S(2)}) %all-to-all-start.1) | async-done | bytes 1048608 | tf_op jit(solution)/shard_map/all_to_all | solution.py:188
  39.5 3.9 %all-to-all-start = ((bf16[32,16,1024]{2,1,0:T(8,128)(2,1)}), bf16[32,16,1024]{2,1,0:T(8,128)(2,1)S(1)}, u32[]{:S(2)}, u32[]{:S(2)}) async-start(bf16[32,16,1024]{2,1,0:T(8,128)(2,1)} %bitcast.54), calls=%async_computation | async-start | bytes 2097152 | tf_op jit(solution)/shard_map/all_to_all | solution.py:187
  43.4 16.9 %all-to-all-done = bf16[32,16,1024]{2,1,0:T(8,128)(2,1)S(1)} async-done(((bf16[32,16,1024]{2,1,0:T(8,128)(2,1)}), bf16[32,16,1024]{2,1,0:T(8,128)(2,1)S(1)}, u32[]{:S(2)}, u32[]{:S(2)}) %all-to-all-start) | async-done | bytes 1048608 | tf_op jit(solution)/shard_map/all_to_all | solution.py:187
  60.3 23.6 %all-gather.2.cloned.1.call-done.gate.up.down_mat = bf16[1024,2304]{1,0:T(8,128)(2,1)} async-done(((bf16[64,2304]{1,0:T(8,128)(2,1)}), bf16[1024,2304]{1,0:T(8,128)(2,1)}) %all-gather.2.cloned.1.call-update) | async-done | bytes 4718608 | tf_op jit(solution)/shard_map/all_gather | solution.py:193
  83.9 6.9 %hidden_and_partial.1 = (bf16[512,768]{1,0:T(8,128)(2,1)}, f32[512,768]{1,0:T(8,128)}, f32[512,768]{1,0:T(8,128)}, bf16[4,64,768]{2,1,0:T(8,128)(2,1)}, bf16[4,6...) custom-call(s32[1]{0:T(128)} %bitcast.1.place, bf16[512,1024]{1,0:T(8,128)(2,1)} %bitcast.53, ...), custom_call_target="tpu_custom_call" | custom-call | tf_op jit(solution)/shard_map/hidden_and_partial/pallas_call | solution.py:47
  90.8 9.1 %rows_back.1 = bf16[512,2048]{1,0:T(8,128)(2,1)} custom-call(bf16[512,768]{1,0:T(8,128)(2,1)} %get-tuple-element.11.hidden, bf16[512,1024]{1,0:T(8,128)(2,1)} %bitcast.49, f32[512,768]{1,0:T(8,128)} %get-tuple-element.12.slope, f32[512,768]{1,0:T(8,128)} %get-tuple-element.13.activated, bf16[1024,2304]{1,0:T(8,128)(2,1)} %all-gather.2.cloned.1.call-done.gate.up.down_mat, ...), custom_call_target="tpu_custom_call" | custom-call | tf_op jit(solution)/shard_map/rows_back/pallas_call | solution.py:104
  99.8 15.7 %all-to-all-start.2 = ((bf16[32,16,2048]{2,1,0:T(8,128)(2,1)}), bf16[32,16,2048]{2,1,0:T(8,128)(2,1)S(1)}, u32[]{:S(2)}, u32[]{:S(2)}) async-start(bf16[32,16,2048]{2,1,0:T(8,128)(2,1)} %bitcast.52), calls=%async_computation.2 | async-start | bytes 4194304 | tf_op jit(solution)/shard_map/all_to_all | solution.py:197
  115.5 2.0 collective-permute-start
  117.5 3.3 %collective-permute-start.2 = (bf16[4,64,768]{2,1,0:T(8,128)(2,1)}, bf16[4,64,768]{2,1,0:T(8,128)(2,1)}, u32[]{:S(2)}, u32[]{:S(2)}) collective-permute-start(bf16[4,64,768]{2,1,0:T(8,128)(2,1)} %get-tuple-element.16), channel_id=1, source_target_pairs={{0,32},{32,64},{64,96},{96,128},{128,160},{160,192},{192,224},{224... | collective-permute-start | bytes 1179656 | tf_op jit(solution)/shard_map/ppermute | solution.py:137
  120.8 7.3 %collective-permute-done = bf16[4,64,768]{2,1,0:T(8,128)(2,1)S(1)} collective-permute-done((bf16[4,64,768]{2,1,0:T(8,128)(2,1)}, bf16[4,64,768]{2,1,0:T(8,128)(2,1)S(1)}, u32[]{:S(2)}, u32[]{:S(2)}) %collective-permute-start) | collective-permute-done | bytes 393248 | tf_op jit(solution)/shard_map/ppermute | solution.py:137
  128.2 2.0 add_convert_fusion
  130.2 2.0 collective-permute-start.1
  132.2 10.2 %collective-permute-done.1 = bf16[4,64,768]{2,1,0:T(8,128)(2,1)} collective-permute-done((bf16[4,64,768]{2,1,0:T(8,128)(2,1)}, bf16[4,64,768]{2,1,0:T(8,128)(2,1)}, u32[]{:S(2)}, u32[]{:S(2)}) %collective-permute-start.1) | collective-permute-done | bytes 393248 | tf_op jit(solution)/shard_map/ppermute | solution.py:137
  142.5 2.4 %fusion.17 = (bf16[4,64,768]{2,1,0:T(8,128)(2,1)S(1)}, f32[4,64,768]{2,1,0:T(8,128)}) fusion(f32[4,64,768]{2,1,0:T(8,128)} %get-tuple-element.17, bf16[4,64,768]{2,1,0:T(8,128)(2,1)} %collective-permute-done.2, bf16[4,64,768]{2,1,0:T(8,128)(2,1)} %collective-permute-done.1), kind=kLoop, calls=%fused_computation.38 | loop fusion | flops 983040 | bytes 2752512 | tf_op jit(solution)/shard_map/convert_element_type | solution.py:144
  144.8 0.7 dynamic-slice_bitcast_fusion.2
  145.5 4.7 %collective-permute-start.3 = (bf16[64,768]{1,0:T(8,128)(2,1)}, bf16[64,768]{1,0:T(8,128)(2,1)S(1)}, u32[]{:S(2)}, u32[]{:S(2)}) collective-permute-start(bf16[64,768]{1,0:T(8,128)(2,1)} %get-tuple-element.24), channel_id=1, source_target_pairs={{0,128},{32,160},{64,192},{96,224},{128,256},{160,288},{192,320},{... | collective-permute-start | bytes 294920 | tf_op jit(solution)/shard_map/ppermute | solution.py:137
  150.2 6.8 %collective-permute-start.4 = (bf16[64,768]{1,0:T(8,128)(2,1)}, bf16[64,768]{1,0:T(8,128)(2,1)S(1)}, u32[]{:S(2)}, u32[]{:S(2)}) collective-permute-start(bf16[64,768]{1,0:T(8,128)(2,1)} %get-tuple-element.26), channel_id=1, source_target_pairs={{0,256},{32,288},{64,320},{96,352},{128,384},{160,416},{192,448},{... | collective-permute-start | bytes 294920 | tf_op jit(solution)/shard_map/ppermute | solution.py:137
  157.0 5.0 %collective-permute-start.5 = (bf16[64,768]{1,0:T(8,128)(2,1)}, bf16[64,768]{1,0:T(8,128)(2,1)S(1)}, u32[]{:S(2)}, u32[]{:S(2)}) collective-permute-start(bf16[64,768]{1,0:T(8,128)(2,1)} %get-tuple-element.25), channel_id=1, source_target_pairs={{0,384},{32,416},{64,448},{96,480},{128,0},{160,32},{192,64},{224,... | collective-permute-start | bytes 294920 | tf_op jit(solution)/shard_map/ppermute | solution.py:137
  162.0 2.8 %collective-permute-done.4 = bf16[64,768]{1,0:T(8,128)(2,1)S(1)} collective-permute-done((bf16[64,768]{1,0:T(8,128)(2,1)}, bf16[64,768]{1,0:T(8,128)(2,1)S(1)}, u32[]{:S(2)}, u32[]{:S(2)}) %collective-permute-start.4) | collective-permute-done | bytes 98336 | tf_op jit(solution)/shard_map/ppermute | solution.py:137
  164.7 14.6 %collective-permute-done.5 = bf16[64,768]{1,0:T(8,128)(2,1)S(1)} collective-permute-done((bf16[64,768]{1,0:T(8,128)(2,1)}, bf16[64,768]{1,0:T(8,128)(2,1)S(1)}, u32[]{:S(2)}, u32[]{:S(2)}) %collective-permute-start.5) | collective-permute-done | bytes 98336 | tf_op jit(solution)/shard_map/ppermute | solution.py:137
  179.4 1.7 fusion.12
  181.0 1.5 multiply_reduce_fusion
  182.6 1.5 fusion
  184.0 1.9 reshape.85
  185.9 1.3 multiply_reduce_fusion.1
  187.3 0.6 reshape.86
  188.0 0.1 reduce_sum.42
  188.1 0.6 copy.19
  188.7 1.2 reduce_sum.40
  190.0 0.9 add_convert_fusion.1
  (21 shorter events, 0.1 us)
Async XLA Ops:
  7.2 76.7 %all-gather.2.cloned.1.call-start = ((), (), s32[]{:S(2)}) async-start(), calls=%async_computation.3 | async-start | bytes 5013504 | tf_op jit(solution)/shard_map/all_gather | solution.py:193
  8.9 3.9 %copy-start.6 = (f32[128,2]{0,1:T(2,128)S(1)}, f32[128,2]{0,1:T(2,128)}, u32[]{:S(2)}) copy-start(f32[128,2]{0,1:T(2,128)} %param.14) | copy-start | bytes 3076
  13.2 9.3 %copy-start.3 = (bf16[128,1024]{1,0:T(8,128)(2,1)S(1)}, bf16[128,1024]{1,0:T(8,128)(2,1)}, u32[]{:S(2)}) copy-start(bf16[128,1024]{1,0:T(8,128)(2,1)} %param.9) | copy-start | bytes 786436
  14.8 24.7 %all-to-all-start.1 = ((bf16[32,16,1024]{2,1,0:T(8,128)(2,1)}), bf16[32,16,1024]{2,1,0:T(8,128)(2,1)S(1)}, u32[]{:S(2)}, u32[]{:S(2)}) async-start(bf16[32,16,1024]{2,1,0:T(8,128)(2,1)} %bitcast.4), calls=%async_computation.1 | async-start | bytes 2097152 | tf_op jit(solution)/shard_map/all_to_all | solution.py:188
  39.5 44.4 %copy-start = (bf16[32,16,1024]{2,1,0:T(8,128)(2,1)}, bf16[32,16,1024]{2,1,0:T(8,128)(2,1)S(1)}, u32[]{:S(2)}) copy-start(bf16[32,16,1024]{2,1,0:T(8,128)(2,1)S(1)} %all-to-all-done.1) | copy-start | bytes 3145732
  39.5 20.8 %all-to-all-start = ((bf16[32,16,1024]{2,1,0:T(8,128)(2,1)}), bf16[32,16,1024]{2,1,0:T(8,128)(2,1)S(1)}, u32[]{:S(2)}, u32[]{:S(2)}) async-start(bf16[32,16,1024]{2,1,0:T(8,128)(2,1)} %bitcast.54), calls=%async_computation | async-start | bytes 2097152 | tf_op jit(solution)/shard_map/all_to_all | solution.py:187
  60.3 23.6 %copy-start.1 = (bf16[32,16,1024]{2,1,0:T(8,128)(2,1)}, bf16[32,16,1024]{2,1,0:T(8,128)(2,1)S(1)}, u32[]{:S(2)}) copy-start(bf16[32,16,1024]{2,1,0:T(8,128)(2,1)S(1)} %all-to-all-done) | copy-start | bytes 3145732
  99.8 81.2 %all-to-all-start.2 = ((bf16[32,16,2048]{2,1,0:T(8,128)(2,1)}), bf16[32,16,2048]{2,1,0:T(8,128)(2,1)S(1)}, u32[]{:S(2)}, u32[]{:S(2)}) async-start(bf16[32,16,2048]{2,1,0:T(8,128)(2,1)} %bitcast.52), calls=%async_computation.2 | async-start | bytes 4194304 | tf_op jit(solution)/shard_map/all_to_all | solution.py:197
  115.5 12.6 %collective-permute-start = (bf16[4,64,768]{2,1,0:T(8,128)(2,1)}, bf16[4,64,768]{2,1,0:T(8,128)(2,1)S(1)}, u32[]{:S(2)}, u32[]{:S(2)}) collective-permute-start(bf16[4,64,768]{2,1,0:T(8,128)(2,1)} %get-tuple-element.14), channel_id=1, source_target_pairs={{0,480},{32,0},{64,32},{96,64},{128,96},{160,128},{192,160},{224,1... | collective-permute-start | bytes 1179656 | tf_op jit(solution)/shard_map/ppermute | solution.py:137
  117.5 14.7 %collective-permute-start.2 = (bf16[4,64,768]{2,1,0:T(8,128)(2,1)}, bf16[4,64,768]{2,1,0:T(8,128)(2,1)}, u32[]{:S(2)}, u32[]{:S(2)}) collective-permute-start(bf16[4,64,768]{2,1,0:T(8,128)(2,1)} %get-tuple-element.16), channel_id=1, source_target_pairs={{0,32},{32,64},{64,96},{96,128},{128,160},{160,192},{192,224},{224... | collective-permute-start | bytes 1179656 | tf_op jit(solution)/shard_map/ppermute | solution.py:137
  130.2 12.3 %collective-permute-start.1 = (bf16[4,64,768]{2,1,0:T(8,128)(2,1)}, bf16[4,64,768]{2,1,0:T(8,128)(2,1)}, u32[]{:S(2)}, u32[]{:S(2)}) collective-permute-start(bf16[4,64,768]{2,1,0:T(8,128)(2,1)} %add_convert_fusion), channel_id=1, source_target_pairs={{0,480},{32,0},{64,32},{96,64},{128,96},{160,128},{192,160},{224,1... | collective-permute-start | bytes 1179656 | tf_op jit(solution)/shard_map/ppermute | solution.py:137
  145.5 16.4 %collective-permute-start.3 = (bf16[64,768]{1,0:T(8,128)(2,1)}, bf16[64,768]{1,0:T(8,128)(2,1)S(1)}, u32[]{:S(2)}, u32[]{:S(2)}) collective-permute-start(bf16[64,768]{1,0:T(8,128)(2,1)} %get-tuple-element.24), channel_id=1, source_target_pairs={{0,128},{32,160},{64,192},{96,224},{128,256},{160,288},{192,320},{... | collective-permute-start | bytes 294920 | tf_op jit(solution)/shard_map/ppermute | solution.py:137
  150.2 14.5 %collective-permute-start.4 = (bf16[64,768]{1,0:T(8,128)(2,1)}, bf16[64,768]{1,0:T(8,128)(2,1)S(1)}, u32[]{:S(2)}, u32[]{:S(2)}) collective-permute-start(bf16[64,768]{1,0:T(8,128)(2,1)} %get-tuple-element.26), channel_id=1, source_target_pairs={{0,256},{32,288},{64,320},{96,352},{128,384},{160,416},{192,448},{... | collective-permute-start | bytes 294920 | tf_op jit(solution)/shard_map/ppermute | solution.py:137
  157.0 22.4 %collective-permute-start.5 = (bf16[64,768]{1,0:T(8,128)(2,1)}, bf16[64,768]{1,0:T(8,128)(2,1)S(1)}, u32[]{:S(2)}, u32[]{:S(2)}) collective-permute-start(bf16[64,768]{1,0:T(8,128)(2,1)} %get-tuple-element.25), channel_id=1, source_target_pairs={{0,384},{32,416},{64,448},{96,480},{128,0},{160,32},{192,64},{224,... | collective-permute-start | bytes 294920 | tf_op jit(solution)/shard_map/ppermute | solution.py:137
  184.0 3.3 %copy-start.2 = (f32[256,1024]{1,0:T(8,128)S(1)}, f32[256,1024]{1,0:T(8,128)}, u32[]{:S(2)}) copy-start(f32[256,1024]{1,0:T(8,128)} %fusion) | copy-start | bytes 3145732
  187.3 2.7 %copy-start.4 = (bf16[128,1024]{1,0:T(8,128)(2,1)S(1)}, bf16[128,1024]{1,0:T(8,128)(2,1)}, u32[]{:S(2)}) copy-start(bf16[128,1024]{1,0:T(8,128)(2,1)} %param.11) | copy-start | bytes 786436
  187.3 2.7 %copy-start.5 = (bf16[128,1024]{1,0:T(8,128)(2,1)S(1)}, bf16[128,1024]{1,0:T(8,128)(2,1)}, u32[]{:S(2)}) copy-start(bf16[128,1024]{1,0:T(8,128)(2,1)} %param.10) | copy-start | bytes 786436
Sparse Core Ops, SparseCore 0:
  10.1 73.8 all-gather.1

commit v3 on v2

--- a/solution.py
+++ b/solution.py
@@ -1,3 +1,4 @@
+import functools
 import math
 
 import jax
@@ -16,11 +17,59 @@
     return lax.dot_general(a, b, ((over[:1], over[1:]), ((), ())), preferred_element_type=jnp.float32)
 
 
-def _hidden_kernel(
-    place, rows, cot, gate, up, hidden, slope, activated, send_two, send_one, own_three, own_zero, classes
-):
-    pre_gate = _dot(rows[...], gate[...], (1, 0))
-    pre_up = _dot(rows[...], up[...], (1, 0))
+def _fetches(place, shards, which, buffer, sems, steps):
+    groups = len(shards)
+    return [
+        [
+            pltpu.make_async_copy(
+                shards[k].at[which, :, pl.ds(j * BLOCK, BLOCK)],
+                buffer.at[j, (place[0] + k) % groups],
+                sems.at[j, k],
+            )
+            for k in range(groups)
+        ]
+        for j in range(steps)
+    ]
+
+
+def _start(fetches):
+    for copies in fetches:
+        for copy in copies:
+            copy.start()
+
+
+def _await(fetches, at):
+    for j, copies in enumerate(fetches):
+
+        @pl.when(at == j)
+        def _():
+            for copy in copies:
+                copy.wait()
+
+
+def _columns(buffer, at):
+    return buffer[at].reshape(buffer.shape[1] * buffer.shape[2], BLOCK)
+
+
+def _hidden_kernel(place, rows, cot, *refs, groups):
+    shards, refs = refs[:groups], refs[groups:]
+    hidden, slope, activated, send_two, send_one, own_three, own_zero = refs[:7]
+    gate_buffer, up_buffer, classes, gate_sems, up_sems = refs[7:]
+    at = pl.program_id(0)
+    steps = gate_buffer.shape[0]
+    gate_copies = _fetches(place, shards, 0, gate_buffer, gate_sems, steps)
+    up_copies = _fetches(place, shards, 1, up_buffer, up_sems, steps)
+
+    @pl.when(at == 0)
+    def _():
+        for j in range(steps):
+            _start(gate_copies[j : j + 1])
+            _start(up_copies[j : j + 1])
+
+    _await(gate_copies, at)
+    pre_gate = _dot(rows[...], _columns(gate_buffer, at), (1, 0))
+    _await(up_copies, at)
+    pre_up = _dot(rows[...], _columns(up_buffer, at), (1, 0))
     squashed = jax.nn.sigmoid(pre_gate)
     active = pre_gate * squashed
     here = (active * pre_up).astype(jnp.bfloat16)
@@ -35,28 +84,33 @@
         target[...] = classes[(place[0] + shift) % STRIDE].astype(target.dtype)
 
 
-def hidden_and_partial(place, rows, cot, mats, groups):
+def _buffers(names, steps, groups, block):
+    return [pltpu.VMEM((steps, groups, block, BLOCK), jnp.bfloat16) for _ in names]
+
+
+def hidden_and_partial(place, rows, cot, shards):
     slots, features = rows.shape
-    width = mats.shape[1] // 3
+    groups = len(shards)
+    _, block, width = shards[0].shape
     steps = width // BLOCK
-    members, block = groups // STRIDE, features // groups
+    members = groups // STRIDE
     whole = pl.BlockSpec((slots, features), lambda j, place: (0, 0))
     column = pl.BlockSpec((slots, BLOCK), lambda j, place: (0, j))
     part = pl.BlockSpec((members, block, BLOCK), lambda j, place: (0, 0, j))
     part_shape = (members, block, width)
     return pl.pallas_call(
-        _hidden_kernel,
+        functools.partial(_hidden_kernel, groups=groups),
         grid_spec=pltpu.PrefetchScalarGridSpec(
             num_scalar_prefetch=1,
             grid=(steps,),
-            in_specs=[
-                whole,
-                whole,
-                pl.BlockSpec((features, BLOCK), lambda j, place: (0, j)),
-                pl.BlockSpec((features, BLOCK), lambda j, place: (0, j + steps)),
+            in_specs=[whole, whole, *[pl.BlockSpec(memory_space=pl.ANY)] * groups],
+            out_specs=[column, column, column, part, part, part, part],
+            scratch_shapes=[
+                *_buffers(("gate", "up"), steps, groups, block),
+                pltpu.VMEM((STRIDE, members, block, BLOCK), jnp.float32),
+                pltpu.SemaphoreType.DMA((steps, groups)),
+                pltpu.SemaphoreType.DMA((steps, groups)),
             ],
-            out_specs=[column, column, column, part, part, part, part],
-            scratch_shapes=[pltpu.VMEM((STRIDE, members, block, BLOCK), jnp.float32)],
         ),
         out_shape=[
             jax.ShapeDtypeStruct((slots, width), jnp.bfloat16),
@@ -68,18 +122,37 @@
             jax.ShapeDtypeStruct(part_shape, jnp.float32),
         ],
         name="hidden_and_partial",
-    )(place, rows, cot, mats, mats)
-
-
-def _back_kernel(hidden, cot, slope, activated, gate, up, down_mat, back, out_sum, cot_sum):
+    )(place, rows, cot, *shards)
+
+
+def _back_kernel(place, hidden, cot, slope, activated, *refs, groups):
+    shards, refs = refs[:groups], refs[groups:]
+    back, gate_buffer, up_buffer, down_buffer, out_sum, cot_sum, gate_sems, up_sems, down_sems = refs
     at = pl.program_id(0)
     features = cot.shape[1]
-    down = down_mat[...]
+    steps = gate_buffer.shape[0]
+    gate_copies = _fetches(place, shards, 0, gate_buffer, gate_sems, steps)
+    up_copies = _fetches(place, shards, 1, up_buffer, up_sems, steps)
+    down_copies = _fetches(place, shards, 2, down_buffer, down_sems, steps)
+
+    @pl.when(at == 0)
+    def _():
+        for j in range(steps):
+            _start(down_copies[j : j + 1])
+            _start(gate_copies[j : j + 1])
+            _start(up_copies[j : j + 1])
+
+    _await(down_copies, at)
+    down = _columns(down_buffer, at)
     hidden_cot = _dot(cot[...], down, (1, 0))
     gate_cot = (hidden_cot * slope[...]).astype(jnp.bfloat16)
     up_cot = (hidden_cot * activated[...]).astype(jnp.bfloat16)
     out_part = _dot(hidden[...], down, (1, 1))
-    cot_part = _dot(gate_cot, gate[...], (1, 1)) + _dot(up_cot, up[...], (1, 1))
+    _await(gate_copies, at)
+    _await(up_copies, at)
+    cot_part = _dot(gate_cot, _columns(gate_buffer, at), (1, 1)) + _dot(
+        up_cot, _columns(up_buffer, at), (1, 1)
+    )
 
     @pl.when(at == 0)
     def _():
@@ -91,42 +164,87 @@
         out_sum[...] += out_part
         cot_sum[...] += cot_part
 
-    @pl.when(at == pl.num_programs(0) - 1)
+    @pl.when(at == steps - 1)
     def _():
         back[:, :features] = out_sum[...].astype(jnp.bfloat16)
         back[:, features:] = cot_sum[...].astype(jnp.bfloat16)
 
 
-def rows_back(hidden, cot, slope, activated, mats):
+def rows_back(place, hidden, cot, slope, activated, shards):
     slots, features = cot.shape
-    steps = hidden.shape[1] // BLOCK
-    column = pl.BlockSpec((slots, BLOCK), lambda j: (0, j))
+    groups = len(shards)
+    _, block, width = shards[0].shape
+    steps = width // BLOCK
+    column = pl.BlockSpec((slots, BLOCK), lambda j, place: (0, j))
     return pl.pallas_call(
-        _back_kernel,
-        grid=(steps,),
-        in_specs=[
-            column,
-            pl.BlockSpec((slots, features), lambda j: (0, 0)),
-            column,
-            column,
-            pl.BlockSpec((features, BLOCK), lambda j: (0, j)),
-            pl.BlockSpec((features, BLOCK), lambda j: (0, j + steps)),
-            pl.BlockSpec((features, BLOCK), lambda j: (0, j + 2 * steps)),
+        functools.partial(_back_kernel, groups=groups),
+        grid_spec=pltpu.PrefetchScalarGridSpec(
+            num_scalar_prefetch=1,
+            grid=(steps,),
+            in_specs=[
+                column,
+                pl.BlockSpec((slots, features), lambda j, place: (0, 0)),
+                column,
+                column,
+                *[pl.BlockSpec(memory_space=pl.ANY)] * groups,
+            ],
+            out_specs=pl.BlockSpec((slots, 2 * features), lambda j, place: (0, 0)),
+            scratch_shapes=[
+                *_buffers(("gate", "up", "down"), steps, groups, block),
+                pltpu.VMEM((slots, features), jnp.float32),
+                pltpu.VMEM((slots, features), jnp.float32),
+                *[pltpu.SemaphoreType.DMA((steps, groups))] * 3,
+            ],
+        ),
+        out_shape=jax.ShapeDtypeStruct((slots, 2 * features), jnp.bfloat16),
+        name="rows_back",
+    )(place, hidden, cot, slope, activated, *shards)
+
+
+def _finish_kernel(slot, gates, second_out, first_grad, second_grad, back, second_in, first_total, gate_grad):
+    count, features = second_out.shape
+    grad = second_grad[...].astype(jnp.float32)
+    combined, cot_sum = 0.0, 0.0
+    for k in range(slot.shape[1]):
+        numbers = lax.broadcasted_iota(jnp.int32, (count, back.shape[0]), 1)
+        chosen = (slot[:, k : k + 1] == numbers).astype(jnp.bfloat16)
+        out_row = _dot(chosen, back[:, :features], (1, 0))
+        combined += gates[:, k : k + 1] * out_row
+        gate_grad[:, k : k + 1] = jnp.sum(grad * out_row, axis=1, keepdims=True)
+        cot_sum += _dot(chosen, back[:, features:], (1, 0))
+    second_in[...] = (second_out[...].astype(jnp.float32) - combined).astype(jnp.bfloat16)
+    first_total[...] = (first_grad[...].astype(jnp.float32) + cot_sum).astype(jnp.bfloat16)
+
+
+def finish(slot, gates, second_out, first_grad, second_grad, back):
+    return pl.pallas_call(
+        _finish_kernel,
+        out_shape=[
+            jax.ShapeDtypeStruct(second_out.shape, jnp.bfloat16),
+            jax.ShapeDtypeStruct(first_grad.shape, jnp.bfloat16),
+            jax.ShapeDtypeStruct(gates.shape, jnp.float32),
         ],
-        out_specs=pl.BlockSpec((slots, 2 * features), lambda j: (0, 0)),
-        out_shape=jax.ShapeDtypeStruct((slots, 2 * features), jnp.bfloat16),
-        scratch_shapes=[
-            pltpu.VMEM((slots, features), jnp.float32),
-            pltpu.VMEM((slots, features), jnp.float32),
-        ],
-        name="rows_back",
-    )(hidden, cot, slope, activated, mats, mats, mats)
+        name="finish",
+    )(slot, gates, second_out, first_grad, second_grad, back)
 
 
 def to_slots(placing, assigned_rows):
     return lax.dot_general(
         placing, assigned_rows, (((0,), (0,)), ((), ())), preferred_element_type=jnp.float32
     ).astype(jnp.bfloat16)
+
+
+def around_ring(own, groups):
+    def ring(by, steps):
+        passed, value = [], own
+        for _ in range(steps):
+            value = lax.ppermute(value, "dp", [(i, (i + by) % groups) for i in range(groups)])
+            passed.append(value)
+        return passed
+
+    from_below = ring(1, groups // 2)
+    from_above = ring(-1, groups - 1 - groups // 2)
+    return [own, *from_above, *from_below[::-1]]
 
 
 def window_reduce(send_two, send_one, own_three, own_zero, groups):
@@ -189,11 +307,11 @@
     )
     rows_in = arrived_input.reshape(slots_all, feature_count)
     rows_cot = arrived_cot.reshape(slots_all, feature_count)
-    shards = jnp.concatenate([w_gate[0], w_up[0], w_down[0]], axis=1)
-    mats = lax.all_gather(shards, "dp", axis=0, tiled=True)
+    own = jnp.concatenate([w_gate, w_up, w_down], axis=0)
+    shards = around_ring(own, groups)
     place = lax.axis_index("dp").astype(jnp.int32).reshape(1)
-    hidden, slope, activated, *parts = hidden_and_partial(place, rows_in, rows_cot, mats, groups)
-    back_rows = rows_back(hidden, rows_cot, slope, activated, mats)
+    hidden, slope, activated, *parts = hidden_and_partial(place, rows_in, rows_cot, shards)
+    back_rows = rows_back(place, hidden, rows_cot, slope, activated, shards)
     back = lax.all_to_all(
         back_rows.reshape(owners, capacity, 2 * feature_count),
         "expert",
@@ -203,16 +321,14 @@
     ).reshape(slots_all, 2 * feature_count)
     grad_scale = 1.0 / math.sqrt(count_here * groups)
     w_down_grad = (window_reduce(*parts, groups) * grad_scale)[None]
-    out_assigned = jnp.dot(placing, back[:, :feature_count], preferred_element_type=jnp.float32)
-    cot_assigned = jnp.dot(placing, back[:, feature_count:], preferred_element_type=jnp.float32)
-    expert_out = out_assigned.reshape(count_here, top_count, feature_count)
-    combined = jnp.sum(gate_values[:, :, None] * expert_out, axis=1)
-    second_in = (second_out.astype(jnp.float32) - combined).astype(jnp.bfloat16)
-    gate_grad = jnp.sum(second_grad.astype(jnp.float32)[:, None, :] * expert_out, axis=2)
-    first_total = (
-        first_grad.astype(jnp.float32)
-        + jnp.sum(cot_assigned.reshape(count_here, top_count, feature_count), axis=1)
-    ).astype(jnp.bfloat16)
+    second_in, first_total, gate_grad = finish(
+        slot_index.reshape(count_here, top_count),
+        gate_values,
+        second_out,
+        first_grad,
+        second_grad,
+        back,
+    )
     return (second_in, first_total, gate_grad, w_down_grad)
 
 

time: 199 us -> 208 us (1.045)
  the two profiles are of different devices: /device:TPU:65 before, /device:TPU:96 now
where the time goes in v3:
time: 208 us; the launch traced here: 207 us
  starting transfers between devices  106 us (51%)
  waiting for transfers between devices  55.3 us (27%)
  Pallas kernels  26.2 us (13%)
  local copies, waits for them, and re-layouts  11.1 us (5%)
  other arithmetic  3.52 us (2%)
  matrix products  3.07 us (1%)
    ppermute x15, starting transfers between devices, ring(): lax.ppermute(value, 'dp', [(i, (i + by) % groups) for i in range(groups)])  54.5 us
    ppermute x6, waiting for transfers between devices, moved(): lax.ppermute(value, 'dp', [(i, (i + by) % groups) for i in range(groups)])  31.7 us
    ppermute x6, starting transfers between devices, moved(): lax.ppermute(value, 'dp', [(i, (i + by) % groups) for i in range(groups)])  30.2 us
    ppermute x15, waiting for transfers between devices, ring(): lax.ppermute(value, 'dp', [(i, (i + by) % groups) for i in range(groups)])  23.6 us
    pallas_call x1, Pallas kernels, rows_back(): pl.pallas_call(functools.partial(_back_kernel, groups=groups), grid_spec=...  12.1 us
    pallas_call x1, Pallas kernels, hidden_and_partial(): pl.pallas_call(functools.partial(_hidden_kernel, groups=groups), grid_spe...  10.6 us
    all_to_all x1, starting transfers between devices, per_device(): lax.all_to_all(send_cot, 'expert', split_axis=0, concat_axis=0, tiled=True)  7.33 us
    all_to_all x1, starting transfers between devices, per_device(): lax.all_to_all(send_input, 'expert', split_axis=0, concat_axis=0, tiled=T...  7.09 us
  transfers between devices with their start and end apart: 24, of which 10 were waited for; matrix products, arithmetic and copies ran while one was open for 6% of the time, Pallas kernels for 0%

profile of v3, /device:TPU:96, one launch (start us, length us, event | category | flops | bytes accessed | tf_op | source)
XLA Modules:
  0.0 206.7 jit_solution(7027907871945894928)
XLA Ops:
  0.6 0.9 constant_dynamic-update-slice_fusion.2
  1.5 0.9 constant_dynamic-update-slice_fusion.1
  2.4 0.9 constant_dynamic-update-slice_fusion.refs_0_
  3.3 5.0 %collective-permute-start.7 = (bf16[3,64,768]{2,1,0:T(8,128)(2,1)S(1)}, bf16[3,64,768]{2,1,0:T(8,128)(2,1)S(1)}, u32[]{:S(2)}, u32[]{:S(2)}) collective-permute-start(bf16[3,64,768]{2,1,0:T(8,128)(2,1)S(1)} %constant_dynamic-update-slice_fusion.refs_0_), channel_id=1, source_target_pairs={{0,32},{32,64},{64,96},{96,128},{128,160},{160,192},{192,224},{224... | collective-permute-start | bytes 884744 | tf_op jit(solution)/shard_map/ppermute | solution.py:241
  8.4 1.9 collective-permute-start
  10.3 0.8 copy.25
  12.2 0.8 copy.30.gates
  13.2 1.2 broadcast_in_dim.7
  15.2 5.3 %collective-permute-start.8 = (bf16[3,64,768]{2,1,0:T(8,128)(2,1)S(1)}, bf16[3,64,768]{2,1,0:T(8,128)(2,1)S(1)}, u32[]{:S(2)}, u32[]{:S(2)}) collective-permute-start(bf16[3,64,768]{2,1,0:T(8,128)(2,1)S(1)} %collective-permute-done.7.refs_15_), channel_id=1, source_target_pairs={{0,32},{32,64},{64,96},{96,128},{128,160},{160,192},{192,224},{224... | collective-permute-start | bytes 884744 | tf_op jit(solution)/shard_map/ppermute | solution.py:241
  20.5 1.5 convolution_convert_fusion
  22.1 7.3 %all-to-all-start.1 = ((bf16[32,16,1024]{2,1,0:T(8,128)(2,1)}), bf16[32,16,1024]{2,1,0:T(8,128)(2,1)S(1)}, u32[]{:S(2)}, u32[]{:S(2)}) async-start(bf16[32,16,1024]{2,1,0:T(8,128)(2,1)} %bitcast.4), calls=%async_computation.1 | async-start | bytes 2097152 | tf_op jit(solution)/shard_map/all_to_all | solution.py:306
  29.4 1.9 collective-permute-start.1
  31.4 5.1 %collective-permute-start.9 = (bf16[3,64,768]{2,1,0:T(8,128)(2,1)S(1)}, bf16[3,64,768]{2,1,0:T(8,128)(2,1)S(1)}, u32[]{:S(2)}, u32[]{:S(2)}) collective-permute-start(bf16[3,64,768]{2,1,0:T(8,128)(2,1)S(1)} %collective-permute-done.8.refs_14_), channel_id=1, source_target_pairs={{0,32},{32,64},{64,96},{96,128},{128,160},{160,192},{192,224},{224... | collective-permute-start | bytes 884744 | tf_op jit(solution)/shard_map/ppermute | solution.py:241
  36.5 5.2 %collective-permute-done.1.refs_2_ = bf16[3,64,768]{2,1,0:T(8,128)(2,1)S(1)} collective-permute-done((bf16[3,64,768]{2,1,0:T(8,128)(2,1)S(1)}, bf16[3,64,768]{2,1,0:T(8,128)(2,1)S(1)}, u32[]{:S(2)}, u32[]{:S(2)}) %collective-permute-start.1) | collective-permute-done | bytes 294944 | tf_op jit(solution)/shard_map/ppermute | solution.py:241
  41.7 1.9 collective-permute-start.2
  43.7 5.1 %collective-permute-start.10 = (bf16[3,64,768]{2,1,0:T(8,128)(2,1)S(1)}, bf16[3,64,768]{2,1,0:T(8,128)(2,1)}, u32[]{:S(2)}, u32[]{:S(2)}) collective-permute-start(bf16[3,64,768]{2,1,0:T(8,128)(2,1)S(1)} %collective-permute-done.9.refs_13_), channel_id=1, source_target_pairs={{0,32},{32,64},{64,96},{96,128},{128,160},{160,192},{192,224},{224... | collective-permute-start | bytes 884744 | tf_op jit(solution)/shard_map/ppermute | solution.py:241
  49.3 4.0 %collective-permute-done.2.refs_3_ = bf16[3,64,768]{2,1,0:T(8,128)(2,1)} collective-permute-done((bf16[3,64,768]{2,1,0:T(8,128)(2,1)S(1)}, bf16[3,64,768]{2,1,0:T(8,128)(2,1)}, u32[]{:S(2)}, u32[]{:S(2)}) %collective-permute-start.2) | collective-permute-done | bytes 294944 | tf_op jit(solution)/shard_map/ppermute | solution.py:241
  53.2 1.9 collective-permute-start.3
  55.2 5.1 %collective-permute-start.11 = (bf16[3,64,768]{2,1,0:T(8,128)(2,1)}, bf16[3,64,768]{2,1,0:T(8,128)(2,1)}, u32[]{:S(2)}, u32[]{:S(2)}) collective-permute-start(bf16[3,64,768]{2,1,0:T(8,128)(2,1)} %collective-permute-done.10.refs_12_), channel_id=1, source_target_pairs={{0,32},{32,64},{64,96},{96,128},{128,160},{160,192},{192,224},{224... | collective-permute-start | bytes 884744 | tf_op jit(solution)/shard_map/ppermute | solution.py:241
  60.3 1.5 convolution_convert_fusion.1
  61.9 7.1 %all-to-all-start = ((bf16[32,16,1024]{2,1,0:T(8,128)(2,1)}), bf16[32,16,1024]{2,1,0:T(8,128)(2,1)S(1)}, u32[]{:S(2)}, u32[]{:S(2)}) async-start(bf16[32,16,1024]{2,1,0:T(8,128)(2,1)} %bitcast.2), calls=%async_computation | async-start | bytes 2097152 | tf_op jit(solution)/shard_map/all_to_all | solution.py:305
  69.0 1.9 collective-permute-start.4
  70.9 5.1 %collective-permute-start.12 = (bf16[3,64,768]{2,1,0:T(8,128)(2,1)}, bf16[3,64,768]{2,1,0:T(8,128)(2,1)S(1)}, u32[]{:S(2)}, u32[]{:S(2)}) collective-permute-start(bf16[3,64,768]{2,1,0:T(8,128)(2,1)} %collective-permute-done.11.refs_11_), channel_id=1, source_target_pairs={{0,32},{32,64},{64,96},{96,128},{128,160},{160,192},{192,224},{224... | collective-permute-start | bytes 884744 | tf_op jit(solution)/shard_map/ppermute | solution.py:241
  76.1 5.4 %collective-permute-done.4.refs_5_ = bf16[3,64,768]{2,1,0:T(8,128)(2,1)S(1)} collective-permute-done((bf16[3,64,768]{2,1,0:T(8,128)(2,1)}, bf16[3,64,768]{2,1,0:T(8,128)(2,1)S(1)}, u32[]{:S(2)}, u32[]{:S(2)}) %collective-permute-start.4) | collective-permute-done | bytes 294944 | tf_op jit(solution)/shard_map/ppermute | solution.py:241
  81.5 1.9 collective-permute-start.5
  83.4 5.1 %collective-permute-start.13 = (bf16[3,64,768]{2,1,0:T(8,128)(2,1)S(1)}, bf16[3,64,768]{2,1,0:T(8,128)(2,1)S(1)}, u32[]{:S(2)}, u32[]{:S(2)}) collective-permute-start(bf16[3,64,768]{2,1,0:T(8,128)(2,1)S(1)} %collective-permute-done.12.refs_10_), channel_id=1, source_target_pairs={{0,32},{32,64},{64,96},{96,128},{128,160},{160,192},{192,224},{224... | collective-permute-start | bytes 884744 | tf_op jit(solution)/shard_map/ppermute | solution.py:241
  88.6 4.3 %collective-permute-done.5.refs_6_ = bf16[3,64,768]{2,1,0:T(8,128)(2,1)S(1)} collective-permute-done((bf16[3,64,768]{2,1,0:T(8,128)(2,1)S(1)}, bf16[3,64,768]{2,1,0:T(8,128)(2,1)S(1)}, u32[]{:S(2)}, u32[]{:S(2)}) %collective-permute-start.5) | collective-permute-done | bytes 294944 | tf_op jit(solution)/shard_map/ppermute | solution.py:241
  92.9 1.9 collective-permute-start.6
  94.9 5.1 %collective-permute-start.14 = (bf16[3,64,768]{2,1,0:T(8,128)(2,1)S(1)}, bf16[3,64,768]{2,1,0:T(8,128)(2,1)}, u32[]{:S(2)}, u32[]{:S(2)}) collective-permute-start(bf16[3,64,768]{2,1,0:T(8,128)(2,1)S(1)} %collective-permute-done.13.refs_9_), channel_id=1, source_target_pairs={{0,32},{32,64},{64,96},{96,128},{128,160},{160,192},{192,224},{224... | collective-permute-start | bytes 884744 | tf_op jit(solution)/shard_map/ppermute | solution.py:241
  100.0 3.6 %collective-permute-done.6.refs_7_ = bf16[3,64,768]{2,1,0:T(8,128)(2,1)} collective-permute-done((bf16[3,64,768]{2,1,0:T(8,128)(2,1)S(1)}, bf16[3,64,768]{2,1,0:T(8,128)(2,1)}, u32[]{:S(2)}, u32[]{:S(2)}) %collective-permute-start.6) | collective-permute-done | bytes 294944 | tf_op jit(solution)/shard_map/ppermute | solution.py:241
  103.6 1.1 collective-permute-done.14.refs_8_
  104.7 10.6 %hidden_and_partial.1 = (bf16[512,768]{1,0:T(8,128)(2,1)}, f32[512,768]{1,0:T(8,128)}, f32[512,768]{1,0:T(8,128)}, bf16[4,64,768]{2,1,0:T(8,128)(2,1)}, bf16[4,6...) custom-call(s32[1]{0:T(128)} %bitcast.1.place, bf16[512,1024]{1,0:T(8,128)(2,1)} %bitcast.49, ...), custom_call_target="tpu_custom_call" | custom-call | tf_op jit(solution)/shard_map/hidden_and_partial/pallas_call | solution.py:101
  115.4 12.1 %rows_back.1 = bf16[512,2048]{1,0:T(8,128)(2,1)} custom-call(s32[1]{0:T(128)} %bitcast.1.place, bf16[512,768]{1,0:T(8,128)(2,1)} %get-tuple-element.14.hidden, bf16[512,1024]{1,0:T(8,128)(2,1)} %bitcast.46, f32[512,768]{1,0:T(8,128)} %get-tuple-element.15.slope, f32[512,768]{1,0:T(8,128)} %get-tuple-element.16.activated, bf16[3,64,768]{2,1,0:T(8,128)(2,1)} %copy-done.3, ...), custom_call_target="tpu_custom_call" | custom-call | tf_op jit(solution)/shard_map/rows_back/pallas_call | solution.py:179
  127.5 7.1 %all-to-all-start.2 = ((bf16[32,16,2048]{2,1,0:T(8,128)(2,1)}), bf16[32,16,2048]{2,1,0:T(8,128)(2,1)S(1)}, u32[]{:S(2)}, u32[]{:S(2)}) async-start(bf16[32,16,2048]{2,1,0:T(8,128)(2,1)} %bitcast.48), calls=%async_computation.2 | async-start | bytes 4194304 | tf_op jit(solution)/shard_map/all_to_all | solution.py:315
  134.5 3.3 %collective-permute-start.15 = (bf16[4,64,768]{2,1,0:T(8,128)(2,1)S(1)}, bf16[4,64,768]{2,1,0:T(8,128)(2,1)S(1)}, u32[]{:S(2)}, u32[]{:S(2)}) collective-permute-start(bf16[4,64,768]{2,1,0:T(8,128)(2,1)S(1)} %copy-done.17), channel_id=1, source_target_pairs={{0,480},{32,0},{64,32},{96,64},{128,96},{160,128},{192,160},{224,1... | collective-permute-start | bytes 1179656 | tf_op jit(solution)/shard_map/ppermute | solution.py:255
  137.8 4.4 %collective-permute-start.17 = (bf16[4,64,768]{2,1,0:T(8,128)(2,1)}, bf16[4,64,768]{2,1,0:T(8,128)(2,1)}, u32[]{:S(2)}, u32[]{:S(2)}) collective-permute-start(bf16[4,64,768]{2,1,0:T(8,128)(2,1)} %get-tuple-element.22), channel_id=1, source_target_pairs={{0,32},{32,64},{64,96},{96,128},{128,160},{160,192},{192,224},{224... | collective-permute-start | bytes 1179656 | tf_op jit(solution)/shard_map/ppermute | solution.py:255
  142.2 7.6 %collective-permute-done.15 = bf16[4,64,768]{2,1,0:T(8,128)(2,1)S(1)} collective-permute-done((bf16[4,64,768]{2,1,0:T(8,128)(2,1)S(1)}, bf16[4,64,768]{2,1,0:T(8,128)(2,1)S(1)}, u32[]{:S(2)}, u32[]{:S(2)}) %collective-permute-start.15) | collective-permute-done | bytes 393248 | tf_op jit(solution)/shard_map/ppermute | solution.py:255
  149.9 1.9 collective-permute-start.16
  152.3 11.4 %collective-permute-done.16 = bf16[4,64,768]{2,1,0:T(8,128)(2,1)S(1)} collective-permute-done((bf16[4,64,768]{2,1,0:T(8,128)(2,1)S(1)}, bf16[4,64,768]{2,1,0:T(8,128)(2,1)S(1)}, u32[]{:S(2)}, u32[]{:S(2)}) %collective-permute-start.16) | collective-permute-done | bytes 393248 | tf_op jit(solution)/shard_map/ppermute | solution.py:255
  163.7 1.4 fusion.11
  165.7 9.1 %collective-permute-start.18 = (bf16[64,768]{1,0:T(8,128)(2,1)}, bf16[64,768]{1,0:T(8,128)(2,1)S(1)}, u32[]{:S(2)}, u32[]{:S(2)}) collective-permute-start(bf16[64,768]{1,0:T(8,128)(2,1)} %get-tuple-element.38), channel_id=1, source_target_pairs={{0,128},{32,160},{64,192},{96,224},{128,256},{160,288},{192,320},{... | collective-permute-start | bytes 294920 | tf_op jit(solution)/shard_map/ppermute | solution.py:255
  174.8 5.1 %collective-permute-start.19 = (bf16[64,768]{1,0:T(8,128)(2,1)S(1)}, bf16[64,768]{1,0:T(8,128)(2,1)S(1)}, u32[]{:S(2)}, u32[]{:S(2)}) collective-permute-start(bf16[64,768]{1,0:T(8,128)(2,1)S(1)} %get-tuple-element.40), channel_id=1, source_target_pairs={{0,256},{32,288},{64,320},{96,352},{128,384},{160,416},{192,448},{... | collective-permute-start | bytes 294920 | tf_op jit(solution)/shard_map/ppermute | solution.py:255
  179.9 6.5 %collective-permute-start.20 = (bf16[64,768]{1,0:T(8,128)(2,1)S(1)}, bf16[64,768]{1,0:T(8,128)(2,1)S(1)}, u32[]{:S(2)}, u32[]{:S(2)}) collective-permute-start(bf16[64,768]{1,0:T(8,128)(2,1)S(1)} %get-tuple-element.39), channel_id=1, source_target_pairs={{0,384},{32,416},{64,448},{96,480},{128,0},{160,32},{192,64},{224,... | collective-permute-start | bytes 294920 | tf_op jit(solution)/shard_map/ppermute | solution.py:255
  187.3 12.3 %collective-permute-done.19 = bf16[64,768]{1,0:T(8,128)(2,1)S(1)} collective-permute-done((bf16[64,768]{1,0:T(8,128)(2,1)S(1)}, bf16[64,768]{1,0:T(8,128)(2,1)S(1)}, u32[]{:S(2)}, u32[]{:S(2)}) %collective-permute-start.19) | collective-permute-done | bytes 98336 | tf_op jit(solution)/shard_map/ppermute | solution.py:255
  199.6 0.7 fusion.6
  200.3 1.4 copy-done.1
  201.7 3.5 %finish.1 = (bf16[128,1024]{1,0:T(8,128)(2,1)}, bf16[128,1024]{1,0:T(8,128)(2,1)}, f32[128,2]{1,0:T(8,128)}) custom-call(s32[128,2]{1,0:T(8,128)} %add.65.slot, f32[128,2]{1,0:T(8,128)} %copy-done.14, bf16[128,1024]{1,0:T(8,128)(2,1)} %second_out.1, bf16[128,1024]{1,0:T(8,128)(2,1)} %first_grad.1, bf16[128,1024]{1,0:T(8,128)(2,1)} %second_grad.1, ...), custom_call_target="tpu_custom_call" | custom-call | tf_op jit(solution)/shard_map/finish/pallas_call | solution.py:220
  205.2 1.5 copy.31
  (69 shorter events, 4.6 us)
Async XLA Ops:
  3.3 18.7 %copy-start.3 = (bf16[3,64,768]{2,1,0:T(8,128)(2,1)}, bf16[3,64,768]{2,1,0:T(8,128)(2,1)S(1)}, u32[]{:S(2)}) copy-start(bf16[3,64,768]{2,1,0:T(8,128)(2,1)S(1)} %constant_dynamic-update-slice_fusion.refs_0_) | copy-start | bytes 884740
  3.3 11.9 %collective-permute-start.7 = (bf16[3,64,768]{2,1,0:T(8,128)(2,1)S(1)}, bf16[3,64,768]{2,1,0:T(8,128)(2,1)S(1)}, u32[]{:S(2)}, u32[]{:S(2)}) collective-permute-start(bf16[3,64,768]{2,1,0:T(8,128)(2,1)S(1)} %constant_dynamic-update-slice_fusion.refs_0_), channel_id=1, source_target_pairs={{0,32},{32,64},{64,96},{96,128},{128,160},{160,192},{192,224},{224... | collective-permute-start | bytes 884744 | tf_op jit(solution)/shard_map/ppermute | solution.py:241
  8.4 21.0 %collective-permute-start = (bf16[3,64,768]{2,1,0:T(8,128)(2,1)S(1)}, bf16[3,64,768]{2,1,0:T(8,128)(2,1)S(1)}, u32[]{:S(2)}, u32[]{:S(2)}) collective-permute-start(bf16[3,64,768]{2,1,0:T(8,128)(2,1)S(1)} %constant_dynamic-update-slice_fusion.refs_0_), channel_id=1, source_target_pairs={{0,480},{32,0},{64,32},{96,64},{128,96},{160,128},{192,160},{224,1... | collective-permute-start | bytes 884744 | tf_op jit(solution)/shard_map/ppermute | solution.py:241
  13.0 9.1 %copy-start.14 = (f32[128,2]{1,0:T(8,128)}, f32[128,2]{1,0:T(8,128)S(1)}, u32[]{:S(2)}) copy-start(f32[128,2]{1,0:T(8,128)S(1)} %copy.30.gates) | copy-start | bytes 3076
  15.2 33.6 %copy-start.15 = (bf16[128,1024]{1,0:T(8,128)(2,1)S(1)}, bf16[128,1024]{1,0:T(8,128)(2,1)}, u32[]{:S(2)}) copy-start(bf16[128,1024]{1,0:T(8,128)(2,1)} %param.9) | copy-start | bytes 786436
  15.2 6.8 %copy-start.4 = (bf16[3,64,768]{2,1,0:T(8,128)(2,1)}, bf16[3,64,768]{2,1,0:T(8,128)(2,1)S(1)}, u32[]{:S(2)}) copy-start(bf16[3,64,768]{2,1,0:T(8,128)(2,1)S(1)} %collective-permute-done.7.refs_15_) | copy-start | bytes 884740
  15.2 16.1 %collective-permute-start.8 = (bf16[3,64,768]{2,1,0:T(8,128)(2,1)S(1)}, bf16[3,64,768]{2,1,0:T(8,128)(2,1)S(1)}, u32[]{:S(2)}, u32[]{:S(2)}) collective-permute-start(bf16[3,64,768]{2,1,0:T(8,128)(2,1)S(1)} %collective-permute-done.7.refs_15_), channel_id=1, source_target_pairs={{0,32},{32,64},{64,96},{96,128},{128,160},{160,192},{192,224},{224... | collective-permute-start | bytes 884744 | tf_op jit(solution)/shard_map/ppermute | solution.py:241
  22.1 39.8 %all-to-all-start.1 = ((bf16[32,16,1024]{2,1,0:T(8,128)(2,1)}), bf16[32,16,1024]{2,1,0:T(8,128)(2,1)S(1)}, u32[]{:S(2)}, u32[]{:S(2)}) async-start(bf16[32,16,1024]{2,1,0:T(8,128)(2,1)} %bitcast.4), calls=%async_computation.1 | async-start | bytes 2097152 | tf_op jit(solution)/shard_map/all_to_all | solution.py:306
  29.4 32.4 %copy-start.5 = (bf16[3,64,768]{2,1,0:T(8,128)(2,1)}, bf16[3,64,768]{2,1,0:T(8,128)(2,1)S(1)}, u32[]{:S(2)}) copy-start(bf16[3,64,768]{2,1,0:T(8,128)(2,1)S(1)} %collective-permute-done.refs_1_) | copy-start | bytes 884740
  29.4 12.3 %collective-permute-start.1 = (bf16[3,64,768]{2,1,0:T(8,128)(2,1)S(1)}, bf16[3,64,768]{2,1,0:T(8,128)(2,1)S(1)}, u32[]{:S(2)}, u32[]{:S(2)}) collective-permute-start(bf16[3,64,768]{2,1,0:T(8,128)(2,1)S(1)} %collective-permute-done.refs_1_), channel_id=1, source_target_pairs={{0,480},{32,0},{64,32},{96,64},{128,96},{160,128},{192,160},{224,1... | collective-permute-start | bytes 884744 | tf_op jit(solution)/shard_map/ppermute | solution.py:241
  31.4 30.5 %copy-start.6 = (bf16[3,64,768]{2,1,0:T(8,128)(2,1)}, bf16[3,64,768]{2,1,0:T(8,128)(2,1)S(1)}, u32[]{:S(2)}) copy-start(bf16[3,64,768]{2,1,0:T(8,128)(2,1)S(1)} %collective-permute-done.8.refs_14_) | copy-start | bytes 884740
  31.4 12.3 %collective-permute-start.9 = (bf16[3,64,768]{2,1,0:T(8,128)(2,1)S(1)}, bf16[3,64,768]{2,1,0:T(8,128)(2,1)S(1)}, u32[]{:S(2)}, u32[]{:S(2)}) collective-permute-start(bf16[3,64,768]{2,1,0:T(8,128)(2,1)S(1)} %collective-permute-done.8.refs_14_), channel_id=1, source_target_pairs={{0,32},{32,64},{64,96},{96,128},{128,160},{160,192},{192,224},{224... | collective-permute-start | bytes 884744 | tf_op jit(solution)/shard_map/ppermute | solution.py:241
  41.7 20.1 %copy-start.7 = (bf16[3,64,768]{2,1,0:T(8,128)(2,1)}, bf16[3,64,768]{2,1,0:T(8,128)(2,1)S(1)}, u32[]{:S(2)}) copy-start(bf16[3,64,768]{2,1,0:T(8,128)(2,1)S(1)} %collective-permute-done.1.refs_2_) | copy-start | bytes 884740
  41.7 11.5 %collective-permute-start.2 = (bf16[3,64,768]{2,1,0:T(8,128)(2,1)S(1)}, bf16[3,64,768]{2,1,0:T(8,128)(2,1)}, u32[]{:S(2)}, u32[]{:S(2)}) collective-permute-start(bf16[3,64,768]{2,1,0:T(8,128)(2,1)S(1)} %collective-permute-done.1.refs_2_), channel_id=1, source_target_pairs={{0,480},{32,0},{64,32},{96,64},{128,96},{160,128},{192,160},{224,1... | collective-permute-start | bytes 884744 | tf_op jit(solution)/shard_map/ppermute | solution.py:241
  43.6 18.2 %copy-start.8 = (bf16[3,64,768]{2,1,0:T(8,128)(2,1)}, bf16[3,64,768]{2,1,0:T(8,128)(2,1)S(1)}, u32[]{:S(2)}) copy-start(bf16[3,64,768]{2,1,0:T(8,128)(2,1)S(1)} %collective-permute-done.9.refs_13_) | copy-start | bytes 884740
  43.7 11.5 %collective-permute-start.10 = (bf16[3,64,768]{2,1,0:T(8,128)(2,1)S(1)}, bf16[3,64,768]{2,1,0:T(8,128)(2,1)}, u32[]{:S(2)}, u32[]{:S(2)}) collective-permute-start(bf16[3,64,768]{2,1,0:T(8,128)(2,1)S(1)} %collective-permute-done.9.refs_13_), channel_id=1, source_target_pairs={{0,32},{32,64},{64,96},{96,128},{128,160},{160,192},{192,224},{224... | collective-permute-start | bytes 884744 | tf_op jit(solution)/shard_map/ppermute | solution.py:241
  53.2 15.7 %collective-permute-start.3 = (bf16[3,64,768]{2,1,0:T(8,128)(2,1)}, bf16[3,64,768]{2,1,0:T(8,128)(2,1)}, u32[]{:S(2)}, u32[]{:S(2)}) collective-permute-start(bf16[3,64,768]{2,1,0:T(8,128)(2,1)} %collective-permute-done.2.refs_3_), channel_id=1, source_target_pairs={{0,480},{32,0},{64,32},{96,64},{128,96},{160,128},{192,160},{224,1... | collective-permute-start | bytes 884744 | tf_op jit(solution)/shard_map/ppermute | solution.py:241
  55.2 15.7 %collective-permute-start.11 = (bf16[3,64,768]{2,1,0:T(8,128)(2,1)}, bf16[3,64,768]{2,1,0:T(8,128)(2,1)}, u32[]{:S(2)}, u32[]{:S(2)}) collective-permute-start(bf16[3,64,768]{2,1,0:T(8,128)(2,1)} %collective-permute-done.10.refs_12_), channel_id=1, source_target_pairs={{0,32},{32,64},{64,96},{96,128},{128,160},{160,192},{192,224},{224... | collective-permute-start | bytes 884744 | tf_op jit(solution)/shard_map/ppermute | solution.py:241
  61.8 42.8 %copy-start = (bf16[32,16,1024]{2,1,0:T(8,128)(2,1)}, bf16[32,16,1024]{2,1,0:T(8,128)(2,1)S(1)}, u32[]{:S(2)}) copy-start(bf16[32,16,1024]{2,1,0:T(8,128)(2,1)S(1)} %all-to-all-done.1) | copy-start | bytes 3145732
  61.9 38.1 %all-to-all-start = ((bf16[32,16,1024]{2,1,0:T(8,128)(2,1)}), bf16[32,16,1024]{2,1,0:T(8,128)(2,1)S(1)}, u32[]{:S(2)}, u32[]{:S(2)}) async-start(bf16[32,16,1024]{2,1,0:T(8,128)(2,1)} %bitcast.2), calls=%async_computation | async-start | bytes 2097152 | tf_op jit(solution)/shard_map/all_to_all | solution.py:305
  69.0 12.5 %collective-permute-start.4 = (bf16[3,64,768]{2,1,0:T(8,128)(2,1)}, bf16[3,64,768]{2,1,0:T(8,128)(2,1)S(1)}, u32[]{:S(2)}, u32[]{:S(2)}) collective-permute-start(bf16[3,64,768]{2,1,0:T(8,128)(2,1)} %collective-permute-done.3.refs_4_), channel_id=1, source_target_pairs={{0,480},{32,0},{64,32},{96,64},{128,96},{160,128},{192,160},{224,1... | collective-permute-start | bytes 884744 | tf_op jit(solution)/shard_map/ppermute | solution.py:241
  70.9 12.5 %collective-permute-start.12 = (bf16[3,64,768]{2,1,0:T(8,128)(2,1)}, bf16[3,64,768]{2,1,0:T(8,128)(2,1)S(1)}, u32[]{:S(2)}, u32[]{:S(2)}) collective-permute-start(bf16[3,64,768]{2,1,0:T(8,128)(2,1)} %collective-permute-done.11.refs_11_), channel_id=1, source_target_pairs={{0,32},{32,64},{64,96},{96,128},{128,160},{160,192},{192,224},{224... | collective-permute-start | bytes 884744 | tf_op jit(solution)/shard_map/ppermute | solution.py:241
  81.5 23.2 %copy-start.9 = (bf16[3,64,768]{2,1,0:T(8,128)(2,1)}, bf16[3,64,768]{2,1,0:T(8,128)(2,1)S(1)}, u32[]{:S(2)}) copy-start(bf16[3,64,768]{2,1,0:T(8,128)(2,1)S(1)} %collective-permute-done.4.refs_5_) | copy-start | bytes 884740
  81.5 11.4 %collective-permute-start.5 = (bf16[3,64,768]{2,1,0:T(8,128)(2,1)S(1)}, bf16[3,64,768]{2,1,0:T(8,128)(2,1)S(1)}, u32[]{:S(2)}, u32[]{:S(2)}) collective-permute-start(bf16[3,64,768]{2,1,0:T(8,128)(2,1)S(1)} %collective-permute-done.4.refs_5_), channel_id=1, source_target_pairs={{0,480},{32,0},{64,32},{96,64},{128,96},{160,128},{192,160},{224,1... | collective-permute-start | bytes 884744 | tf_op jit(solution)/shard_map/ppermute | solution.py:241
  83.4 21.3 %copy-start.10 = (bf16[3,64,768]{2,1,0:T(8,128)(2,1)}, bf16[3,64,768]{2,1,0:T(8,128)(2,1)S(1)}, u32[]{:S(2)}) copy-start(bf16[3,64,768]{2,1,0:T(8,128)(2,1)S(1)} %collective-permute-done.12.refs_10_) | copy-start | bytes 884740
  83.4 11.4 %collective-permute-start.13 = (bf16[3,64,768]{2,1,0:T(8,128)(2,1)S(1)}, bf16[3,64,768]{2,1,0:T(8,128)(2,1)S(1)}, u32[]{:S(2)}, u32[]{:S(2)}) collective-permute-start(bf16[3,64,768]{2,1,0:T(8,128)(2,1)S(1)} %collective-permute-done.12.refs_10_), channel_id=1, source_target_pairs={{0,32},{32,64},{64,96},{96,128},{128,160},{160,192},{192,224},{224... | collective-permute-start | bytes 884744 | tf_op jit(solution)/shard_map/ppermute | solution.py:241
  92.9 11.8 %copy-start.11 = (bf16[3,64,768]{2,1,0:T(8,128)(2,1)}, bf16[3,64,768]{2,1,0:T(8,128)(2,1)S(1)}, u32[]{:S(2)}) copy-start(bf16[3,64,768]{2,1,0:T(8,128)(2,1)S(1)} %collective-permute-done.5.refs_6_) | copy-start | bytes 884740
  92.9 10.7 %collective-permute-start.6 = (bf16[3,64,768]{2,1,0:T(8,128)(2,1)S(1)}, bf16[3,64,768]{2,1,0:T(8,128)(2,1)}, u32[]{:S(2)}, u32[]{:S(2)}) collective-permute-start(bf16[3,64,768]{2,1,0:T(8,128)(2,1)S(1)} %collective-permute-done.5.refs_6_), channel_id=1, source_target_pairs={{0,480},{32,0},{64,32},{96,64},{128,96},{160,128},{192,160},{224,1... | collective-permute-start | bytes 884744 | tf_op jit(solution)/shard_map/ppermute | solution.py:241
  94.8 9.9 %copy-start.12 = (bf16[3,64,768]{2,1,0:T(8,128)(2,1)}, bf16[3,64,768]{2,1,0:T(8,128)(2,1)S(1)}, u32[]{:S(2)}) copy-start(bf16[3,64,768]{2,1,0:T(8,128)(2,1)S(1)} %collective-permute-done.13.refs_9_) | copy-start | bytes 884740
  94.9 9.8 %collective-permute-start.14 = (bf16[3,64,768]{2,1,0:T(8,128)(2,1)S(1)}, bf16[3,64,768]{2,1,0:T(8,128)(2,1)}, u32[]{:S(2)}, u32[]{:S(2)}) collective-permute-start(bf16[3,64,768]{2,1,0:T(8,128)(2,1)S(1)} %collective-permute-done.13.refs_9_), channel_id=1, source_target_pairs={{0,32},{32,64},{64,96},{96,128},{128,160},{160,192},{192,224},{224... | collective-permute-start | bytes 884744 | tf_op jit(solution)/shard_map/ppermute | solution.py:241
  100.0 4.7 %copy-start.2 = (bf16[32,16,1024]{2,1,0:T(8,128)(2,1)}, bf16[32,16,1024]{2,1,0:T(8,128)(2,1)S(1)}, u32[]{:S(2)}) copy-start(bf16[32,16,1024]{2,1,0:T(8,128)(2,1)S(1)} %all-to-all-done) | copy-start | bytes 3145732
  127.4 7.1 %copy-start.17 = (bf16[4,64,768]{2,1,0:T(8,128)(2,1)S(1)}, bf16[4,64,768]{2,1,0:T(8,128)(2,1)}, u32[]{:S(2)}) copy-start(bf16[4,64,768]{2,1,0:T(8,128)(2,1)} %get-tuple-element.20) | copy-start | bytes 1179652
  127.4 22.3 %copy-start.13 = (f32[4,64,768]{2,1,0:T(8,128)S(1)}, f32[4,64,768]{2,1,0:T(8,128)}, u32[]{:S(2)}) copy-start(f32[4,64,768]{2,1,0:T(8,128)} %get-tuple-element.21) | copy-start | bytes 2359300
  127.5 72.9 %all-to-all-start.2 = ((bf16[32,16,2048]{2,1,0:T(8,128)(2,1)}), bf16[32,16,2048]{2,1,0:T(8,128)(2,1)S(1)}, u32[]{:S(2)}, u32[]{:S(2)}) async-start(bf16[32,16,2048]{2,1,0:T(8,128)(2,1)} %bitcast.48), calls=%async_computation.2 | async-start | bytes 4194304 | tf_op jit(solution)/shard_map/all_to_all | solution.py:315
  134.5 15.2 %collective-permute-start.15 = (bf16[4,64,768]{2,1,0:T(8,128)(2,1)S(1)}, bf16[4,64,768]{2,1,0:T(8,128)(2,1)S(1)}, u32[]{:S(2)}, u32[]{:S(2)}) collective-permute-start(bf16[4,64,768]{2,1,0:T(8,128)(2,1)S(1)} %copy-done.17), channel_id=1, source_target_pairs={{0,480},{32,0},{64,32},{96,64},{128,96},{160,128},{192,160},{224,1... | collective-permute-start | bytes 1179656 | tf_op jit(solution)/shard_map/ppermute | solution.py:255
  137.8 14.4 %collective-permute-start.17 = (bf16[4,64,768]{2,1,0:T(8,128)(2,1)}, bf16[4,64,768]{2,1,0:T(8,128)(2,1)}, u32[]{:S(2)}, u32[]{:S(2)}) collective-permute-start(bf16[4,64,768]{2,1,0:T(8,128)(2,1)} %get-tuple-element.22), channel_id=1, source_target_pairs={{0,32},{32,64},{64,96},{96,128},{128,160},{160,192},{192,224},{224... | collective-permute-start | bytes 1179656 | tf_op jit(solution)/shard_map/ppermute | solution.py:255
  149.9 36.5 %copy-start.16 = (s32[128,2]{0,1:T(2,128)S(1)}, s32[128,2]{0,1:T(2,128)}, u32[]{:S(2)}) copy-start(s32[128,2]{0,1:T(2,128)} %param.13) | copy-start | bytes 3076
  149.9 13.8 %collective-permute-start.16 = (bf16[4,64,768]{2,1,0:T(8,128)(2,1)S(1)}, bf16[4,64,768]{2,1,0:T(8,128)(2,1)S(1)}, u32[]{:S(2)}, u32[]{:S(2)}) collective-permute-start(bf16[4,64,768]{2,1,0:T(8,128)(2,1)S(1)} %add_convert_fusion), channel_id=1, source_target_pairs={{0,480},{32,0},{64,32},{96,64},{128,96},{160,128},{192,160},{224,1... | collective-permute-start | bytes 1179656 | tf_op jit(solution)/shard_map/ppermute | solution.py:255
  165.7 21.6 %collective-permute-start.18 = (bf16[64,768]{1,0:T(8,128)(2,1)}, bf16[64,768]{1,0:T(8,128)(2,1)S(1)}, u32[]{:S(2)}, u32[]{:S(2)}) collective-permute-start(bf16[64,768]{1,0:T(8,128)(2,1)} %get-tuple-element.38), channel_id=1, source_target_pairs={{0,128},{32,160},{64,192},{96,224},{128,256},{160,288},{192,320},{... | collective-permute-start | bytes 294920 | tf_op jit(solution)/shard_map/ppermute | solution.py:255
  174.8 24.8 %collective-permute-start.19 = (bf16[64,768]{1,0:T(8,128)(2,1)S(1)}, bf16[64,768]{1,0:T(8,128)(2,1)S(1)}, u32[]{:S(2)}, u32[]{:S(2)}) collective-permute-start(bf16[64,768]{1,0:T(8,128)(2,1)S(1)} %get-tuple-element.40), channel_id=1, source_target_pairs={{0,256},{32,288},{64,320},{96,352},{128,384},{160,416},{192,448},{... | collective-permute-start | bytes 294920 | tf_op jit(solution)/shard_map/ppermute | solution.py:255
  179.9 19.7 %collective-permute-start.20 = (bf16[64,768]{1,0:T(8,128)(2,1)S(1)}, bf16[64,768]{1,0:T(8,128)(2,1)S(1)}, u32[]{:S(2)}, u32[]{:S(2)}) collective-permute-start(bf16[64,768]{1,0:T(8,128)(2,1)S(1)} %get-tuple-element.39), channel_id=1, source_target_pairs={{0,384},{32,416},{64,448},{96,480},{128,0},{160,32},{192,64},{224,... | collective-permute-start | bytes 294920 | tf_op jit(solution)/shard_map/ppermute | solution.py:255
  200.3 1.4 copy-start.1

commit v4 on v2

--- a/solution.py
+++ b/solution.py
@@ -27,7 +27,7 @@
     hidden[...] = here
     activated[...] = active
     slope[...] = pre_up * squashed * (1.0 + pre_gate * (1.0 - squashed))
-    partial = _dot(cot[...], here, (0, 0))
+    partial = _dot(cot[...], here, (1, 0))
     members, block = classes.shape[1], classes.shape[2]
     for index in range(members * STRIDE):
         classes[index % STRIDE, index // STRIDE] = partial[index * block : (index + 1) * block]
@@ -51,7 +51,7 @@
             grid=(steps,),
             in_specs=[
                 whole,
-                whole,
+                pl.BlockSpec((features, slots), lambda j, place: (0, 0)),
                 pl.BlockSpec((features, BLOCK), lambda j, place: (0, j)),
                 pl.BlockSpec((features, BLOCK), lambda j, place: (0, j + steps)),
             ],
@@ -121,6 +121,36 @@
         ],
         name="rows_back",
     )(hidden, cot, slope, activated, mats, mats, mats)
+
+
+def _finish_kernel(slot, gates, second_out, first_grad, second_grad, back, second_in, first_total, gate_grad):
+    count, features = second_out.shape
+    grad = second_grad[...].astype(jnp.float32)
+    combined, cot_sum = 0.0, 0.0
+    for k in range(slot.shape[1]):
+        numbers = lax.broadcasted_iota(jnp.int32, (count, back.shape[0]), 1)
+        chosen = (slot[:, k : k + 1] == numbers).astype(jnp.bfloat16)
+        out_row = _dot(chosen, back[:, :features], (1, 0))
+        combined += gates[:, k : k + 1] * out_row
+        gate_grad[:, k : k + 1] = jnp.sum(grad * out_row, axis=1, keepdims=True)
+        cot_sum += _dot(chosen, back[:, features:], (1, 0))
+    second_in[...] = (second_out[...].astype(jnp.float32) - combined).astype(jnp.bfloat16)
+    first_total[...] = (first_grad[...].astype(jnp.float32) + cot_sum).astype(jnp.bfloat16)
+
+
+def finish(slot, gates, second_out, first_grad, second_grad, back):
+    held = pl.BlockSpec(memory_space=pltpu.VMEM)
+    return pl.pallas_call(
+        _finish_kernel,
+        in_specs=[held] * 6,
+        out_specs=[held] * 3,
+        out_shape=[
+            jax.ShapeDtypeStruct(second_out.shape, jnp.bfloat16),
+            jax.ShapeDtypeStruct(first_grad.shape, jnp.bfloat16),
+            jax.ShapeDtypeStruct(gates.shape, jnp.float32),
+        ],
+        name="finish",
+    )(slot, gates, second_out, first_grad, second_grad, back)
 
 
 def to_slots(placing, assigned_rows):
@@ -192,7 +222,7 @@
     shards = jnp.concatenate([w_gate[0], w_up[0], w_down[0]], axis=1)
     mats = lax.all_gather(shards, "dp", axis=0, tiled=True)
     place = lax.axis_index("dp").astype(jnp.int32).reshape(1)
-    hidden, slope, activated, *parts = hidden_and_partial(place, rows_in, rows_cot, mats, groups)
+    hidden, slope, activated, *parts = hidden_and_partial(place, rows_in, rows_cot.T, mats, groups)
     back_rows = rows_back(hidden, rows_cot, slope, activated, mats)
     back = lax.all_to_all(
         back_rows.reshape(owners, capacity, 2 * feature_count),
@@ -203,16 +233,14 @@
     ).reshape(slots_all, 2 * feature_count)
     grad_scale = 1.0 / math.sqrt(count_here * groups)
     w_down_grad = (window_reduce(*parts, groups) * grad_scale)[None]
-    out_assigned = jnp.dot(placing, back[:, :feature_count], preferred_element_type=jnp.float32)
-    cot_assigned = jnp.dot(placing, back[:, feature_count:], preferred_element_type=jnp.float32)
-    expert_out = out_assigned.reshape(count_here, top_count, feature_count)
-    combined = jnp.sum(gate_values[:, :, None] * expert_out, axis=1)
-    second_in = (second_out.astype(jnp.float32) - combined).astype(jnp.bfloat16)
-    gate_grad = jnp.sum(second_grad.astype(jnp.float32)[:, None, :] * expert_out, axis=2)
-    first_total = (
-        first_grad.astype(jnp.float32)
-        + jnp.sum(cot_assigned.reshape(count_here, top_count, feature_count), axis=1)
-    ).astype(jnp.bfloat16)
+    second_in, first_total, gate_grad = finish(
+        slot_index.reshape(count_here, top_count),
+        gate_values,
+        second_out,
+        first_grad,
+        second_grad,
+        back,
+    )
     return (second_in, first_total, gate_grad, w_down_grad)
 
 

time: 199 us -> 191 us (0.960)
  other arithmetic: 12 us -> 5.26 us
  waiting for transfers between devices: 90.4 us -> 86.5 us
  Pallas kernels: 15.9 us -> 19.4 us
  matrix products: 6.12 us -> 3.09 us
    pallas_call x0 -> x1, Pallas kernels: none -> 3.53 us  [finish(): pl.pallas_call(_finish_kernel, in_specs=[held] * 6, out_specs=[held] * 3,...]
    dot_general x2 -> x0, matrix products: 2.98 us -> none  [the longest x1 1.52 us: per_device(): jnp.dot(placing, back[:, :feature_count], preferred_element_type=jnp.floa...]
    unnamed x17 -> x19, local copies, waits for them, and re-layouts: 1.57 us -> 4.42 us
    reshape x3 -> x0, local copies, waits for them, and re-layouts: 2.69 us -> none  [the longest x1 1.93 us: per_device(): expert_out = out_assigned.reshape(count_here, top_count, feature_count)]
    reduce_sum x2 -> x0, other arithmetic: 2.59 us -> none  [the longest x1 1.35 us: per_device(): combined = jnp.sum(gate_values[:, :, None] * expert_out, axis=1)]
where the time goes in v4:
time: 191 us; the launch traced here: 190 us
  waiting for transfers between devices  86.5 us (45%)
  starting transfers between devices  51.3 us (27%)
  Pallas kernels  19.4 us (10%)
  between operations  14.3 us (7%)
  local copies, waits for them, and re-layouts  9.72 us (5%)
  other arithmetic  5.26 us (3%)
  matrix products  3.09 us (2%)
    ppermute x6, waiting for transfers between devices, moved(): lax.ppermute(value, 'dp', [(i, (i + by) % groups) for i in range(groups)])  33.2 us
    ppermute x6, starting transfers between devices, moved(): lax.ppermute(value, 'dp', [(i, (i + by) % groups) for i in range(groups)])  23.6 us
    all_gather x1, waiting for transfers between devices, per_device(): mats = lax.all_gather(shards, 'dp', axis=0, tiled=True)  22.9 us
    all_to_all x1, starting transfers between devices, per_device(): lax.all_to_all(back_rows.reshape(owners, capacity, 2 * feature_count), 'e...  16.1 us
    all_to_all x1, waiting for transfers between devices, per_device(): lax.all_to_all(send_input, 'expert', split_axis=0, concat_axis=0, tiled=T...  15.5 us
    all_to_all x1, waiting for transfers between devices, per_device(): lax.all_to_all(send_cot, 'expert', split_axis=0, concat_axis=0, tiled=True)  14.9 us
    pallas_call x1, Pallas kernels, rows_back(): pl.pallas_call(_back_kernel, grid=(steps,), in_specs=[column, pl.BlockSpe...  9.06 us
    all_to_all x1, starting transfers between devices, per_device(): lax.all_to_all(send_cot, 'expert', split_axis=0, concat_axis=0, tiled=True)  7.76 us
  transfers between devices with their start and end apart: 10, of which 7 were waited for; matrix products, arithmetic and copies ran while one was open for 7% of the time, Pallas kernels for 0%

profile of v4, /device:TPU:65, one launch (start us, length us, event | category | flops | bytes accessed | tf_op | source)
XLA Modules:
  0.0 189.7 jit_solution(8799243350197296363)
XLA Ops:
  7.2 0.0 all-gather.2.cloned.1.call-start
  7.2 1.7 pad_maximum_fusion
  9.0 0.0 all-gather.2.cloned.1.call-update
  9.0 0.8 copy.27
  9.8 0.1 eq.47
  9.9 0.1 eq.43
  10.1 0.6 reduce-window.6
  10.7 0.2 slice_reduce_fusion
  10.9 0.8 copy.33.gates
  11.7 0.1 mul.39
  11.8 1.2 broadcast_in_dim.7
  13.1 0.7 convert_element_type.52
  13.8 0.1 fusion.9
  13.9 0.0 copy-start.5
  13.9 1.6 convolution_convert_fusion
  15.5 7.8 %all-to-all-start.1 = ((bf16[32,16,1024]{2,1,0:T(8,128)(2,1)}), bf16[32,16,1024]{2,1,0:T(8,128)(2,1)S(1)}, u32[]{:S(2)}, u32[]{:S(2)}) async-start(bf16[32,16,1024]{2,1,0:T(8,128)(2,1)} %bitcast.4), calls=%async_computation.1 | async-start | bytes 2097152 | tf_op jit(solution)/shard_map/all_to_all | solution.py:218
  23.2 0.3 broadcast_in_dim.6
  23.5 0.2 reshape.67
  23.7 1.5 convolution_convert_fusion.1
  25.3 14.9 %all-to-all-done.1 = bf16[32,16,1024]{2,1,0:T(8,128)(2,1)S(1)} async-done(((bf16[32,16,1024]{2,1,0:T(8,128)(2,1)}), bf16[32,16,1024]{2,1,0:T(8,128)(2,1)S(1)}, u32[]{:S(2)}, u32[]{:S(2)}) %all-to-all-start.1) | async-done | bytes 1048608 | tf_op jit(solution)/shard_map/all_to_all | solution.py:218
  40.1 3.9 %all-to-all-start = ((bf16[32,16,1024]{2,1,0:T(8,128)(2,1)}), bf16[32,16,1024]{2,1,0:T(8,128)(2,1)S(1)}, u32[]{:S(2)}, u32[]{:S(2)}) async-start(bf16[32,16,1024]{2,1,0:T(8,128)(2,1)} %bitcast.2), calls=%async_computation | async-start | bytes 2097152 | tf_op jit(solution)/shard_map/all_to_all | solution.py:217
  44.1 1.4 copy.32.cot
  45.4 15.5 %all-to-all-done = bf16[32,16,1024]{2,1,0:T(8,128)(2,1)S(1)} async-done(((bf16[32,16,1024]{2,1,0:T(8,128)(2,1)}), bf16[32,16,1024]{2,1,0:T(8,128)(2,1)S(1)}, u32[]{:S(2)}, u32[]{:S(2)}) %all-to-all-start) | async-done | bytes 1048608 | tf_op jit(solution)/shard_map/all_to_all | solution.py:217
  61.0 22.9 %all-gather.2.cloned.1.call-done.gate.up.down_mat = bf16[1024,2304]{1,0:T(8,128)(2,1)} async-done(((bf16[64,2304]{1,0:T(8,128)(2,1)}), bf16[1024,2304]{1,0:T(8,128)(2,1)}) %all-gather.2.cloned.1.call-update) | async-done | bytes 4718608 | tf_op jit(solution)/shard_map/all_gather | solution.py:223
  83.9 6.8 %hidden_and_partial.1 = (bf16[512,768]{1,0:T(8,128)(2,1)}, f32[512,768]{1,0:T(8,128)}, f32[512,768]{1,0:T(8,128)}, bf16[4,64,768]{2,1,0:T(8,128)(2,1)}, bf16[4,6...) custom-call(s32[1]{0:T(128)} %bitcast.1.place, bf16[512,1024]{1,0:T(8,128)(2,1)} %bitcast.54, ...), custom_call_target="tpu_custom_call" | custom-call | tf_op jit(solution)/shard_map/hidden_and_partial/pallas_call | solution.py:47
  90.7 9.1 %rows_back.1 = bf16[512,2048]{1,0:T(8,128)(2,1)} custom-call(bf16[512,768]{1,0:T(8,128)(2,1)} %get-tuple-element.14.hidden, bf16[512,1024]{1,0:T(8,128)(2,1)} %bitcast.51, f32[512,768]{1,0:T(8,128)} %get-tuple-element.15.slope, f32[512,768]{1,0:T(8,128)} %get-tuple-element.16.activated, bf16[1024,2304]{1,0:T(8,128)(2,1)} %all-gather.2.cloned.1.call-done.gate.up.down_mat, ...), custom_call_target="tpu_custom_call" | custom-call | tf_op jit(solution)/shard_map/rows_back/pallas_call | solution.py:104
  99.8 16.1 %all-to-all-start.2 = ((bf16[32,16,2048]{2,1,0:T(8,128)(2,1)}), bf16[32,16,2048]{2,1,0:T(8,128)(2,1)S(1)}, u32[]{:S(2)}, u32[]{:S(2)}) async-start(bf16[32,16,2048]{2,1,0:T(8,128)(2,1)} %bitcast.53), calls=%async_computation.2 | async-start | bytes 4194304 | tf_op jit(solution)/shard_map/all_to_all | solution.py:227
  115.9 1.9 %collective-permute-start = (bf16[4,64,768]{2,1,0:T(8,128)(2,1)S(1)}, bf16[4,64,768]{2,1,0:T(8,128)(2,1)S(1)}, u32[]{:S(2)}, u32[]{:S(2)}) collective-permute-start(bf16[4,64,768]{2,1,0:T(8,128)(2,1)S(1)} %copy-done.7), channel_id=1, source_target_pairs={{0,480},{32,0},{64,32},{96,64},{128,96},{160,128},{192,160},{224,1... | collective-permute-start | bytes 1179656 | tf_op jit(solution)/shard_map/ppermute | solution.py:167
  117.8 3.4 %collective-permute-start.2 = (bf16[4,64,768]{2,1,0:T(8,128)(2,1)}, bf16[4,64,768]{2,1,0:T(8,128)(2,1)}, u32[]{:S(2)}, u32[]{:S(2)}) collective-permute-start(bf16[4,64,768]{2,1,0:T(8,128)(2,1)} %get-tuple-element.22), channel_id=1, source_target_pairs={{0,32},{32,64},{64,96},{96,128},{128,160},{160,192},{192,224},{224... | collective-permute-start | bytes 1179656 | tf_op jit(solution)/shard_map/ppermute | solution.py:167
  121.2 7.1 %collective-permute-done = bf16[4,64,768]{2,1,0:T(8,128)(2,1)S(1)} collective-permute-done((bf16[4,64,768]{2,1,0:T(8,128)(2,1)S(1)}, bf16[4,64,768]{2,1,0:T(8,128)(2,1)S(1)}, u32[]{:S(2)}, u32[]{:S(2)}) %collective-permute-start) | collective-permute-done | bytes 393248 | tf_op jit(solution)/shard_map/ppermute | solution.py:167
  128.3 0.1 add_convert_fusion
  128.4 0.0 copy-start.6
  128.4 2.1 %collective-permute-start.1 = (bf16[4,64,768]{2,1,0:T(8,128)(2,1)S(1)}, bf16[4,64,768]{2,1,0:T(8,128)(2,1)S(1)}, u32[]{:S(2)}, u32[]{:S(2)}) collective-permute-start(bf16[4,64,768]{2,1,0:T(8,128)(2,1)S(1)} %add_convert_fusion), channel_id=1, source_target_pairs={{0,480},{32,0},{64,32},{96,64},{128,96},{160,128},{192,160},{224,1... | collective-permute-start | bytes 1179656 | tf_op jit(solution)/shard_map/ppermute | solution.py:167
  130.6 9.7 %collective-permute-done.1 = bf16[4,64,768]{2,1,0:T(8,128)(2,1)S(1)} collective-permute-done((bf16[4,64,768]{2,1,0:T(8,128)(2,1)S(1)}, bf16[4,64,768]{2,1,0:T(8,128)(2,1)S(1)}, u32[]{:S(2)}, u32[]{:S(2)}) %collective-permute-start.1) | collective-permute-done | bytes 393248 | tf_op jit(solution)/shard_map/ppermute | solution.py:167
  140.3 1.4 fusion.11
  141.6 0.7 dynamic-slice_bitcast_fusion.2
  142.3 4.6 %collective-permute-start.3 = (bf16[64,768]{1,0:T(8,128)(2,1)}, bf16[64,768]{1,0:T(8,128)(2,1)S(1)}, u32[]{:S(2)}, u32[]{:S(2)}) collective-permute-start(bf16[64,768]{1,0:T(8,128)(2,1)} %get-tuple-element.38), channel_id=1, source_target_pairs={{0,128},{32,160},{64,192},{96,224},{128,256},{160,288},{192,320},{... | collective-permute-start | bytes 294920 | tf_op jit(solution)/shard_map/ppermute | solution.py:167
  147.0 6.9 %collective-permute-start.4 = (bf16[64,768]{1,0:T(8,128)(2,1)S(1)}, bf16[64,768]{1,0:T(8,128)(2,1)S(1)}, u32[]{:S(2)}, u32[]{:S(2)}) collective-permute-start(bf16[64,768]{1,0:T(8,128)(2,1)S(1)} %get-tuple-element.40), channel_id=1, source_target_pairs={{0,256},{32,288},{64,320},{96,352},{128,384},{160,416},{192,448},{... | collective-permute-start | bytes 294920 | tf_op jit(solution)/shard_map/ppermute | solution.py:167
  153.9 4.6 %collective-permute-start.5 = (bf16[64,768]{1,0:T(8,128)(2,1)S(1)}, bf16[64,768]{1,0:T(8,128)(2,1)S(1)}, u32[]{:S(2)}, u32[]{:S(2)}) collective-permute-start(bf16[64,768]{1,0:T(8,128)(2,1)S(1)} %get-tuple-element.39), channel_id=1, source_target_pairs={{0,384},{32,416},{64,448},{96,480},{128,0},{160,32},{192,64},{224,... | collective-permute-start | bytes 294920 | tf_op jit(solution)/shard_map/ppermute | solution.py:167
  158.6 0.1 reduce_sum.12
  158.7 0.1 copy.30
  158.8 0.6 add.65.slot
  159.5 1.9 %collective-permute-done.4 = bf16[64,768]{1,0:T(8,128)(2,1)S(1)} collective-permute-done((bf16[64,768]{1,0:T(8,128)(2,1)S(1)}, bf16[64,768]{1,0:T(8,128)(2,1)S(1)}, u32[]{:S(2)}, u32[]{:S(2)}) %collective-permute-start.4) | collective-permute-done | bytes 98336 | tf_op jit(solution)/shard_map/ppermute | solution.py:167
  161.4 14.4 %collective-permute-done.5 = bf16[64,768]{1,0:T(8,128)(2,1)S(1)} collective-permute-done((bf16[64,768]{1,0:T(8,128)(2,1)S(1)}, bf16[64,768]{1,0:T(8,128)(2,1)S(1)}, u32[]{:S(2)}, u32[]{:S(2)}) %collective-permute-start.5) | collective-permute-done | bytes 98336 | tf_op jit(solution)/shard_map/ppermute | solution.py:167
  175.8 0.7 fusion.6
  176.5 1.3 copy-done.1
  177.9 3.5 %finish.1 = (bf16[128,1024]{1,0:T(8,128)(2,1)}, bf16[128,1024]{1,0:T(8,128)(2,1)}, f32[128,2]{1,0:T(8,128)}) custom-call(s32[128,2]{1,0:T(8,128)} %add.65.slot, f32[128,2]{1,0:T(8,128)} %copy-done.4, bf16[128,1024]{1,0:T(8,128)(2,1)} %second_out.1, bf16[128,1024]{1,0:T(8,128)(2,1)} %first_grad.1, bf16[128,1024]{1,0:T(8,128)(2,1)} %second_grad.1, ...), custom_call_target="tpu_custom_call" | custom-call | tf_op jit(solution)/shard_map/finish/pallas_call | solution.py:143
  181.4 1.5 copy.34
  (21 shorter events, 0.1 us)
Async XLA Ops:
  7.2 76.7 %all-gather.2.cloned.1.call-start = ((), (), s32[]{:S(2)}) async-start(), calls=%async_computation.3 | async-start | bytes 5013504 | tf_op jit(solution)/shard_map/all_gather | solution.py:223
  11.7 3.8 %copy-start.4 = (f32[128,2]{1,0:T(8,128)}, f32[128,2]{1,0:T(8,128)S(1)}, u32[]{:S(2)}) copy-start(f32[128,2]{1,0:T(8,128)S(1)} %copy.33.gates) | copy-start | bytes 3076
  13.9 9.3 %copy-start.5 = (bf16[128,1024]{1,0:T(8,128)(2,1)S(1)}, bf16[128,1024]{1,0:T(8,128)(2,1)}, u32[]{:S(2)}) copy-start(bf16[128,1024]{1,0:T(8,128)(2,1)} %param.9) | copy-start | bytes 786436
  15.5 24.7 %all-to-all-start.1 = ((bf16[32,16,1024]{2,1,0:T(8,128)(2,1)}), bf16[32,16,1024]{2,1,0:T(8,128)(2,1)S(1)}, u32[]{:S(2)}, u32[]{:S(2)}) async-start(bf16[32,16,1024]{2,1,0:T(8,128)(2,1)} %bitcast.4), calls=%async_computation.1 | async-start | bytes 2097152 | tf_op jit(solution)/shard_map/all_to_all | solution.py:218
  40.1 5.3 %copy-start = (bf16[32,16,1024]{2,1,0:T(8,128)(2,1)}, bf16[32,16,1024]{2,1,0:T(8,128)(2,1)S(1)}, u32[]{:S(2)}) copy-start(bf16[32,16,1024]{2,1,0:T(8,128)(2,1)S(1)} %all-to-all-done.1) | copy-start | bytes 3145732
  40.1 20.8 %all-to-all-start = ((bf16[32,16,1024]{2,1,0:T(8,128)(2,1)}), bf16[32,16,1024]{2,1,0:T(8,128)(2,1)S(1)}, u32[]{:S(2)}, u32[]{:S(2)}) async-start(bf16[32,16,1024]{2,1,0:T(8,128)(2,1)} %bitcast.2), calls=%async_computation | async-start | bytes 2097152 | tf_op jit(solution)/shard_map/all_to_all | solution.py:217
  61.0 22.9 %copy-start.2 = (bf16[32,16,1024]{2,1,0:T(8,128)(2,1)}, bf16[32,16,1024]{2,1,0:T(8,128)(2,1)S(1)}, u32[]{:S(2)}) copy-start(bf16[32,16,1024]{2,1,0:T(8,128)(2,1)S(1)} %all-to-all-done) | copy-start | bytes 3145732
  99.8 16.1 %copy-start.7 = (bf16[4,64,768]{2,1,0:T(8,128)(2,1)S(1)}, bf16[4,64,768]{2,1,0:T(8,128)(2,1)}, u32[]{:S(2)}) copy-start(bf16[4,64,768]{2,1,0:T(8,128)(2,1)} %get-tuple-element.20) | copy-start | bytes 1179652
  99.8 28.5 %copy-start.3 = (f32[4,64,768]{2,1,0:T(8,128)S(1)}, f32[4,64,768]{2,1,0:T(8,128)}, u32[]{:S(2)}) copy-start(f32[4,64,768]{2,1,0:T(8,128)} %get-tuple-element.21) | copy-start | bytes 2359300
  99.8 76.7 %all-to-all-start.2 = ((bf16[32,16,2048]{2,1,0:T(8,128)(2,1)}), bf16[32,16,2048]{2,1,0:T(8,128)(2,1)S(1)}, u32[]{:S(2)}, u32[]{:S(2)}) async-start(bf16[32,16,2048]{2,1,0:T(8,128)(2,1)} %bitcast.53), calls=%async_computation.2 | async-start | bytes 4194304 | tf_op jit(solution)/shard_map/all_to_all | solution.py:227
  115.9 12.4 %collective-permute-start = (bf16[4,64,768]{2,1,0:T(8,128)(2,1)S(1)}, bf16[4,64,768]{2,1,0:T(8,128)(2,1)S(1)}, u32[]{:S(2)}, u32[]{:S(2)}) collective-permute-start(bf16[4,64,768]{2,1,0:T(8,128)(2,1)S(1)} %copy-done.7), channel_id=1, source_target_pairs={{0,480},{32,0},{64,32},{96,64},{128,96},{160,128},{192,160},{224,1... | collective-permute-start | bytes 1179656 | tf_op jit(solution)/shard_map/ppermute | solution.py:167
  117.8 12.8 %collective-permute-start.2 = (bf16[4,64,768]{2,1,0:T(8,128)(2,1)}, bf16[4,64,768]{2,1,0:T(8,128)(2,1)}, u32[]{:S(2)}, u32[]{:S(2)}) collective-permute-start(bf16[4,64,768]{2,1,0:T(8,128)(2,1)} %get-tuple-element.22), channel_id=1, source_target_pairs={{0,32},{32,64},{64,96},{96,128},{128,160},{160,192},{192,224},{224... | collective-permute-start | bytes 1179656 | tf_op jit(solution)/shard_map/ppermute | solution.py:167
  128.4 30.1 %copy-start.6 = (s32[128,2]{0,1:T(2,128)S(1)}, s32[128,2]{0,1:T(2,128)}, u32[]{:S(2)}) copy-start(s32[128,2]{0,1:T(2,128)} %param.13) | copy-start | bytes 3076
  128.4 11.9 %collective-permute-start.1 = (bf16[4,64,768]{2,1,0:T(8,128)(2,1)S(1)}, bf16[4,64,768]{2,1,0:T(8,128)(2,1)S(1)}, u32[]{:S(2)}, u32[]{:S(2)}) collective-permute-start(bf16[4,64,768]{2,1,0:T(8,128)(2,1)S(1)} %add_convert_fusion), channel_id=1, source_target_pairs={{0,480},{32,0},{64,32},{96,64},{128,96},{160,128},{192,160},{224,1... | collective-permute-start | bytes 1179656 | tf_op jit(solution)/shard_map/ppermute | solution.py:167
  142.3 17.1 %collective-permute-start.3 = (bf16[64,768]{1,0:T(8,128)(2,1)}, bf16[64,768]{1,0:T(8,128)(2,1)S(1)}, u32[]{:S(2)}, u32[]{:S(2)}) collective-permute-start(bf16[64,768]{1,0:T(8,128)(2,1)} %get-tuple-element.38), channel_id=1, source_target_pairs={{0,128},{32,160},{64,192},{96,224},{128,256},{160,288},{192,320},{... | collective-permute-start | bytes 294920 | tf_op jit(solution)/shard_map/ppermute | solution.py:167
  147.0 14.4 %collective-permute-start.4 = (bf16[64,768]{1,0:T(8,128)(2,1)S(1)}, bf16[64,768]{1,0:T(8,128)(2,1)S(1)}, u32[]{:S(2)}, u32[]{:S(2)}) collective-permute-start(bf16[64,768]{1,0:T(8,128)(2,1)S(1)} %get-tuple-element.40), channel_id=1, source_target_pairs={{0,256},{32,288},{64,320},{96,352},{128,384},{160,416},{192,448},{... | collective-permute-start | bytes 294920 | tf_op jit(solution)/shard_map/ppermute | solution.py:167
  153.9 21.9 %collective-permute-start.5 = (bf16[64,768]{1,0:T(8,128)(2,1)S(1)}, bf16[64,768]{1,0:T(8,128)(2,1)S(1)}, u32[]{:S(2)}, u32[]{:S(2)}) collective-permute-start(bf16[64,768]{1,0:T(8,128)(2,1)S(1)} %get-tuple-element.39), channel_id=1, source_target_pairs={{0,384},{32,416},{64,448},{96,480},{128,0},{160,32},{192,64},{224,... | collective-permute-start | bytes 294920 | tf_op jit(solution)/shard_map/ppermute | solution.py:167
  176.5 1.3 copy-start.1
Sparse Core Ops, SparseCore 0:
  10.1 73.8 all-gather.1

commit v5 on v4

--- a/solution.py
+++ b/solution.py
@@ -31,8 +31,12 @@
     members, block = classes.shape[1], classes.shape[2]
     for index in range(members * STRIDE):
         classes[index % STRIDE, index // STRIDE] = partial[index * block : (index + 1) * block]
-    for shift, target in ((2, send_two), (1, send_one), (3, own_three), (0, own_zero)):
-        target[...] = classes[(place[0] + shift) % STRIDE].astype(target.dtype)
+    groups = members * STRIDE
+    for ahead, target in ((-2, send_two), (1, send_one), (-1, own_three), (0, own_zero)):
+        owner = (place[0] + ahead + groups) % groups
+        for m in range(members):
+            block_at = (owner // STRIDE + m) % members
+            target[m] = classes[owner % STRIDE, block_at].astype(target.dtype)
 
 
 def hidden_and_partial(place, rows, cot, mats, groups):
@@ -40,7 +44,7 @@
     width = mats.shape[1] // 3
     steps = width // BLOCK
     members, block = groups // STRIDE, features // groups
-    whole = pl.BlockSpec((slots, features), lambda j, place: (0, 0))
+    held = pl.BlockSpec(memory_space=pltpu.VMEM)
     column = pl.BlockSpec((slots, BLOCK), lambda j, place: (0, j))
     part = pl.BlockSpec((members, block, BLOCK), lambda j, place: (0, 0, j))
     part_shape = (members, block, width)
@@ -50,8 +54,8 @@
             num_scalar_prefetch=1,
             grid=(steps,),
             in_specs=[
-                whole,
-                pl.BlockSpec((features, slots), lambda j, place: (0, 0)),
+                held,
+                held,
                 pl.BlockSpec((features, BLOCK), lambda j, place: (0, j)),
                 pl.BlockSpec((features, BLOCK), lambda j, place: (0, j + steps)),
             ],
@@ -106,7 +110,7 @@
         grid=(steps,),
         in_specs=[
             column,
-            pl.BlockSpec((slots, features), lambda j: (0, 0)),
+            pl.BlockSpec(memory_space=pltpu.VMEM),
             column,
             column,
             pl.BlockSpec((features, BLOCK), lambda j: (0, j)),
@@ -121,6 +125,20 @@
         ],
         name="rows_back",
     )(hidden, cot, slope, activated, mats, mats, mats)
+
+
+def _beside_kernel(gate, up, down, out):
+    width = gate.shape[2]
+    for at, value in enumerate((gate, up, down)):
+        out[:, at * width : (at + 1) * width] = value[0]
+
+
+def side_by_side(gate, up, down):
+    return pl.pallas_call(
+        _beside_kernel,
+        out_shape=jax.ShapeDtypeStruct((gate.shape[1], 3 * gate.shape[2]), gate.dtype),
+        name="side_by_side",
+    )(gate, up, down)
 
 
 def _finish_kernel(slot, gates, second_out, first_grad, second_grad, back, second_in, first_total, gate_grad):
@@ -132,7 +150,7 @@
         chosen = (slot[:, k : k + 1] == numbers).astype(jnp.bfloat16)
         out_row = _dot(chosen, back[:, :features], (1, 0))
         combined += gates[:, k : k + 1] * out_row
-        gate_grad[:, k : k + 1] = jnp.sum(grad * out_row, axis=1, keepdims=True)
+        gate_grad[k : k + 1, :] = jnp.sum(grad * out_row, axis=1)[None, :]
         cot_sum += _dot(chosen, back[:, features:], (1, 0))
     second_in[...] = (second_out[...].astype(jnp.float32) - combined).astype(jnp.bfloat16)
     first_total[...] = (first_grad[...].astype(jnp.float32) + cot_sum).astype(jnp.bfloat16)
@@ -147,7 +165,7 @@
         out_shape=[
             jax.ShapeDtypeStruct(second_out.shape, jnp.bfloat16),
             jax.ShapeDtypeStruct(first_grad.shape, jnp.bfloat16),
-            jax.ShapeDtypeStruct(gates.shape, jnp.float32),
+            jax.ShapeDtypeStruct(gates.shape[::-1], jnp.float32),
         ],
         name="finish",
     )(slot, gates, second_out, first_grad, second_grad, back)
@@ -161,7 +179,6 @@
 
 def window_reduce(send_two, send_one, own_three, own_zero, groups):
     members = groups // STRIDE
-    place = lax.axis_index("dp")
 
     def moved(value, by):
         return lax.ppermute(value, "dp", [(i, (i + by) % groups) for i in range(groups)])
@@ -170,16 +187,14 @@
     from_below = moved(send_one, 1)
     passed_on = (from_second.astype(jnp.float32) + own_three).astype(jnp.bfloat16)
     from_above = moved(passed_on, -1)
-    window = from_above.astype(jnp.float32) + (from_below.astype(jnp.float32) + own_zero)
-    rounded = window.astype(jnp.bfloat16)
-    member = place // STRIDE
-
-    def block_of(values, ahead):
-        return lax.dynamic_index_in_dim(values, (member + ahead) % members, 0, keepdims=False)
-
-    total = block_of(window, 0)
-    for ahead in range(1, members):
-        total = total + moved(block_of(rounded, ahead), ahead * STRIDE).astype(jnp.float32)
+    own = [
+        from_above[m].astype(jnp.float32) + (from_below[m].astype(jnp.float32) + own_zero[m])
+        for m in range(members)
+    ]
+    total = own[0]
+    for m in range(1, members):
+        crossed = moved(own[m].astype(jnp.bfloat16), m * STRIDE)
+        total = total + crossed.astype(jnp.float32)
     return total
 
 
@@ -219,10 +234,14 @@
     )
     rows_in = arrived_input.reshape(slots_all, feature_count)
     rows_cot = arrived_cot.reshape(slots_all, feature_count)
-    shards = jnp.concatenate([w_gate[0], w_up[0], w_down[0]], axis=1)
+    shards = side_by_side(w_gate, w_up, w_down)
     mats = lax.all_gather(shards, "dp", axis=0, tiled=True)
     place = lax.axis_index("dp").astype(jnp.int32).reshape(1)
-    hidden, slope, activated, *parts = hidden_and_partial(place, rows_in, rows_cot.T, mats, groups)
+    rows_in, rows_cot, cot_turned = (
+        pltpu.with_memory_space_constraint(value, pltpu.VMEM)
+        for value in (rows_in, rows_cot, rows_cot.T)
+    )
+    hidden, slope, activated, *parts = hidden_and_partial(place, rows_in, cot_turned, mats, groups)
     back_rows = rows_back(hidden, rows_cot, slope, activated, mats)
     back = lax.all_to_all(
         back_rows.reshape(owners, capacity, 2 * feature_count),
@@ -231,6 +250,7 @@
         concat_axis=0,
         tiled=True,
     ).reshape(slots_all, 2 * feature_count)
+    back = pltpu.with_memory_space_constraint(back, pltpu.VMEM)
     grad_scale = 1.0 / math.sqrt(count_here * groups)
     w_down_grad = (window_reduce(*parts, groups) * grad_scale)[None]
     second_in, first_total, gate_grad = finish(
@@ -241,7 +261,7 @@
         second_grad,
         back,
     )
-    return (second_in, first_total, gate_grad, w_down_grad)
+    return (second_in, first_total, gate_grad.T, w_down_grad)
 
 
 def solution(mesh):

time: 191 us -> 187 us (0.979)
  local copies, waits for them, and re-layouts: 9.72 us -> 5.41 us
    unnamed x19 -> x10, local copies, waits for them, and re-layouts: 4.42 us -> 1.6 us
where the time goes in v5:
time: 187 us; the launch traced here: 186 us
  waiting for transfers between devices  87.2 us (47%)
  starting transfers between devices  51.6 us (28%)
  Pallas kernels  19.4 us (10%)
  between operations  14.2 us (8%)
  local copies, waits for them, and re-layouts  5.41 us (3%)
  other arithmetic  5.06 us (3%)
  matrix products  3.13 us (2%)
    ppermute x6, waiting for transfers between devices, moved(): lax.ppermute(value, 'dp', [(i, (i + by) % groups) for i in range(groups)])  33.1 us
    ppermute x6, starting transfers between devices, moved(): lax.ppermute(value, 'dp', [(i, (i + by) % groups) for i in range(groups)])  23.8 us
    all_gather x1, waiting for transfers between devices, per_device(): mats = lax.all_gather(shards, 'dp', axis=0, tiled=True)  22.9 us
    all_to_all x1, waiting for transfers between devices, per_device(): lax.all_to_all(send_input, 'expert', split_axis=0, concat_axis=0, tiled=T...  16.4 us
    all_to_all x1, starting transfers between devices, per_device(): lax.all_to_all(back_rows.reshape(owners, capacity, 2 * feature_count), 'e...  16.1 us
    all_to_all x1, waiting for transfers between devices, per_device(): lax.all_to_all(send_cot, 'expert', split_axis=0, concat_axis=0, tiled=True)  14.8 us
    pallas_call x1, Pallas kernels, rows_back(): pl.pallas_call(_back_kernel, grid=(steps,), in_specs=[column, pl.BlockSpe...  8.38 us
    all_to_all x1, starting transfers between devices, per_device(): lax.all_to_all(send_cot, 'expert', split_axis=0, concat_axis=0, tiled=True)  7.76 us
  transfers between devices with their start and end apart: 10, of which 7 were waited for; matrix products, arithmetic and copies ran while one was open for 7% of the time, Pallas kernels for 0%

profile of v5, /device:TPU:65, one launch (start us, length us, event | category | flops | bytes accessed | tf_op | source)
XLA Modules:
  0.0 186.0 jit_solution(12890494407497759180)
XLA Ops:
  7.2 0.0 all-gather.2.cloned.1.call-start
  7.2 1.7 side_by_side.1
  8.9 0.0 all-gather.2.cloned.1.call-update
  9.0 0.8 copy.25
  9.8 0.1 eq.42
  9.9 0.1 eq.38
  10.0 0.6 reduce-window.6
  10.6 0.2 slice_reduce_fusion
  10.9 0.8 copy.31.gates
  11.7 0.1 mul.39
  11.8 1.2 broadcast_in_dim.7
  13.0 0.7 convert_element_type.93
  13.8 0.1 fusion.12
  13.9 0.0 copy-start.2
  13.9 1.6 convolution_convert_fusion
  15.4 7.8 %all-to-all-start.1 = ((bf16[32,16,1024]{2,1,0:T(8,128)(2,1)}), bf16[32,16,1024]{2,1,0:T(8,128)(2,1)S(1)}, u32[]{:S(2)}, u32[]{:S(2)}) async-start(bf16[32,16,1024]{2,1,0:T(8,128)(2,1)} %bitcast.4), calls=%async_computation.1 | async-start | bytes 2097152 | tf_op jit(solution)/shard_map/all_to_all | solution.py:233
  23.2 0.3 broadcast_in_dim.6
  23.5 0.2 reshape.86
  23.7 1.6 convolution_convert_fusion.1
  25.3 14.8 %all-to-all-done.1 = bf16[32,16,1024]{2,1,0:T(8,128)(2,1)S(1)} async-done(((bf16[32,16,1024]{2,1,0:T(8,128)(2,1)}), bf16[32,16,1024]{2,1,0:T(8,128)(2,1)S(1)}, u32[]{:S(2)}, u32[]{:S(2)}) %all-to-all-start.1) | async-done | bytes 1048608 | tf_op jit(solution)/shard_map/all_to_all | solution.py:233
  40.1 3.9 %all-to-all-start = ((bf16[32,16,1024]{2,1,0:T(8,128)(2,1)}), bf16[32,16,1024]{2,1,0:T(8,128)(2,1)S(1)}, u32[]{:S(2)}, u32[]{:S(2)}) async-start(bf16[32,16,1024]{2,1,0:T(8,128)(2,1)} %bitcast.2), calls=%async_computation | async-start | bytes 2097152 | tf_op jit(solution)/shard_map/all_to_all | solution.py:232
  44.1 0.5 copy.30.cot
  44.6 16.4 %all-to-all-done = bf16[32,16,1024]{2,1,0:T(8,128)(2,1)S(1)} async-done(((bf16[32,16,1024]{2,1,0:T(8,128)(2,1)}), bf16[32,16,1024]{2,1,0:T(8,128)(2,1)S(1)}, u32[]{:S(2)}, u32[]{:S(2)}) %all-to-all-start) | async-done | bytes 1048608 | tf_op jit(solution)/shard_map/all_to_all | solution.py:232
  61.0 22.9 %all-gather.2.cloned.1.call-done.gate.up.down_mat = bf16[1024,2304]{1,0:T(8,128)(2,1)} async-done(((bf16[64,2304]{1,0:T(8,128)(2,1)}), bf16[1024,2304]{1,0:T(8,128)(2,1)}) %all-gather.2.cloned.1.call-update) | async-done | bytes 4718608 | tf_op jit(solution)/shard_map/all_gather | solution.py:238
  83.9 6.4 %hidden_and_partial.1 = (bf16[512,768]{1,0:T(8,128)(2,1)}, f32[512,768]{1,0:T(8,128)}, f32[512,768]{1,0:T(8,128)}, bf16[4,64,768]{2,1,0:T(8,128)(2,1)}, bf16[4,6...) custom-call(s32[1]{0:T(128)} %bitcast.1.place, bf16[512,1024]{1,0:T(8,128)(2,1)S(1)} %bitcast.51, ...), custom_call_target="tpu_custom_call" | custom-call | tf_op jit(solution)/shard_map/hidden_and_partial/pallas_call | solution.py:51
  90.3 8.4 %rows_back.1 = bf16[512,2048]{1,0:T(8,128)(2,1)} custom-call(bf16[512,768]{1,0:T(8,128)(2,1)} %get-tuple-element.14.hidden, bf16[512,1024]{1,0:T(8,128)(2,1)S(1)} %bitcast.49, f32[512,768]{1,0:T(8,128)} %get-tuple-element.15.slope, f32[512,768]{1,0:T(8,128)} %get-tuple-element.16.activated, bf16[1024,2304]{1,0:T(8,128)(2,1)} %all-gather.2.cloned.1.call-done.gate.up.down_mat, ...), custom_call_target="tpu_custom_call" | custom-call | tf_op jit(solution)/shard_map/rows_back/pallas_call | solution.py:108
  98.7 16.1 %all-to-all-start.2 = ((bf16[32,16,2048]{2,1,0:T(8,128)(2,1)}), bf16[32,16,2048]{2,1,0:T(8,128)(2,1)S(1)}, u32[]{:S(2)}, u32[]{:S(2)}) async-start(bf16[32,16,2048]{2,1,0:T(8,128)(2,1)} %bitcast.52), calls=%async_computation.2 | async-start | bytes 4194304 | tf_op jit(solution)/shard_map/all_to_all | solution.py:246
  114.8 0.0 copy-start.3
  114.8 1.9 %collective-permute-start = (bf16[4,64,768]{2,1,0:T(8,128)(2,1)}, bf16[4,64,768]{2,1,0:T(8,128)(2,1)S(1)}, u32[]{:S(2)}, u32[]{:S(2)}) collective-permute-start(bf16[4,64,768]{2,1,0:T(8,128)(2,1)} %get-tuple-element.20), channel_id=1, source_target_pairs={{0,480},{32,0},{64,32},{96,64},{128,96},{160,128},{192,160},{224,1... | collective-permute-start | bytes 1179656 | tf_op jit(solution)/shard_map/ppermute | solution.py:184
  116.7 3.4 %collective-permute-start.2 = (bf16[4,64,768]{2,1,0:T(8,128)(2,1)}, bf16[4,64,768]{2,1,0:T(8,128)(2,1)S(1)}, u32[]{:S(2)}, u32[]{:S(2)}) collective-permute-start(bf16[4,64,768]{2,1,0:T(8,128)(2,1)} %get-tuple-element.22), channel_id=1, source_target_pairs={{0,32},{32,64},{64,96},{96,128},{128,160},{160,192},{192,224},{224... | collective-permute-start | bytes 1179656 | tf_op jit(solution)/shard_map/ppermute | solution.py:184
  120.1 7.2 %collective-permute-done = bf16[4,64,768]{2,1,0:T(8,128)(2,1)S(1)} collective-permute-done((bf16[4,64,768]{2,1,0:T(8,128)(2,1)}, bf16[4,64,768]{2,1,0:T(8,128)(2,1)S(1)}, u32[]{:S(2)}, u32[]{:S(2)}) %collective-permute-start) | collective-permute-done | bytes 393248 | tf_op jit(solution)/shard_map/ppermute | solution.py:184
  127.3 0.1 add_convert_fusion
  127.4 2.1 %collective-permute-start.1 = (bf16[4,64,768]{2,1,0:T(8,128)(2,1)S(1)}, bf16[4,64,768]{2,1,0:T(8,128)(2,1)S(1)}, u32[]{:S(2)}, u32[]{:S(2)}) collective-permute-start(bf16[4,64,768]{2,1,0:T(8,128)(2,1)S(1)} %add_convert_fusion), channel_id=1, source_target_pairs={{0,480},{32,0},{64,32},{96,64},{128,96},{160,128},{192,160},{224,1... | collective-permute-start | bytes 1179656 | tf_op jit(solution)/shard_map/ppermute | solution.py:184
  129.5 0.0 collective-permute-done.2
  129.6 9.6 %collective-permute-done.1 = bf16[4,64,768]{2,1,0:T(8,128)(2,1)S(1)} collective-permute-done((bf16[4,64,768]{2,1,0:T(8,128)(2,1)S(1)}, bf16[4,64,768]{2,1,0:T(8,128)(2,1)S(1)}, u32[]{:S(2)}, u32[]{:S(2)}) %collective-permute-start.1) | collective-permute-done | bytes 393248 | tf_op jit(solution)/shard_map/ppermute | solution.py:184
  139.2 1.9 %fusion.7 = (bf16[64,768]{1,0:T(8,128)(2,1)}, bf16[64,768]{1,0:T(8,128)(2,1)S(1)}, bf16[64,768]{1,0:T(8,128)(2,1)S(1)}) fusion(f32[4,64,768]{2,1,0:T(8,128)} %get-tuple-element.23, bf16[4,64,768]{2,1,0:T(8,128)(2,1)S(1)} %collective-permute-done.2, bf16[4,64,768]{2,1,0:T(8,128)(2,1)S(1)} %collective-permute-done.1), kind=kLoop, calls=%fused_computation.16 | loop fusion | flops 737280 | bytes 1474560 | tf_op jit(solution)/shard_map/convert_element_type | solution.py:196
  141.0 4.8 %collective-permute-start.3 = (bf16[64,768]{1,0:T(8,128)(2,1)}, bf16[64,768]{1,0:T(8,128)(2,1)S(1)}, u32[]{:S(2)}, u32[]{:S(2)}) collective-permute-start(bf16[64,768]{1,0:T(8,128)(2,1)} %get-tuple-element.24), channel_id=1, source_target_pairs={{0,128},{32,160},{64,192},{96,224},{128,256},{160,288},{192,320},{... | collective-permute-start | bytes 294920 | tf_op jit(solution)/shard_map/ppermute | solution.py:184
  145.9 6.9 %collective-permute-start.4 = (bf16[64,768]{1,0:T(8,128)(2,1)S(1)}, bf16[64,768]{1,0:T(8,128)(2,1)S(1)}, u32[]{:S(2)}, u32[]{:S(2)}) collective-permute-start(bf16[64,768]{1,0:T(8,128)(2,1)S(1)} %get-tuple-element.26), channel_id=1, source_target_pairs={{0,256},{32,288},{64,320},{96,352},{128,384},{160,416},{192,448},{... | collective-permute-start | bytes 294920 | tf_op jit(solution)/shard_map/ppermute | solution.py:184
  152.8 4.6 %collective-permute-start.5 = (bf16[64,768]{1,0:T(8,128)(2,1)S(1)}, bf16[64,768]{1,0:T(8,128)(2,1)}, u32[]{:S(2)}, u32[]{:S(2)}) collective-permute-start(bf16[64,768]{1,0:T(8,128)(2,1)S(1)} %get-tuple-element.25), channel_id=1, source_target_pairs={{0,384},{32,416},{64,448},{96,480},{128,0},{160,32},{192,64},{224,... | collective-permute-start | bytes 294920 | tf_op jit(solution)/shard_map/ppermute | solution.py:184
  157.5 0.1 reduce_sum.12
  157.7 0.1 copy.28
  157.8 0.6 add.56.slot
  158.4 0.0 collective-permute-done.3
  158.4 1.9 %collective-permute-done.4 = bf16[64,768]{1,0:T(8,128)(2,1)S(1)} collective-permute-done((bf16[64,768]{1,0:T(8,128)(2,1)S(1)}, bf16[64,768]{1,0:T(8,128)(2,1)S(1)}, u32[]{:S(2)}, u32[]{:S(2)}) %collective-permute-start.4) | collective-permute-done | bytes 98336 | tf_op jit(solution)/shard_map/ppermute | solution.py:184
  160.3 14.3 %collective-permute-done.5 = bf16[64,768]{1,0:T(8,128)(2,1)} collective-permute-done((bf16[64,768]{1,0:T(8,128)(2,1)S(1)}, bf16[64,768]{1,0:T(8,128)(2,1)}, u32[]{:S(2)}, u32[]{:S(2)}) %collective-permute-start.5) | collective-permute-done | bytes 98336 | tf_op jit(solution)/shard_map/ppermute | solution.py:184
  174.6 1.7 fusion.6
  176.4 0.0 all-to-all-done.2
  176.4 2.8 %finish.1 = (bf16[128,1024]{1,0:T(8,128)(2,1)}, bf16[128,1024]{1,0:T(8,128)(2,1)}, f32[2,128]{1,0:T(2,128)}) custom-call(s32[128,2]{1,0:T(8,128)} %add.56.slot, f32[128,2]{1,0:T(8,128)} %copy-done.1, bf16[128,1024]{1,0:T(8,128)(2,1)} %second_out.1, bf16[128,1024]{1,0:T(8,128)(2,1)} %first_grad.1, bf16[128,1024]{1,0:T(8,128)(2,1)} %second_grad.1, ...), custom_call_target="tpu_custom_call" | custom-call | tf_op jit(solution)/shard_map/finish/pallas_call | solution.py:161
  (11 shorter events, 0.1 us)
Async XLA Ops:
  7.2 76.7 %all-gather.2.cloned.1.call-start = ((), (), s32[]{:S(2)}) async-start(), calls=%async_computation.3 | async-start | bytes 5013504 | tf_op jit(solution)/shard_map/all_gather | solution.py:238
  11.7 3.8 %copy-start.1 = (f32[128,2]{1,0:T(8,128)}, f32[128,2]{1,0:T(8,128)S(1)}, u32[]{:S(2)}) copy-start(f32[128,2]{1,0:T(8,128)S(1)} %copy.31.gates) | copy-start | bytes 3076
  13.9 9.3 %copy-start.2 = (bf16[128,1024]{1,0:T(8,128)(2,1)S(1)}, bf16[128,1024]{1,0:T(8,128)(2,1)}, u32[]{:S(2)}) copy-start(bf16[128,1024]{1,0:T(8,128)(2,1)} %param.9) | copy-start | bytes 786436
  15.4 24.7 %all-to-all-start.1 = ((bf16[32,16,1024]{2,1,0:T(8,128)(2,1)}), bf16[32,16,1024]{2,1,0:T(8,128)(2,1)S(1)}, u32[]{:S(2)}, u32[]{:S(2)}) async-start(bf16[32,16,1024]{2,1,0:T(8,128)(2,1)} %bitcast.4), calls=%async_computation.1 | async-start | bytes 2097152 | tf_op jit(solution)/shard_map/all_to_all | solution.py:233
  40.1 20.8 %all-to-all-start = ((bf16[32,16,1024]{2,1,0:T(8,128)(2,1)}), bf16[32,16,1024]{2,1,0:T(8,128)(2,1)S(1)}, u32[]{:S(2)}, u32[]{:S(2)}) async-start(bf16[32,16,1024]{2,1,0:T(8,128)(2,1)} %bitcast.2), calls=%async_computation | async-start | bytes 2097152 | tf_op jit(solution)/shard_map/all_to_all | solution.py:232
  98.7 28.6 %copy-start = (f32[4,64,768]{2,1,0:T(8,128)S(1)}, f32[4,64,768]{2,1,0:T(8,128)}, u32[]{:S(2)}) copy-start(f32[4,64,768]{2,1,0:T(8,128)} %get-tuple-element.21) | copy-start | bytes 2359300
  98.7 77.6 %all-to-all-start.2 = ((bf16[32,16,2048]{2,1,0:T(8,128)(2,1)}), bf16[32,16,2048]{2,1,0:T(8,128)(2,1)S(1)}, u32[]{:S(2)}, u32[]{:S(2)}) async-start(bf16[32,16,2048]{2,1,0:T(8,128)(2,1)} %bitcast.52), calls=%async_computation.2 | async-start | bytes 4194304 | tf_op jit(solution)/shard_map/all_to_all | solution.py:246
  114.8 42.7 %copy-start.3 = (s32[128,2]{0,1:T(2,128)S(1)}, s32[128,2]{0,1:T(2,128)}, u32[]{:S(2)}) copy-start(s32[128,2]{0,1:T(2,128)} %param.13) | copy-start | bytes 3076
  114.8 12.5 %collective-permute-start = (bf16[4,64,768]{2,1,0:T(8,128)(2,1)}, bf16[4,64,768]{2,1,0:T(8,128)(2,1)S(1)}, u32[]{:S(2)}, u32[]{:S(2)}) collective-permute-start(bf16[4,64,768]{2,1,0:T(8,128)(2,1)} %get-tuple-element.20), channel_id=1, source_target_pairs={{0,480},{32,0},{64,32},{96,64},{128,96},{160,128},{192,160},{224,1... | collective-permute-start | bytes 1179656 | tf_op jit(solution)/shard_map/ppermute | solution.py:184
  116.7 12.8 %collective-permute-start.2 = (bf16[4,64,768]{2,1,0:T(8,128)(2,1)}, bf16[4,64,768]{2,1,0:T(8,128)(2,1)S(1)}, u32[]{:S(2)}, u32[]{:S(2)}) collective-permute-start(bf16[4,64,768]{2,1,0:T(8,128)(2,1)} %get-tuple-element.22), channel_id=1, source_target_pairs={{0,32},{32,64},{64,96},{96,128},{128,160},{160,192},{192,224},{224... | collective-permute-start | bytes 1179656 | tf_op jit(solution)/shard_map/ppermute | solution.py:184
  127.4 11.8 %collective-permute-start.1 = (bf16[4,64,768]{2,1,0:T(8,128)(2,1)S(1)}, bf16[4,64,768]{2,1,0:T(8,128)(2,1)S(1)}, u32[]{:S(2)}, u32[]{:S(2)}) collective-permute-start(bf16[4,64,768]{2,1,0:T(8,128)(2,1)S(1)} %add_convert_fusion), channel_id=1, source_target_pairs={{0,480},{32,0},{64,32},{96,64},{128,96},{160,128},{192,160},{224,1... | collective-permute-start | bytes 1179656 | tf_op jit(solution)/shard_map/ppermute | solution.py:184
  141.0 17.4 %collective-permute-start.3 = (bf16[64,768]{1,0:T(8,128)(2,1)}, bf16[64,768]{1,0:T(8,128)(2,1)S(1)}, u32[]{:S(2)}, u32[]{:S(2)}) collective-permute-start(bf16[64,768]{1,0:T(8,128)(2,1)} %get-tuple-element.24), channel_id=1, source_target_pairs={{0,128},{32,160},{64,192},{96,224},{128,256},{160,288},{192,320},{... | collective-permute-start | bytes 294920 | tf_op jit(solution)/shard_map/ppermute | solution.py:184
  145.9 14.4 %collective-permute-start.4 = (bf16[64,768]{1,0:T(8,128)(2,1)S(1)}, bf16[64,768]{1,0:T(8,128)(2,1)S(1)}, u32[]{:S(2)}, u32[]{:S(2)}) collective-permute-start(bf16[64,768]{1,0:T(8,128)(2,1)S(1)} %get-tuple-element.26), channel_id=1, source_target_pairs={{0,256},{32,288},{64,320},{96,352},{128,384},{160,416},{192,448},{... | collective-permute-start | bytes 294920 | tf_op jit(solution)/shard_map/ppermute | solution.py:184
  152.8 21.8 %collective-permute-start.5 = (bf16[64,768]{1,0:T(8,128)(2,1)S(1)}, bf16[64,768]{1,0:T(8,128)(2,1)}, u32[]{:S(2)}, u32[]{:S(2)}) collective-permute-start(bf16[64,768]{1,0:T(8,128)(2,1)S(1)} %get-tuple-element.25), channel_id=1, source_target_pairs={{0,384},{32,416},{64,448},{96,480},{128,0},{160,32},{192,64},{224,... | collective-permute-start | bytes 294920 | tf_op jit(solution)/shard_map/ppermute | solution.py:184
Sparse Core Ops, SparseCore 0:
  10.1 73.7 all-gather.1

commit v6 on v5

--- a/solution.py
+++ b/solution.py
@@ -8,30 +8,67 @@
 from jax.sharding import PartitionSpec as P
 
 
-BLOCK = 256
 STRIDE = 4
+ROWS_STEP = 64
+HIDDEN_BYTES = 48 * 1024 * 1024
+BACK_BYTES = 57 * 1024 * 1024
+HELD = pl.BlockSpec(memory_space=pltpu.VMEM)
 
 
 def _dot(a, b, over):
     return lax.dot_general(a, b, ((over[:1], over[1:]), ((), ())), preferred_element_type=jnp.float32)
 
 
+def in_vmem(value):
+    return pltpu.with_memory_space_constraint(value, pltpu.VMEM)
+
+
 def _hidden_kernel(
-    place, rows, cot, gate, up, hidden, slope, activated, send_two, send_one, own_three, own_zero, classes
+    place,
+    mats,
+    rows,
+    cot,
+    hidden,
+    slope,
+    activated,
+    send_two,
+    send_one,
+    own_three,
+    own_zero,
+    gate,
+    up,
+    classes,
+    sems,
 ):
-    pre_gate = _dot(rows[...], gate[...], (1, 0))
-    pre_up = _dot(rows[...], up[...], (1, 0))
-    squashed = jax.nn.sigmoid(pre_gate)
-    active = pre_gate * squashed
-    here = (active * pre_up).astype(jnp.bfloat16)
-    hidden[...] = here
-    activated[...] = active
-    slope[...] = pre_up * squashed * (1.0 + pre_gate * (1.0 - squashed))
-    partial = _dot(cot[...], here, (1, 0))
+    slots, width = hidden.shape
+    copies = [
+        pltpu.make_async_copy(mats.at[:, pl.ds(k * width, width)], target, sems.at[k])
+        for k, target in enumerate((gate, up))
+    ]
+    for copy in copies:
+        copy.start()
+    copies[0].wait()
+    activated[...] = _dot(rows[...], gate[...], (1, 0))
+    copies[1].wait()
+    slope[...] = _dot(rows[...], up[...], (1, 0))
+
+    def some_rows(step, carry):
+        at = pl.ds(pl.multiple_of(step * ROWS_STEP, ROWS_STEP), ROWS_STEP)
+        pre_gate = activated[at, :]
+        pre_up = slope[at, :]
+        squashed = jax.nn.sigmoid(pre_gate)
+        active = pre_gate * squashed
+        hidden[at, :] = (active * pre_up).astype(jnp.bfloat16)
+        activated[at, :] = active
+        slope[at, :] = pre_up * squashed * (1.0 + pre_gate * (1.0 - squashed))
+        return carry
+
+    lax.fori_loop(0, slots // ROWS_STEP, some_rows, 0)
     members, block = classes.shape[1], classes.shape[2]
-    for index in range(members * STRIDE):
+    groups = members * STRIDE
+    partial = _dot(cot[...], hidden[...], (1, 0))
+    for index in range(groups):
         classes[index % STRIDE, index // STRIDE] = partial[index * block : (index + 1) * block]
-    groups = members * STRIDE
     for ahead, target in ((-2, send_two), (1, send_one), (-1, own_three), (0, own_zero)):
         owner = (place[0] + ahead + groups) % groups
         for m in range(members):
@@ -42,26 +79,17 @@
 def hidden_and_partial(place, rows, cot, mats, groups):
     slots, features = rows.shape
     width = mats.shape[1] // 3
-    steps = width // BLOCK
     members, block = groups // STRIDE, features // groups
-    held = pl.BlockSpec(memory_space=pltpu.VMEM)
-    column = pl.BlockSpec((slots, BLOCK), lambda j, place: (0, j))
-    part = pl.BlockSpec((members, block, BLOCK), lambda j, place: (0, 0, j))
     part_shape = (members, block, width)
-    return pl.pallas_call(
+    results = pl.pallas_call(
         _hidden_kernel,
-        grid_spec=pltpu.PrefetchScalarGridSpec(
-            num_scalar_prefetch=1,
-            grid=(steps,),
-            in_specs=[
-                held,
-                held,
-                pl.BlockSpec((features, BLOCK), lambda j, place: (0, j)),
-                pl.BlockSpec((features, BLOCK), lambda j, place: (0, j + steps)),
-            ],
-            out_specs=[column, column, column, part, part, part, part],
-            scratch_shapes=[pltpu.VMEM((STRIDE, members, block, BLOCK), jnp.float32)],
-        ),
+        in_specs=[
+            pl.BlockSpec(memory_space=pltpu.SMEM),
+            pl.BlockSpec(memory_space=pltpu.HBM),
+            HELD,
+            HELD,
+        ],
+        out_specs=[HELD] * 7,
         out_shape=[
             jax.ShapeDtypeStruct((slots, width), jnp.bfloat16),
             jax.ShapeDtypeStruct((slots, width), jnp.float32),
@@ -71,60 +99,62 @@
             jax.ShapeDtypeStruct(part_shape, jnp.float32),
             jax.ShapeDtypeStruct(part_shape, jnp.float32),
         ],
+        scratch_shapes=[
+            pltpu.VMEM((features, width), jnp.bfloat16),
+            pltpu.VMEM((features, width), jnp.bfloat16),
+            pltpu.VMEM((STRIDE, members, block, width), jnp.float32),
+            pltpu.SemaphoreType.DMA((2,)),
+        ],
+        compiler_params=pltpu.CompilerParams(vmem_limit_bytes=HIDDEN_BYTES),
         name="hidden_and_partial",
-    )(place, rows, cot, mats, mats)
-
-
-def _back_kernel(hidden, cot, slope, activated, gate, up, down_mat, back, out_sum, cot_sum):
-    at = pl.program_id(0)
-    features = cot.shape[1]
-    down = down_mat[...]
-    hidden_cot = _dot(cot[...], down, (1, 0))
-    gate_cot = (hidden_cot * slope[...]).astype(jnp.bfloat16)
-    up_cot = (hidden_cot * activated[...]).astype(jnp.bfloat16)
-    out_part = _dot(hidden[...], down, (1, 1))
-    cot_part = _dot(gate_cot, gate[...], (1, 1)) + _dot(up_cot, up[...], (1, 1))
-
-    @pl.when(at == 0)
-    def _():
-        out_sum[...] = out_part
-        cot_sum[...] = cot_part
-
-    @pl.when(at > 0)
-    def _():
-        out_sum[...] += out_part
-        cot_sum[...] += cot_part
-
-    @pl.when(at == pl.num_programs(0) - 1)
-    def _():
-        back[:, :features] = out_sum[...].astype(jnp.bfloat16)
-        back[:, features:] = cot_sum[...].astype(jnp.bfloat16)
+    )(place, mats, rows, cot)
+    return [*[in_vmem(value) for value in results[:3]], *results[3:]]
+
+
+def _back_kernel(mats, hidden, cot, slope, activated, back, down, gate_up, cots, out_rows, cot_rows, sems):
+    features, width = down.shape
+    leaving = [
+        pltpu.make_async_copy(source, back.at[:, pl.ds(k * features, features)], sems.at[2 + k])
+        for k, source in enumerate((out_rows, cot_rows))
+    ]
+    copies = [
+        pltpu.make_async_copy(mats.at[:, pl.ds(at, size)], target, sems.at[k])
+        for k, (at, size, target) in enumerate(((2 * width, width, down), (0, 2 * width, gate_up)))
+    ]
+    for copy in copies:
+        copy.start()
+    copies[0].wait()
+    hidden_cot = _dot(cot[...], down[...], (1, 0))
+    cots[:, :width] = (hidden_cot * slope[...]).astype(jnp.bfloat16)
+    cots[:, width:] = (hidden_cot * activated[...]).astype(jnp.bfloat16)
+    out_rows[...] = _dot(hidden[...], down[...], (1, 1)).astype(jnp.bfloat16)
+    leaving[0].start()
+    copies[1].wait()
+    cot_rows[...] = _dot(cots[...], gate_up[...], (1, 1)).astype(jnp.bfloat16)
+    leaving[1].start()
+    for copy in leaving:
+        copy.wait()
 
 
 def rows_back(hidden, cot, slope, activated, mats):
     slots, features = cot.shape
-    steps = hidden.shape[1] // BLOCK
-    column = pl.BlockSpec((slots, BLOCK), lambda j: (0, j))
+    width = hidden.shape[1]
     return pl.pallas_call(
         _back_kernel,
-        grid=(steps,),
-        in_specs=[
-            column,
-            pl.BlockSpec(memory_space=pltpu.VMEM),
-            column,
-            column,
-            pl.BlockSpec((features, BLOCK), lambda j: (0, j)),
-            pl.BlockSpec((features, BLOCK), lambda j: (0, j + steps)),
-            pl.BlockSpec((features, BLOCK), lambda j: (0, j + 2 * steps)),
-        ],
-        out_specs=pl.BlockSpec((slots, 2 * features), lambda j: (0, 0)),
+        in_specs=[pl.BlockSpec(memory_space=pltpu.HBM), *[HELD] * 4],
+        out_specs=pl.BlockSpec(memory_space=pltpu.HBM),
         out_shape=jax.ShapeDtypeStruct((slots, 2 * features), jnp.bfloat16),
         scratch_shapes=[
-            pltpu.VMEM((slots, features), jnp.float32),
-            pltpu.VMEM((slots, features), jnp.float32),
-        ],
+            pltpu.VMEM((features, width), jnp.bfloat16),
+            pltpu.VMEM((features, 2 * width), jnp.bfloat16),
+            pltpu.VMEM((slots, 2 * width), jnp.bfloat16),
+            pltpu.VMEM((slots, features), jnp.bfloat16),
+            pltpu.VMEM((slots, features), jnp.bfloat16),
+            pltpu.SemaphoreType.DMA((4,)),
+        ],
+        compiler_params=pltpu.CompilerParams(vmem_limit_bytes=BACK_BYTES),
         name="rows_back",
-    )(hidden, cot, slope, activated, mats, mats, mats)
+    )(mats, hidden, cot, slope, activated)
 
 
 def _beside_kernel(gate, up, down, out):
@@ -157,11 +187,10 @@
 
 
 def finish(slot, gates, second_out, first_grad, second_grad, back):
-    held = pl.BlockSpec(memory_space=pltpu.VMEM)
     return pl.pallas_call(
         _finish_kernel,
-        in_specs=[held] * 6,
-        out_specs=[held] * 3,
+        in_specs=[HELD] * 6,
+        out_specs=[HELD] * 3,
         out_shape=[
             jax.ShapeDtypeStruct(second_out.shape, jnp.bfloat16),
             jax.ShapeDtypeStruct(first_grad.shape, jnp.bfloat16),
@@ -236,11 +265,9 @@
     rows_cot = arrived_cot.reshape(slots_all, feature_count)
     shards = side_by_side(w_gate, w_up, w_down)
     mats = lax.all_gather(shards, "dp", axis=0, tiled=True)
+    mats = pltpu.with_memory_space_constraint(mats, pltpu.HBM)
     place = lax.axis_index("dp").astype(jnp.int32).reshape(1)
-    rows_in, rows_cot, cot_turned = (
-        pltpu.with_memory_space_constraint(value, pltpu.VMEM)
-        for value in (rows_in, rows_cot, rows_cot.T)
-    )
+    rows_in, rows_cot, cot_turned = (in_vmem(value) for value in (rows_in, rows_cot, rows_cot.T))
     hidden, slope, activated, *parts = hidden_and_partial(place, rows_in, cot_turned, mats, groups)
     back_rows = rows_back(hidden, rows_cot, slope, activated, mats)
     back = lax.all_to_all(
@@ -250,7 +277,7 @@
         concat_axis=0,
         tiled=True,
     ).reshape(slots_all, 2 * feature_count)
-    back = pltpu.with_memory_space_constraint(back, pltpu.VMEM)
+    back = in_vmem(back)
     grad_scale = 1.0 / math.sqrt(count_here * groups)
     w_down_grad = (window_reduce(*parts, groups) * grad_scale)[None]
     second_in, first_total, gate_grad = finish(

time: 187 us -> 190 us (1.016)
  local copies, waits for them, and re-layouts: 5.41 us -> 10.7 us
    unnamed x10 -> x20, local copies, waits for them, and re-layouts: 1.6 us -> 6.94 us
where the time goes in v6:
time: 190 us; the launch traced here: 189 us
  waiting for transfers between devices  87.3 us (46%)
  starting transfers between devices  51.4 us (27%)
  Pallas kernels  18 us (9%)
  between operations  14.3 us (8%)
  local copies, waits for them, and re-layouts  10.7 us (6%)
  other arithmetic  4.53 us (2%)
  matrix products  3.09 us (2%)
    ppermute x6, waiting for transfers between devices, moved(): lax.ppermute(value, 'dp', [(i, (i + by) % groups) for i in range(groups)])  33.6 us
    ppermute x6, starting transfers between devices, moved(): lax.ppermute(value, 'dp', [(i, (i + by) % groups) for i in range(groups)])  23.6 us
    all_gather x1, waiting for transfers between devices, per_device(): mats = lax.all_gather(shards, 'dp', axis=0, tiled=True)  22.5 us
    all_to_all x1, waiting for transfers between devices, per_device(): lax.all_to_all(send_input, 'expert', split_axis=0, concat_axis=0, tiled=T...  16.4 us
    all_to_all x1, starting transfers between devices, per_device(): lax.all_to_all(back_rows.reshape(owners, capacity, 2 * feature_count), 'e...  16.1 us
    all_to_all x1, waiting for transfers between devices, per_device(): lax.all_to_all(send_cot, 'expert', split_axis=0, concat_axis=0, tiled=True)  14.9 us
    all_to_all x1, starting transfers between devices, per_device(): lax.all_to_all(send_cot, 'expert', split_axis=0, concat_axis=0, tiled=True)  7.76 us
    pallas_call x1, Pallas kernels, hidden_and_partial(): pl.pallas_call(_hidden_kernel, in_specs=[pl.BlockSpec(memory_space=pltpu....  7.4 us
  transfers between devices with their start and end apart: 10, of which 7 were waited for; matrix products, arithmetic and copies ran while one was open for 7% of the time, Pallas kernels for 0%

profile of v6, /device:TPU:65, one launch (start us, length us, event | category | flops | bytes accessed | tf_op | source)
XLA Modules:
  0.0 189.4 jit_solution(1189889820772798068)
XLA Ops:
  7.2 0.0 all-gather.2.cloned.1.call-start
  7.2 1.7 side_by_side.1
  9.0 0.0 all-gather.2.cloned.1.call-update
  9.0 0.8 copy.25
  9.8 0.1 eq.42
  9.9 0.1 eq.38
  10.1 0.6 reduce-window.6
  10.7 0.2 slice_reduce_fusion
  10.9 0.8 copy.31.gates
  11.7 0.1 mul.39
  11.8 0.5 copy-done.6
  12.3 1.2 broadcast_in_dim.7
  13.5 0.7 convert_element_type.93
  14.3 0.1 fusion.12
  14.4 1.5 convolution_convert_fusion
  15.9 7.8 %all-to-all-start.1 = ((bf16[32,16,1024]{2,1,0:T(8,128)(2,1)}), bf16[32,16,1024]{2,1,0:T(8,128)(2,1)S(1)}, u32[]{:S(2)}, u32[]{:S(2)}) async-start(bf16[32,16,1024]{2,1,0:T(8,128)(2,1)} %bitcast.4), calls=%async_computation.1 | async-start | bytes 2097152 | tf_op jit(solution)/shard_map/all_to_all | solution.py:262
  23.7 0.3 broadcast_in_dim.6
  24.0 0.2 reshape.86
  24.2 1.6 convolution_convert_fusion.1
  25.7 14.9 %all-to-all-done.1 = bf16[32,16,1024]{2,1,0:T(8,128)(2,1)S(1)} async-done(((bf16[32,16,1024]{2,1,0:T(8,128)(2,1)}), bf16[32,16,1024]{2,1,0:T(8,128)(2,1)S(1)}, u32[]{:S(2)}, u32[]{:S(2)}) %all-to-all-start.1) | async-done | bytes 1048608 | tf_op jit(solution)/shard_map/all_to_all | solution.py:262
  40.6 3.9 %all-to-all-start = ((bf16[32,16,1024]{2,1,0:T(8,128)(2,1)}), bf16[32,16,1024]{2,1,0:T(8,128)(2,1)S(1)}, u32[]{:S(2)}, u32[]{:S(2)}) async-start(bf16[32,16,1024]{2,1,0:T(8,128)(2,1)} %bitcast.2), calls=%async_computation | async-start | bytes 2097152 | tf_op jit(solution)/shard_map/all_to_all | solution.py:261
  44.5 0.5 copy.30.cot
  45.1 16.4 %all-to-all-done = bf16[32,16,1024]{2,1,0:T(8,128)(2,1)S(1)} async-done(((bf16[32,16,1024]{2,1,0:T(8,128)(2,1)}), bf16[32,16,1024]{2,1,0:T(8,128)(2,1)S(1)}, u32[]{:S(2)}, u32[]{:S(2)}) %all-to-all-start) | async-done | bytes 1048608 | tf_op jit(solution)/shard_map/all_to_all | solution.py:261
  61.4 22.5 %all-gather.2.cloned.1.call-done.mats = bf16[1024,2304]{1,0:T(8,128)(2,1)} async-done(((bf16[64,2304]{1,0:T(8,128)(2,1)}), bf16[1024,2304]{1,0:T(8,128)(2,1)}) %all-gather.2.cloned.1.call-update) | async-done | bytes 4718608 | tf_op jit(solution)/shard_map/all_gather | solution.py:267
  83.9 7.4 %hidden_and_partial.1 = (bf16[512,768]{1,0:T(8,128)(2,1)S(1)}, f32[512,768]{1,0:T(8,128)}, f32[512,768]{1,0:T(8,128)}, bf16[4,64,768]{2,1,0:T(8,128)(2,1)S(1)}, ...) custom-call(s32[1]{0:T(128)} %bitcast.1.place, ...), custom_call_target="tpu_custom_call" | custom-call | tf_op jit(solution)/shard_map/hidden_and_partial/pallas_call | solution.py:84
  91.3 1.0 copy-done.2
  92.3 1.0 copy-done.4
  93.2 1.5 copy-done
  94.8 1.4 copy-done.1
  96.2 6.1 %rows_back.1 = bf16[512,2048]{1,0:T(8,128)(2,1)} custom-call(bf16[1024,2304]{1,0:T(8,128)(2,1)} %all-gather.2.cloned.1.call-done.mats, bf16[512,768]{1,0:T(8,128)(2,1)S(1)} %get-tuple-element.14.hidden, bf16[512,1024]{1,0:T(8,128)(2,1)S(1)} %bitcast.49, f32[512,768]{1,0:T(8,128)S(1)} %copy-done, f32[512,768]{1,0:T(8,128)S(1)} %copy-done.1), custom_call_target="tpu_custom_call" | custom-call | tf_op jit(solution)/shard_map/rows_back/pallas_call | solution.py:142
  102.3 16.1 %all-to-all-start.2 = ((bf16[32,16,2048]{2,1,0:T(8,128)(2,1)}), bf16[32,16,2048]{2,1,0:T(8,128)(2,1)S(1)}, u32[]{:S(2)}, u32[]{:S(2)}) async-start(bf16[32,16,2048]{2,1,0:T(8,128)(2,1)} %bitcast.52), calls=%async_computation.2 | async-start | bytes 4194304 | tf_op jit(solution)/shard_map/all_to_all | solution.py:273
  118.4 1.9 %collective-permute-start = (bf16[4,64,768]{2,1,0:T(8,128)(2,1)}, bf16[4,64,768]{2,1,0:T(8,128)(2,1)S(1)}, u32[]{:S(2)}, u32[]{:S(2)}) collective-permute-start(bf16[4,64,768]{2,1,0:T(8,128)(2,1)} %copy-done.5), channel_id=1, source_target_pairs={{0,480},{32,0},{64,32},{96,64},{128,96},{160,128},{192,160},{224,1... | collective-permute-start | bytes 1179656 | tf_op jit(solution)/shard_map/ppermute | solution.py:213
  120.4 3.4 %collective-permute-start.2 = (bf16[4,64,768]{2,1,0:T(8,128)(2,1)S(1)}, bf16[4,64,768]{2,1,0:T(8,128)(2,1)}, u32[]{:S(2)}, u32[]{:S(2)}) collective-permute-start(bf16[4,64,768]{2,1,0:T(8,128)(2,1)S(1)} %get-tuple-element.22), channel_id=1, source_target_pairs={{0,32},{32,64},{64,96},{96,128},{128,160},{160,192},{192,224},{224... | collective-permute-start | bytes 1179656 | tf_op jit(solution)/shard_map/ppermute | solution.py:213
  123.7 7.3 %collective-permute-done = bf16[4,64,768]{2,1,0:T(8,128)(2,1)S(1)} collective-permute-done((bf16[4,64,768]{2,1,0:T(8,128)(2,1)}, bf16[4,64,768]{2,1,0:T(8,128)(2,1)S(1)}, u32[]{:S(2)}, u32[]{:S(2)}) %collective-permute-start) | collective-permute-done | bytes 393248 | tf_op jit(solution)/shard_map/ppermute | solution.py:213
  131.1 0.1 add_convert_fusion
  131.2 2.1 %collective-permute-start.1 = (bf16[4,64,768]{2,1,0:T(8,128)(2,1)S(1)}, bf16[4,64,768]{2,1,0:T(8,128)(2,1)S(1)}, u32[]{:S(2)}, u32[]{:S(2)}) collective-permute-start(bf16[4,64,768]{2,1,0:T(8,128)(2,1)S(1)} %add_convert_fusion), channel_id=1, source_target_pairs={{0,480},{32,0},{64,32},{96,64},{128,96},{160,128},{192,160},{224,1... | collective-permute-start | bytes 1179656 | tf_op jit(solution)/shard_map/ppermute | solution.py:213
  133.3 9.7 %collective-permute-done.1 = bf16[4,64,768]{2,1,0:T(8,128)(2,1)S(1)} collective-permute-done((bf16[4,64,768]{2,1,0:T(8,128)(2,1)S(1)}, bf16[4,64,768]{2,1,0:T(8,128)(2,1)S(1)}, u32[]{:S(2)}, u32[]{:S(2)}) %collective-permute-start.1) | collective-permute-done | bytes 393248 | tf_op jit(solution)/shard_map/ppermute | solution.py:213
  143.0 1.3 fusion.7
  144.4 4.4 %collective-permute-start.3 = (bf16[64,768]{1,0:T(8,128)(2,1)S(1)}, bf16[64,768]{1,0:T(8,128)(2,1)S(1)}, u32[]{:S(2)}, u32[]{:S(2)}) collective-permute-start(bf16[64,768]{1,0:T(8,128)(2,1)S(1)} %get-tuple-element.24), channel_id=1, source_target_pairs={{0,128},{32,160},{64,192},{96,224},{128,256},{160,288},{192,320},{... | collective-permute-start | bytes 294920 | tf_op jit(solution)/shard_map/ppermute | solution.py:213
  148.8 6.9 %collective-permute-start.4 = (bf16[64,768]{1,0:T(8,128)(2,1)S(1)}, bf16[64,768]{1,0:T(8,128)(2,1)S(1)}, u32[]{:S(2)}, u32[]{:S(2)}) collective-permute-start(bf16[64,768]{1,0:T(8,128)(2,1)S(1)} %get-tuple-element.26), channel_id=1, source_target_pairs={{0,256},{32,288},{64,320},{96,352},{128,384},{160,416},{192,448},{... | collective-permute-start | bytes 294920 | tf_op jit(solution)/shard_map/ppermute | solution.py:213
  155.7 4.9 %collective-permute-start.5 = (bf16[64,768]{1,0:T(8,128)(2,1)S(1)}, bf16[64,768]{1,0:T(8,128)(2,1)S(1)}, u32[]{:S(2)}, u32[]{:S(2)}) collective-permute-start(bf16[64,768]{1,0:T(8,128)(2,1)S(1)} %get-tuple-element.25), channel_id=1, source_target_pairs={{0,384},{32,416},{64,448},{96,480},{128,0},{160,32},{192,64},{224,... | collective-permute-start | bytes 294920 | tf_op jit(solution)/shard_map/ppermute | solution.py:213
  160.6 0.1 reduce_sum.12
  160.8 0.1 copy.28
  160.9 0.6 add.56.slot
  161.5 1.7 collective-permute-done.4
  163.2 14.8 %collective-permute-done.5 = bf16[64,768]{1,0:T(8,128)(2,1)S(1)} collective-permute-done((bf16[64,768]{1,0:T(8,128)(2,1)S(1)}, bf16[64,768]{1,0:T(8,128)(2,1)S(1)}, u32[]{:S(2)}, u32[]{:S(2)}) %collective-permute-start.5) | collective-permute-done | bytes 98336 | tf_op jit(solution)/shard_map/ppermute | solution.py:213
  178.0 1.7 fusion.6
  179.8 2.8 %finish.1 = (bf16[128,1024]{1,0:T(8,128)(2,1)}, bf16[128,1024]{1,0:T(8,128)(2,1)}, f32[2,128]{1,0:T(2,128)}) custom-call(s32[128,2]{1,0:T(8,128)} %add.56.slot, f32[128,2]{1,0:T(8,128)} %copy-done.6, bf16[128,1024]{1,0:T(8,128)(2,1)} %second_out.1, bf16[128,1024]{1,0:T(8,128)(2,1)} %first_grad.1, bf16[128,1024]{1,0:T(8,128)(2,1)} %second_grad.1, ...), custom_call_target="tpu_custom_call" | custom-call | tf_op jit(solution)/shard_map/finish/pallas_call | solution.py:190
  (21 shorter events, 0.1 us)
Async XLA Ops:
  7.2 76.7 %all-gather.2.cloned.1.call-start = ((), (), s32[]{:S(2)}) async-start(), calls=%async_computation.3 | async-start | bytes 5013504 | tf_op jit(solution)/shard_map/all_gather | solution.py:267
  11.7 0.6 copy-start.6
  14.4 9.3 %copy-start.7 = (bf16[128,1024]{1,0:T(8,128)(2,1)S(1)}, bf16[128,1024]{1,0:T(8,128)(2,1)}, u32[]{:S(2)}) copy-start(bf16[128,1024]{1,0:T(8,128)(2,1)} %param.9) | copy-start | bytes 786436
  15.9 24.7 %all-to-all-start.1 = ((bf16[32,16,1024]{2,1,0:T(8,128)(2,1)}), bf16[32,16,1024]{2,1,0:T(8,128)(2,1)S(1)}, u32[]{:S(2)}, u32[]{:S(2)}) async-start(bf16[32,16,1024]{2,1,0:T(8,128)(2,1)} %bitcast.4), calls=%async_computation.1 | async-start | bytes 2097152 | tf_op jit(solution)/shard_map/all_to_all | solution.py:262
  40.6 20.8 %all-to-all-start = ((bf16[32,16,1024]{2,1,0:T(8,128)(2,1)}), bf16[32,16,1024]{2,1,0:T(8,128)(2,1)S(1)}, u32[]{:S(2)}, u32[]{:S(2)}) async-start(bf16[32,16,1024]{2,1,0:T(8,128)(2,1)} %bitcast.2), calls=%async_computation | async-start | bytes 2097152 | tf_op jit(solution)/shard_map/all_to_all | solution.py:261
  91.3 1.0 copy-start.2
  92.3 1.0 copy-start.4
  93.2 9.1 %copy-start.5 = (bf16[4,64,768]{2,1,0:T(8,128)(2,1)}, bf16[4,64,768]{2,1,0:T(8,128)(2,1)S(1)}, u32[]{:S(2)}) copy-start(bf16[4,64,768]{2,1,0:T(8,128)(2,1)S(1)} %get-tuple-element.20) | copy-start | bytes 1179652
  93.2 1.5 copy-start
  94.8 1.4 copy-start.1
  102.3 28.8 %copy-start.3 = (f32[4,64,768]{2,1,0:T(8,128)S(1)}, f32[4,64,768]{2,1,0:T(8,128)}, u32[]{:S(2)}) copy-start(f32[4,64,768]{2,1,0:T(8,128)} %copy-done.2) | copy-start | bytes 2359300
  102.3 77.5 %all-to-all-start.2 = ((bf16[32,16,2048]{2,1,0:T(8,128)(2,1)}), bf16[32,16,2048]{2,1,0:T(8,128)(2,1)S(1)}, u32[]{:S(2)}, u32[]{:S(2)}) async-start(bf16[32,16,2048]{2,1,0:T(8,128)(2,1)} %bitcast.52), calls=%async_computation.2 | async-start | bytes 4194304 | tf_op jit(solution)/shard_map/all_to_all | solution.py:273
  118.4 42.2 %copy-start.8 = (s32[128,2]{0,1:T(2,128)S(1)}, s32[128,2]{0,1:T(2,128)}, u32[]{:S(2)}) copy-start(s32[128,2]{0,1:T(2,128)} %param.13) | copy-start | bytes 3076
  118.4 12.6 %collective-permute-start = (bf16[4,64,768]{2,1,0:T(8,128)(2,1)}, bf16[4,64,768]{2,1,0:T(8,128)(2,1)S(1)}, u32[]{:S(2)}, u32[]{:S(2)}) collective-permute-start(bf16[4,64,768]{2,1,0:T(8,128)(2,1)} %copy-done.5), channel_id=1, source_target_pairs={{0,480},{32,0},{64,32},{96,64},{128,96},{160,128},{192,160},{224,1... | collective-permute-start | bytes 1179656 | tf_op jit(solution)/shard_map/ppermute | solution.py:213
  120.4 12.9 %collective-permute-start.2 = (bf16[4,64,768]{2,1,0:T(8,128)(2,1)S(1)}, bf16[4,64,768]{2,1,0:T(8,128)(2,1)}, u32[]{:S(2)}, u32[]{:S(2)}) collective-permute-start(bf16[4,64,768]{2,1,0:T(8,128)(2,1)S(1)} %get-tuple-element.22), channel_id=1, source_target_pairs={{0,32},{32,64},{64,96},{96,128},{128,160},{160,192},{192,224},{224... | collective-permute-start | bytes 1179656 | tf_op jit(solution)/shard_map/ppermute | solution.py:213
  131.2 11.9 %collective-permute-start.1 = (bf16[4,64,768]{2,1,0:T(8,128)(2,1)S(1)}, bf16[4,64,768]{2,1,0:T(8,128)(2,1)S(1)}, u32[]{:S(2)}, u32[]{:S(2)}) collective-permute-start(bf16[4,64,768]{2,1,0:T(8,128)(2,1)S(1)} %add_convert_fusion), channel_id=1, source_target_pairs={{0,480},{32,0},{64,32},{96,64},{128,96},{160,128},{192,160},{224,1... | collective-permute-start | bytes 1179656 | tf_op jit(solution)/shard_map/ppermute | solution.py:213
  144.4 17.1 %collective-permute-start.3 = (bf16[64,768]{1,0:T(8,128)(2,1)S(1)}, bf16[64,768]{1,0:T(8,128)(2,1)S(1)}, u32[]{:S(2)}, u32[]{:S(2)}) collective-permute-start(bf16[64,768]{1,0:T(8,128)(2,1)S(1)} %get-tuple-element.24), channel_id=1, source_target_pairs={{0,128},{32,160},{64,192},{96,224},{128,256},{160,288},{192,320},{... | collective-permute-start | bytes 294920 | tf_op jit(solution)/shard_map/ppermute | solution.py:213
  148.8 14.4 %collective-permute-start.4 = (bf16[64,768]{1,0:T(8,128)(2,1)S(1)}, bf16[64,768]{1,0:T(8,128)(2,1)S(1)}, u32[]{:S(2)}, u32[]{:S(2)}) collective-permute-start(bf16[64,768]{1,0:T(8,128)(2,1)S(1)} %get-tuple-element.26), channel_id=1, source_target_pairs={{0,256},{32,288},{64,320},{96,352},{128,384},{160,416},{192,448},{... | collective-permute-start | bytes 294920 | tf_op jit(solution)/shard_map/ppermute | solution.py:213
  155.7 22.3 %collective-permute-start.5 = (bf16[64,768]{1,0:T(8,128)(2,1)S(1)}, bf16[64,768]{1,0:T(8,128)(2,1)S(1)}, u32[]{:S(2)}, u32[]{:S(2)}) collective-permute-start(bf16[64,768]{1,0:T(8,128)(2,1)S(1)} %get-tuple-element.25), channel_id=1, source_target_pairs={{0,384},{32,416},{64,448},{96,480},{128,0},{160,32},{192,64},{224,... | collective-permute-start | bytes 294920 | tf_op jit(solution)/shard_map/ppermute | solution.py:213
Sparse Core Ops, SparseCore 0:
  10.1 73.8 all-gather.1

commit v7 on v5

--- a/solution.py
+++ b/solution.py
@@ -75,56 +75,76 @@
     )(place, rows, cot, mats, mats)
 
 
-def _back_kernel(hidden, cot, slope, activated, gate, up, down_mat, back, out_sum, cot_sum):
-    at = pl.program_id(0)
-    features = cot.shape[1]
-    down = down_mat[...]
-    hidden_cot = _dot(cot[...], down, (1, 0))
-    gate_cot = (hidden_cot * slope[...]).astype(jnp.bfloat16)
-    up_cot = (hidden_cot * activated[...]).astype(jnp.bfloat16)
-    out_part = _dot(hidden[...], down, (1, 1))
-    cot_part = _dot(gate_cot, gate[...], (1, 1)) + _dot(up_cot, up[...], (1, 1))
-
-    @pl.when(at == 0)
-    def _():
-        out_sum[...] = out_part
-        cot_sum[...] = cot_part
-
-    @pl.when(at > 0)
-    def _():
-        out_sum[...] += out_part
-        cot_sum[...] += cot_part
-
-    @pl.when(at == pl.num_programs(0) - 1)
-    def _():
-        back[:, :features] = out_sum[...].astype(jnp.bfloat16)
-        back[:, features:] = cot_sum[...].astype(jnp.bfloat16)
+def _back_kernel(
+    mats,
+    hidden_far,
+    slope_far,
+    activated_far,
+    cot,
+    back,
+    down,
+    hidden,
+    slope,
+    activated,
+    gate_up,
+    cots,
+    out_rows,
+    cot_rows,
+    sems,
+):
+    features, width = down.shape
+    sources = (
+        (mats.at[:, pl.ds(2 * width, width)], down),
+        (hidden_far, hidden),
+        (slope_far, slope),
+        (activated_far, activated),
+        (mats.at[:, pl.ds(0, 2 * width)], gate_up),
+    )
+    coming = [pltpu.make_async_copy(*pair, sems.at[k]) for k, pair in enumerate(sources)]
+    leaving = [
+        pltpu.make_async_copy(source, back.at[:, pl.ds(k * features, features)], sems.at[5 + k])
+        for k, source in enumerate((out_rows, cot_rows))
+    ]
+    for copy in coming:
+        copy.start()
+    coming[0].wait()
+    hidden_cot = _dot(cot[...], down[...], (1, 0))
+    coming[1].wait()
+    out_rows[...] = _dot(hidden[...], down[...], (1, 1)).astype(jnp.bfloat16)
+    leaving[0].start()
+    coming[2].wait()
+    coming[3].wait()
+    cots[:, :width] = (hidden_cot * slope[...]).astype(jnp.bfloat16)
+    cots[:, width:] = (hidden_cot * activated[...]).astype(jnp.bfloat16)
+    coming[4].wait()
+    cot_rows[...] = _dot(cots[...], gate_up[...], (1, 1)).astype(jnp.bfloat16)
+    leaving[1].start()
+    for copy in leaving:
+        copy.wait()
 
 
 def rows_back(hidden, cot, slope, activated, mats):
     slots, features = cot.shape
-    steps = hidden.shape[1] // BLOCK
-    column = pl.BlockSpec((slots, BLOCK), lambda j: (0, j))
+    width = hidden.shape[1]
+    far = pl.BlockSpec(memory_space=pltpu.HBM)
     return pl.pallas_call(
         _back_kernel,
-        grid=(steps,),
-        in_specs=[
-            column,
-            pl.BlockSpec(memory_space=pltpu.VMEM),
-            column,
-            column,
-            pl.BlockSpec((features, BLOCK), lambda j: (0, j)),
-            pl.BlockSpec((features, BLOCK), lambda j: (0, j + steps)),
-            pl.BlockSpec((features, BLOCK), lambda j: (0, j + 2 * steps)),
-        ],
-        out_specs=pl.BlockSpec((slots, 2 * features), lambda j: (0, 0)),
+        in_specs=[far, far, far, far, pl.BlockSpec(memory_space=pltpu.VMEM)],
+        out_specs=far,
         out_shape=jax.ShapeDtypeStruct((slots, 2 * features), jnp.bfloat16),
         scratch_shapes=[
-            pltpu.VMEM((slots, features), jnp.float32),
-            pltpu.VMEM((slots, features), jnp.float32),
+            pltpu.VMEM((features, width), jnp.bfloat16),
+            pltpu.VMEM((slots, width), jnp.bfloat16),
+            pltpu.VMEM((slots, width), jnp.float32),
+            pltpu.VMEM((slots, width), jnp.float32),
+            pltpu.VMEM((features, 2 * width), jnp.bfloat16),
+            pltpu.VMEM((slots, 2 * width), jnp.bfloat16),
+            pltpu.VMEM((slots, features), jnp.bfloat16),
+            pltpu.VMEM((slots, features), jnp.bfloat16),
+            pltpu.SemaphoreType.DMA((7,)),
         ],
         name="rows_back",
-    )(hidden, cot, slope, activated, mats, mats, mats)
+    )(mats, hidden, slope, activated, cot)
 
 
 def _beside_kernel(gate, up, down, out):

time: 187 us -> 186 us (level)
  no operation moved by 1% of the time
where the time goes in v7:
time: 186 us; the launch traced here: 185 us
  waiting for transfers between devices  87.2 us (47%)
  starting transfers between devices  51.6 us (28%)
  Pallas kernels  18.4 us (10%)
  between operations  14.2 us (8%)
  local copies, waits for them, and re-layouts  5.41 us (3%)
  other arithmetic  5.06 us (3%)
  matrix products  3.13 us (2%)
    ppermute x6, waiting for transfers between devices, moved(): lax.ppermute(value, 'dp', [(i, (i + by) % groups) for i in range(groups)])  33.1 us
    ppermute x6, starting transfers between devices, moved(): lax.ppermute(value, 'dp', [(i, (i + by) % groups) for i in range(groups)])  23.8 us
    all_gather x1, waiting for transfers between devices, per_device(): mats = lax.all_gather(shards, 'dp', axis=0, tiled=True)  22.9 us
    all_to_all x1, waiting for transfers between devices, per_device(): lax.all_to_all(send_input, 'expert', split_axis=0, concat_axis=0, tiled=T...  16.4 us
    all_to_all x1, starting transfers between devices, per_device(): lax.all_to_all(back_rows.reshape(owners, capacity, 2 * feature_count), 'e...  16.1 us
    all_to_all x1, waiting for transfers between devices, per_device(): lax.all_to_all(send_cot, 'expert', split_axis=0, concat_axis=0, tiled=True)  14.8 us
    all_to_all x1, starting transfers between devices, per_device(): lax.all_to_all(send_cot, 'expert', split_axis=0, concat_axis=0, tiled=True)  7.76 us
    pallas_call x1, Pallas kernels, rows_back(): pl.pallas_call(_back_kernel, in_specs=[far, far, far, far, pl.BlockSpec(m...  7.39 us
  transfers between devices with their start and end apart: 10, of which 7 were waited for; matrix products, arithmetic and copies ran while one was open for 7% of the time, Pallas kernels for 0%

profile of v7, /device:TPU:65, one launch (start us, length us, event | category | flops | bytes accessed | tf_op | source)
XLA Modules:
  0.0 185.1 jit_solution(11544226729729693858)
XLA Ops:
  7.2 0.0 all-gather.2.cloned.1.call-start
  7.2 1.7 side_by_side.1
  8.9 0.0 all-gather.2.cloned.1.call-update
  9.0 0.8 copy.25
  9.8 0.1 eq.42
  9.9 0.1 eq.38
  10.0 0.6 reduce-window.6
  10.6 0.2 slice_reduce_fusion
  10.9 0.8 copy.31.gates
  11.7 0.1 mul.39
  11.8 1.2 broadcast_in_dim.7
  13.0 0.7 convert_element_type.93
  13.8 0.1 fusion.12
  13.9 0.0 copy-start.2
  13.9 1.6 convolution_convert_fusion
  15.4 7.8 %all-to-all-start.1 = ((bf16[32,16,1024]{2,1,0:T(8,128)(2,1)}), bf16[32,16,1024]{2,1,0:T(8,128)(2,1)S(1)}, u32[]{:S(2)}, u32[]{:S(2)}) async-start(bf16[32,16,1024]{2,1,0:T(8,128)(2,1)} %bitcast.4), calls=%async_computation.1 | async-start | bytes 2097152 | tf_op jit(solution)/shard_map/all_to_all | solution.py:253
  23.2 0.3 broadcast_in_dim.6
  23.5 0.2 reshape.86
  23.7 1.6 convolution_convert_fusion.1
  25.3 14.8 %all-to-all-done.1 = bf16[32,16,1024]{2,1,0:T(8,128)(2,1)S(1)} async-done(((bf16[32,16,1024]{2,1,0:T(8,128)(2,1)}), bf16[32,16,1024]{2,1,0:T(8,128)(2,1)S(1)}, u32[]{:S(2)}, u32[]{:S(2)}) %all-to-all-start.1) | async-done | bytes 1048608 | tf_op jit(solution)/shard_map/all_to_all | solution.py:253
  40.1 3.9 %all-to-all-start = ((bf16[32,16,1024]{2,1,0:T(8,128)(2,1)}), bf16[32,16,1024]{2,1,0:T(8,128)(2,1)S(1)}, u32[]{:S(2)}, u32[]{:S(2)}) async-start(bf16[32,16,1024]{2,1,0:T(8,128)(2,1)} %bitcast.2), calls=%async_computation | async-start | bytes 2097152 | tf_op jit(solution)/shard_map/all_to_all | solution.py:252
  44.1 0.5 copy.30.cot
  44.6 16.4 %all-to-all-done = bf16[32,16,1024]{2,1,0:T(8,128)(2,1)S(1)} async-done(((bf16[32,16,1024]{2,1,0:T(8,128)(2,1)}), bf16[32,16,1024]{2,1,0:T(8,128)(2,1)S(1)}, u32[]{:S(2)}, u32[]{:S(2)}) %all-to-all-start) | async-done | bytes 1048608 | tf_op jit(solution)/shard_map/all_to_all | solution.py:252
  61.0 22.9 %all-gather.2.cloned.1.call-done.gate.up.mats = bf16[1024,2304]{1,0:T(8,128)(2,1)} async-done(((bf16[64,2304]{1,0:T(8,128)(2,1)}), bf16[1024,2304]{1,0:T(8,128)(2,1)}) %all-gather.2.cloned.1.call-update) | async-done | bytes 4718608 | tf_op jit(solution)/shard_map/all_gather | solution.py:258
  83.9 6.4 %hidden_and_partial.1 = (bf16[512,768]{1,0:T(8,128)(2,1)}, f32[512,768]{1,0:T(8,128)}, f32[512,768]{1,0:T(8,128)}, bf16[4,64,768]{2,1,0:T(8,128)(2,1)}, bf16[4,6...) custom-call(s32[1]{0:T(128)} %bitcast.1.place, bf16[512,1024]{1,0:T(8,128)(2,1)S(1)} %bitcast.51, ...), custom_call_target="tpu_custom_call" | custom-call | tf_op jit(solution)/shard_map/hidden_and_partial/pallas_call | solution.py:51
  90.3 7.4 %rows_back.1 = bf16[512,2048]{1,0:T(8,128)(2,1)} custom-call(bf16[1024,2304]{1,0:T(8,128)(2,1)} %all-gather.2.cloned.1.call-done.gate.up.mats, bf16[512,768]{1,0:T(8,128)(2,1)} %get-tuple-element.14.hidden_far, f32[512,768]{1,0:T(8,128)} %get-tuple-element.15.slope_far, f32[512,768]{1,0:T(8,128)} %get-tuple-element.16.activated_far, ...), custom_call_target="tpu_custom_call" | custom-call | tf_op jit(solution)/shard_map/rows_back/pallas_call | solution.py:130
  97.7 16.1 %all-to-all-start.2 = ((bf16[32,16,2048]{2,1,0:T(8,128)(2,1)}), bf16[32,16,2048]{2,1,0:T(8,128)(2,1)S(1)}, u32[]{:S(2)}, u32[]{:S(2)}) async-start(bf16[32,16,2048]{2,1,0:T(8,128)(2,1)} %bitcast.52), calls=%async_computation.2 | async-start | bytes 4194304 | tf_op jit(solution)/shard_map/all_to_all | solution.py:266
  113.8 0.0 copy-start.3
  113.8 1.9 %collective-permute-start = (bf16[4,64,768]{2,1,0:T(8,128)(2,1)}, bf16[4,64,768]{2,1,0:T(8,128)(2,1)S(1)}, u32[]{:S(2)}, u32[]{:S(2)}) collective-permute-start(bf16[4,64,768]{2,1,0:T(8,128)(2,1)} %get-tuple-element.20), channel_id=1, source_target_pairs={{0,480},{32,0},{64,32},{96,64},{128,96},{160,128},{192,160},{224,1... | collective-permute-start | bytes 1179656 | tf_op jit(solution)/shard_map/ppermute | solution.py:204
  115.8 3.4 %collective-permute-start.2 = (bf16[4,64,768]{2,1,0:T(8,128)(2,1)}, bf16[4,64,768]{2,1,0:T(8,128)(2,1)S(1)}, u32[]{:S(2)}, u32[]{:S(2)}) collective-permute-start(bf16[4,64,768]{2,1,0:T(8,128)(2,1)} %get-tuple-element.22), channel_id=1, source_target_pairs={{0,32},{32,64},{64,96},{96,128},{128,160},{160,192},{192,224},{224... | collective-permute-start | bytes 1179656 | tf_op jit(solution)/shard_map/ppermute | solution.py:204
  119.1 7.2 %collective-permute-done = bf16[4,64,768]{2,1,0:T(8,128)(2,1)S(1)} collective-permute-done((bf16[4,64,768]{2,1,0:T(8,128)(2,1)}, bf16[4,64,768]{2,1,0:T(8,128)(2,1)S(1)}, u32[]{:S(2)}, u32[]{:S(2)}) %collective-permute-start) | collective-permute-done | bytes 393248 | tf_op jit(solution)/shard_map/ppermute | solution.py:204
  126.4 0.1 add_convert_fusion
  126.5 2.1 %collective-permute-start.1 = (bf16[4,64,768]{2,1,0:T(8,128)(2,1)S(1)}, bf16[4,64,768]{2,1,0:T(8,128)(2,1)S(1)}, u32[]{:S(2)}, u32[]{:S(2)}) collective-permute-start(bf16[4,64,768]{2,1,0:T(8,128)(2,1)S(1)} %add_convert_fusion), channel_id=1, source_target_pairs={{0,480},{32,0},{64,32},{96,64},{128,96},{160,128},{192,160},{224,1... | collective-permute-start | bytes 1179656 | tf_op jit(solution)/shard_map/ppermute | solution.py:204
  128.6 0.0 collective-permute-done.2
  128.6 9.6 %collective-permute-done.1 = bf16[4,64,768]{2,1,0:T(8,128)(2,1)S(1)} collective-permute-done((bf16[4,64,768]{2,1,0:T(8,128)(2,1)S(1)}, bf16[4,64,768]{2,1,0:T(8,128)(2,1)S(1)}, u32[]{:S(2)}, u32[]{:S(2)}) %collective-permute-start.1) | collective-permute-done | bytes 393248 | tf_op jit(solution)/shard_map/ppermute | solution.py:204
  138.2 1.9 %fusion.7 = (bf16[64,768]{1,0:T(8,128)(2,1)}, bf16[64,768]{1,0:T(8,128)(2,1)S(1)}, bf16[64,768]{1,0:T(8,128)(2,1)S(1)}) fusion(f32[4,64,768]{2,1,0:T(8,128)} %get-tuple-element.23, bf16[4,64,768]{2,1,0:T(8,128)(2,1)S(1)} %collective-permute-done.2, bf16[4,64,768]{2,1,0:T(8,128)(2,1)S(1)} %collective-permute-done.1), kind=kLoop, calls=%fused_computation.16 | loop fusion | flops 737280 | bytes 1474560 | tf_op jit(solution)/shard_map/convert_element_type | solution.py:216
  140.1 4.8 %collective-permute-start.3 = (bf16[64,768]{1,0:T(8,128)(2,1)}, bf16[64,768]{1,0:T(8,128)(2,1)S(1)}, u32[]{:S(2)}, u32[]{:S(2)}) collective-permute-start(bf16[64,768]{1,0:T(8,128)(2,1)} %get-tuple-element.24), channel_id=1, source_target_pairs={{0,128},{32,160},{64,192},{96,224},{128,256},{160,288},{192,320},{... | collective-permute-start | bytes 294920 | tf_op jit(solution)/shard_map/ppermute | solution.py:204
  144.9 6.9 %collective-permute-start.4 = (bf16[64,768]{1,0:T(8,128)(2,1)S(1)}, bf16[64,768]{1,0:T(8,128)(2,1)S(1)}, u32[]{:S(2)}, u32[]{:S(2)}) collective-permute-start(bf16[64,768]{1,0:T(8,128)(2,1)S(1)} %get-tuple-element.26), channel_id=1, source_target_pairs={{0,256},{32,288},{64,320},{96,352},{128,384},{160,416},{192,448},{... | collective-permute-start | bytes 294920 | tf_op jit(solution)/shard_map/ppermute | solution.py:204
  151.9 4.6 %collective-permute-start.5 = (bf16[64,768]{1,0:T(8,128)(2,1)S(1)}, bf16[64,768]{1,0:T(8,128)(2,1)}, u32[]{:S(2)}, u32[]{:S(2)}) collective-permute-start(bf16[64,768]{1,0:T(8,128)(2,1)S(1)} %get-tuple-element.25), channel_id=1, source_target_pairs={{0,384},{32,416},{64,448},{96,480},{128,0},{160,32},{192,64},{224,... | collective-permute-start | bytes 294920 | tf_op jit(solution)/shard_map/ppermute | solution.py:204
  156.6 0.1 reduce_sum.12
  156.7 0.1 copy.28
  156.8 0.6 add.56.slot
  157.4 0.0 collective-permute-done.3
  157.4 1.9 %collective-permute-done.4 = bf16[64,768]{1,0:T(8,128)(2,1)S(1)} collective-permute-done((bf16[64,768]{1,0:T(8,128)(2,1)S(1)}, bf16[64,768]{1,0:T(8,128)(2,1)S(1)}, u32[]{:S(2)}, u32[]{:S(2)}) %collective-permute-start.4) | collective-permute-done | bytes 98336 | tf_op jit(solution)/shard_map/ppermute | solution.py:204
  159.3 14.3 %collective-permute-done.5 = bf16[64,768]{1,0:T(8,128)(2,1)} collective-permute-done((bf16[64,768]{1,0:T(8,128)(2,1)S(1)}, bf16[64,768]{1,0:T(8,128)(2,1)}, u32[]{:S(2)}, u32[]{:S(2)}) %collective-permute-start.5) | collective-permute-done | bytes 98336 | tf_op jit(solution)/shard_map/ppermute | solution.py:204
  173.7 1.7 fusion.6
  175.4 0.0 all-to-all-done.2
  175.4 2.8 %finish.1 = (bf16[128,1024]{1,0:T(8,128)(2,1)}, bf16[128,1024]{1,0:T(8,128)(2,1)}, f32[2,128]{1,0:T(2,128)}) custom-call(s32[128,2]{1,0:T(8,128)} %add.56.slot, f32[128,2]{1,0:T(8,128)} %copy-done.1, bf16[128,1024]{1,0:T(8,128)(2,1)} %second_out.1, bf16[128,1024]{1,0:T(8,128)(2,1)} %first_grad.1, bf16[128,1024]{1,0:T(8,128)(2,1)} %second_grad.1, ...), custom_call_target="tpu_custom_call" | custom-call | tf_op jit(solution)/shard_map/finish/pallas_call | solution.py:181
  (11 shorter events, 0.1 us)
Async XLA Ops:
  7.2 76.7 %all-gather.2.cloned.1.call-start = ((), (), s32[]{:S(2)}) async-start(), calls=%async_computation.3 | async-start | bytes 5013504 | tf_op jit(solution)/shard_map/all_gather | solution.py:258
  11.7 3.8 %copy-start.1 = (f32[128,2]{1,0:T(8,128)}, f32[128,2]{1,0:T(8,128)S(1)}, u32[]{:S(2)}) copy-start(f32[128,2]{1,0:T(8,128)S(1)} %copy.31.gates) | copy-start | bytes 3076
  13.9 9.3 %copy-start.2 = (bf16[128,1024]{1,0:T(8,128)(2,1)S(1)}, bf16[128,1024]{1,0:T(8,128)(2,1)}, u32[]{:S(2)}) copy-start(bf16[128,1024]{1,0:T(8,128)(2,1)} %param.9) | copy-start | bytes 786436
  15.4 24.7 %all-to-all-start.1 = ((bf16[32,16,1024]{2,1,0:T(8,128)(2,1)}), bf16[32,16,1024]{2,1,0:T(8,128)(2,1)S(1)}, u32[]{:S(2)}, u32[]{:S(2)}) async-start(bf16[32,16,1024]{2,1,0:T(8,128)(2,1)} %bitcast.4), calls=%async_computation.1 | async-start | bytes 2097152 | tf_op jit(solution)/shard_map/all_to_all | solution.py:253
  40.1 20.8 %all-to-all-start = ((bf16[32,16,1024]{2,1,0:T(8,128)(2,1)}), bf16[32,16,1024]{2,1,0:T(8,128)(2,1)S(1)}, u32[]{:S(2)}, u32[]{:S(2)}) async-start(bf16[32,16,1024]{2,1,0:T(8,128)(2,1)} %bitcast.2), calls=%async_computation | async-start | bytes 2097152 | tf_op jit(solution)/shard_map/all_to_all | solution.py:252
  97.7 28.7 %copy-start = (f32[4,64,768]{2,1,0:T(8,128)S(1)}, f32[4,64,768]{2,1,0:T(8,128)}, u32[]{:S(2)}) copy-start(f32[4,64,768]{2,1,0:T(8,128)} %get-tuple-element.21) | copy-start | bytes 2359300
  97.7 77.7 %all-to-all-start.2 = ((bf16[32,16,2048]{2,1,0:T(8,128)(2,1)}), bf16[32,16,2048]{2,1,0:T(8,128)(2,1)S(1)}, u32[]{:S(2)}, u32[]{:S(2)}) async-start(bf16[32,16,2048]{2,1,0:T(8,128)(2,1)} %bitcast.52), calls=%async_computation.2 | async-start | bytes 4194304 | tf_op jit(solution)/shard_map/all_to_all | solution.py:266
  113.8 42.7 %copy-start.3 = (s32[128,2]{0,1:T(2,128)S(1)}, s32[128,2]{0,1:T(2,128)}, u32[]{:S(2)}) copy-start(s32[128,2]{0,1:T(2,128)} %param.13) | copy-start | bytes 3076
  113.8 12.5 %collective-permute-start = (bf16[4,64,768]{2,1,0:T(8,128)(2,1)}, bf16[4,64,768]{2,1,0:T(8,128)(2,1)S(1)}, u32[]{:S(2)}, u32[]{:S(2)}) collective-permute-start(bf16[4,64,768]{2,1,0:T(8,128)(2,1)} %get-tuple-element.20), channel_id=1, source_target_pairs={{0,480},{32,0},{64,32},{96,64},{128,96},{160,128},{192,160},{224,1... | collective-permute-start | bytes 1179656 | tf_op jit(solution)/shard_map/ppermute | solution.py:204
  115.8 12.8 %collective-permute-start.2 = (bf16[4,64,768]{2,1,0:T(8,128)(2,1)}, bf16[4,64,768]{2,1,0:T(8,128)(2,1)S(1)}, u32[]{:S(2)}, u32[]{:S(2)}) collective-permute-start(bf16[4,64,768]{2,1,0:T(8,128)(2,1)} %get-tuple-element.22), channel_id=1, source_target_pairs={{0,32},{32,64},{64,96},{96,128},{128,160},{160,192},{192,224},{224... | collective-permute-start | bytes 1179656 | tf_op jit(solution)/shard_map/ppermute | solution.py:204
  126.5 11.8 %collective-permute-start.1 = (bf16[4,64,768]{2,1,0:T(8,128)(2,1)S(1)}, bf16[4,64,768]{2,1,0:T(8,128)(2,1)S(1)}, u32[]{:S(2)}, u32[]{:S(2)}) collective-permute-start(bf16[4,64,768]{2,1,0:T(8,128)(2,1)S(1)} %add_convert_fusion), channel_id=1, source_target_pairs={{0,480},{32,0},{64,32},{96,64},{128,96},{160,128},{192,160},{224,1... | collective-permute-start | bytes 1179656 | tf_op jit(solution)/shard_map/ppermute | solution.py:204
  140.1 17.4 %collective-permute-start.3 = (bf16[64,768]{1,0:T(8,128)(2,1)}, bf16[64,768]{1,0:T(8,128)(2,1)S(1)}, u32[]{:S(2)}, u32[]{:S(2)}) collective-permute-start(bf16[64,768]{1,0:T(8,128)(2,1)} %get-tuple-element.24), channel_id=1, source_target_pairs={{0,128},{32,160},{64,192},{96,224},{128,256},{160,288},{192,320},{... | collective-permute-start | bytes 294920 | tf_op jit(solution)/shard_map/ppermute | solution.py:204
  144.9 14.4 %collective-permute-start.4 = (bf16[64,768]{1,0:T(8,128)(2,1)S(1)}, bf16[64,768]{1,0:T(8,128)(2,1)S(1)}, u32[]{:S(2)}, u32[]{:S(2)}) collective-permute-start(bf16[64,768]{1,0:T(8,128)(2,1)S(1)} %get-tuple-element.26), channel_id=1, source_target_pairs={{0,256},{32,288},{64,320},{96,352},{128,384},{160,416},{192,448},{... | collective-permute-start | bytes 294920 | tf_op jit(solution)/shard_map/ppermute | solution.py:204
  151.9 21.8 %collective-permute-start.5 = (bf16[64,768]{1,0:T(8,128)(2,1)S(1)}, bf16[64,768]{1,0:T(8,128)(2,1)}, u32[]{:S(2)}, u32[]{:S(2)}) collective-permute-start(bf16[64,768]{1,0:T(8,128)(2,1)S(1)} %get-tuple-element.25), channel_id=1, source_target_pairs={{0,384},{32,416},{64,448},{96,480},{128,0},{160,32},{192,64},{224,... | collective-permute-start | bytes 294920 | tf_op jit(solution)/shard_map/ppermute | solution.py:204
Sparse Core Ops, SparseCore 0:
  10.1 73.7 all-gather.1

commit v8 on v7

--- a/solution.py
+++ b/solution.py
@@ -147,16 +147,26 @@
     )(mats, hidden, slope, activated, cot)
 
 
-def _beside_kernel(gate, up, down, out):
+def _beside_kernel(gate, up, down, out, sems):
     width = gate.shape[2]
-    for at, value in enumerate((gate, up, down)):
-        out[:, at * width : (at + 1) * width] = value[0]
+    copies = [
+        pltpu.make_async_copy(source.at[0], out.at[:, pl.ds(k * width, width)], sems.at[k])
+        for k, source in enumerate((gate, up, down))
+    ]
+    for copy in copies:
+        copy.start()
+    for copy in copies:
+        copy.wait()
 
 
 def side_by_side(gate, up, down):
+    far = pl.BlockSpec(memory_space=pltpu.HBM)
     return pl.pallas_call(
         _beside_kernel,
+        in_specs=[far] * 3,
+        out_specs=far,
         out_shape=jax.ShapeDtypeStruct((gate.shape[1], 3 * gate.shape[2]), gate.dtype),
+        scratch_shapes=[pltpu.SemaphoreType.DMA((3,))],
         name="side_by_side",
     )(gate, up, down)
 

time: 186 us -> 193 us (1.038)
  Pallas kernels: 18.4 us -> 26.7 us
    pallas_call x1, Pallas kernels: 1.73 us -> 10.1 us  [side_by_side(): pl.pallas_call(_beside_kernel, in_specs=[far] * 3, out_specs=far, out_sha...]
where the time goes in v8:
time: 193 us
  waiting for transfers between devices  86.5 us (45%)
  starting transfers between devices  51.5 us (27%)
  Pallas kernels  26.7 us (14%)
  between operations  14.3 us (7%)
  local copies, waits for them, and re-layouts  5.41 us (3%)
  other arithmetic  5.06 us (3%)
  matrix products  3.13 us (2%)
    ppermute x6, waiting for transfers between devices, moved(): lax.ppermute(value, 'dp', [(i, (i + by) % groups) for i in range(groups)])  33.2 us
    ppermute x6, starting transfers between devices, moved(): lax.ppermute(value, 'dp', [(i, (i + by) % groups) for i in range(groups)])  23.8 us
    all_gather x1, waiting for transfers between devices, per_device(): mats = lax.all_gather(shards, 'dp', axis=0, tiled=True)  22.1 us
    all_to_all x1, waiting for transfers between devices, per_device(): lax.all_to_all(send_input, 'expert', split_axis=0, concat_axis=0, tiled=T...  16.4 us
    all_to_all x1, starting transfers between devices, per_device(): lax.all_to_all(back_rows.reshape(owners, capacity, 2 * feature_count), 'e...  16 us
    all_to_all x1, waiting for transfers between devices, per_device(): lax.all_to_all(send_cot, 'expert', split_axis=0, concat_axis=0, tiled=True)  14.8 us
    pallas_call x1, Pallas kernels, side_by_side(): pl.pallas_call(_beside_kernel, in_specs=[far] * 3, out_specs=far, out_sha...  10.1 us
    all_to_all x1, starting transfers between devices, per_device(): lax.all_to_all(send_cot, 'expert', split_axis=0, concat_axis=0, tiled=True)  7.76 us
  transfers between devices with their start and end apart: 10, of which 7 were waited for; matrix products, arithmetic and copies ran while one was open for 7% of the time, Pallas kernels for 0%

profile of v8, /device:TPU:65, one launch (start us, length us, event | category | flops | bytes accessed | tf_op | source)
XLA Modules:
  0.0 192.6 jit_solution(7683832701631855928)
XLA Ops:
  7.2 0.0 all-gather.2.cloned.1.call-start
  7.2 10.1 %side_by_side.1 = bf16[64,2304]{1,0:T(8,128)(2,1)} custom-call(bf16[1,64,768]{2,1,0:T(8,128)(2,1)} %gate.1, bf16[1,64,768]{2,1,0:T(8,128)(2,1)} %up.1, bf16[1,64,768]{2,1,0:T(8,128)(2,1)} %down.1), custom_call_target="tpu_custom_call" | custom-call | tf_op jit(solution)/shard_map/side_by_side/pallas_call | solution.py:164
  17.3 0.0 all-gather.2.cloned.1.call-update
  17.3 0.8 copy.25
  18.1 0.1 eq.42
  18.2 0.1 eq.38
  18.4 0.6 reduce-window.6
  19.0 0.2 slice_reduce_fusion
  19.2 0.8 copy.31.gates
  20.0 0.1 mul.39
  20.1 1.2 broadcast_in_dim.7
  21.4 0.7 convert_element_type.93
  22.1 0.1 fusion.12
  22.2 0.0 copy-start.2
  22.2 1.6 convolution_convert_fusion
  23.8 7.8 %all-to-all-start.1 = ((bf16[32,16,1024]{2,1,0:T(8,128)(2,1)}), bf16[32,16,1024]{2,1,0:T(8,128)(2,1)S(1)}, u32[]{:S(2)}, u32[]{:S(2)}) async-start(bf16[32,16,1024]{2,1,0:T(8,128)(2,1)} %bitcast.4), calls=%async_computation.1 | async-start | bytes 2097152 | tf_op jit(solution)/shard_map/all_to_all | solution.py:263
  31.6 0.3 broadcast_in_dim.6
  31.8 0.2 reshape.86
  32.1 1.6 convolution_convert_fusion.1
  33.6 14.8 %all-to-all-done.1 = bf16[32,16,1024]{2,1,0:T(8,128)(2,1)S(1)} async-done(((bf16[32,16,1024]{2,1,0:T(8,128)(2,1)}), bf16[32,16,1024]{2,1,0:T(8,128)(2,1)S(1)}, u32[]{:S(2)}, u32[]{:S(2)}) %all-to-all-start.1) | async-done | bytes 1048608 | tf_op jit(solution)/shard_map/all_to_all | solution.py:263
  48.5 3.9 %all-to-all-start = ((bf16[32,16,1024]{2,1,0:T(8,128)(2,1)}), bf16[32,16,1024]{2,1,0:T(8,128)(2,1)S(1)}, u32[]{:S(2)}, u32[]{:S(2)}) async-start(bf16[32,16,1024]{2,1,0:T(8,128)(2,1)} %bitcast.2), calls=%async_computation | async-start | bytes 2097152 | tf_op jit(solution)/shard_map/all_to_all | solution.py:262
  52.4 0.5 copy.30.cot
  53.0 16.4 %all-to-all-done = bf16[32,16,1024]{2,1,0:T(8,128)(2,1)S(1)} async-done(((bf16[32,16,1024]{2,1,0:T(8,128)(2,1)}), bf16[32,16,1024]{2,1,0:T(8,128)(2,1)S(1)}, u32[]{:S(2)}, u32[]{:S(2)}) %all-to-all-start) | async-done | bytes 1048608 | tf_op jit(solution)/shard_map/all_to_all | solution.py:262
  69.3 22.1 %all-gather.2.cloned.1.call-done.gate.up.mats = bf16[1024,2304]{1,0:T(8,128)(2,1)} async-done(((bf16[64,2304]{1,0:T(8,128)(2,1)}), bf16[1024,2304]{1,0:T(8,128)(2,1)}) %all-gather.2.cloned.1.call-update) | async-done | bytes 4718608 | tf_op jit(solution)/shard_map/all_gather | solution.py:268
  91.4 6.4 %hidden_and_partial.1 = (bf16[512,768]{1,0:T(8,128)(2,1)}, f32[512,768]{1,0:T(8,128)}, f32[512,768]{1,0:T(8,128)}, bf16[4,64,768]{2,1,0:T(8,128)(2,1)}, bf16[4,6...) custom-call(s32[1]{0:T(128)} %bitcast.1.place, bf16[512,1024]{1,0:T(8,128)(2,1)S(1)} %bitcast.51, ...), custom_call_target="tpu_custom_call" | custom-call | tf_op jit(solution)/shard_map/hidden_and_partial/pallas_call | solution.py:51
  97.8 7.4 %rows_back.1 = bf16[512,2048]{1,0:T(8,128)(2,1)} custom-call(bf16[1024,2304]{1,0:T(8,128)(2,1)} %all-gather.2.cloned.1.call-done.gate.up.mats, bf16[512,768]{1,0:T(8,128)(2,1)} %get-tuple-element.14.hidden_far, f32[512,768]{1,0:T(8,128)} %get-tuple-element.15.slope_far, f32[512,768]{1,0:T(8,128)} %get-tuple-element.16.activated_far, ...), custom_call_target="tpu_custom_call" | custom-call | tf_op jit(solution)/shard_map/rows_back/pallas_call | solution.py:130
  105.2 16.0 %all-to-all-start.2 = ((bf16[32,16,2048]{2,1,0:T(8,128)(2,1)}), bf16[32,16,2048]{2,1,0:T(8,128)(2,1)S(1)}, u32[]{:S(2)}, u32[]{:S(2)}) async-start(bf16[32,16,2048]{2,1,0:T(8,128)(2,1)} %bitcast.52), calls=%async_computation.2 | async-start | bytes 4194304 | tf_op jit(solution)/shard_map/all_to_all | solution.py:276
  121.2 0.0 copy-start.3
  121.2 1.9 collective-permute-start
  123.1 3.4 %collective-permute-start.2 = (bf16[4,64,768]{2,1,0:T(8,128)(2,1)}, bf16[4,64,768]{2,1,0:T(8,128)(2,1)S(1)}, u32[]{:S(2)}, u32[]{:S(2)}) collective-permute-start(bf16[4,64,768]{2,1,0:T(8,128)(2,1)} %get-tuple-element.22), channel_id=1, source_target_pairs={{0,32},{32,64},{64,96},{96,128},{128,160},{160,192},{192,224},{224... | collective-permute-start | bytes 1179656 | tf_op jit(solution)/shard_map/ppermute | solution.py:214
  126.5 7.2 %collective-permute-done = bf16[4,64,768]{2,1,0:T(8,128)(2,1)S(1)} collective-permute-done((bf16[4,64,768]{2,1,0:T(8,128)(2,1)}, bf16[4,64,768]{2,1,0:T(8,128)(2,1)S(1)}, u32[]{:S(2)}, u32[]{:S(2)}) %collective-permute-start) | collective-permute-done | bytes 393248 | tf_op jit(solution)/shard_map/ppermute | solution.py:214
  133.8 0.1 add_convert_fusion
  133.8 2.1 %collective-permute-start.1 = (bf16[4,64,768]{2,1,0:T(8,128)(2,1)S(1)}, bf16[4,64,768]{2,1,0:T(8,128)(2,1)S(1)}, u32[]{:S(2)}, u32[]{:S(2)}) collective-permute-start(bf16[4,64,768]{2,1,0:T(8,128)(2,1)S(1)} %add_convert_fusion), channel_id=1, source_target_pairs={{0,480},{32,0},{64,32},{96,64},{128,96},{160,128},{192,160},{224,1... | collective-permute-start | bytes 1179656 | tf_op jit(solution)/shard_map/ppermute | solution.py:214
  136.0 0.0 collective-permute-done.2
  136.0 9.7 %collective-permute-done.1 = bf16[4,64,768]{2,1,0:T(8,128)(2,1)S(1)} collective-permute-done((bf16[4,64,768]{2,1,0:T(8,128)(2,1)S(1)}, bf16[4,64,768]{2,1,0:T(8,128)(2,1)S(1)}, u32[]{:S(2)}, u32[]{:S(2)}) %collective-permute-start.1) | collective-permute-done | bytes 393248 | tf_op jit(solution)/shard_map/ppermute | solution.py:214
  145.7 1.9 fusion.7
  147.6 4.8 %collective-permute-start.3 = (bf16[64,768]{1,0:T(8,128)(2,1)}, bf16[64,768]{1,0:T(8,128)(2,1)S(1)}, u32[]{:S(2)}, u32[]{:S(2)}) collective-permute-start(bf16[64,768]{1,0:T(8,128)(2,1)} %get-tuple-element.24), channel_id=1, source_target_pairs={{0,128},{32,160},{64,192},{96,224},{128,256},{160,288},{192,320},{... | collective-permute-start | bytes 294920 | tf_op jit(solution)/shard_map/ppermute | solution.py:214
  152.4 6.8 %collective-permute-start.4 = (bf16[64,768]{1,0:T(8,128)(2,1)S(1)}, bf16[64,768]{1,0:T(8,128)(2,1)S(1)}, u32[]{:S(2)}, u32[]{:S(2)}) collective-permute-start(bf16[64,768]{1,0:T(8,128)(2,1)S(1)} %get-tuple-element.26), channel_id=1, source_target_pairs={{0,256},{32,288},{64,320},{96,352},{128,384},{160,416},{192,448},{... | collective-permute-start | bytes 294920 | tf_op jit(solution)/shard_map/ppermute | solution.py:214
  159.2 4.8 %collective-permute-start.5 = (bf16[64,768]{1,0:T(8,128)(2,1)S(1)}, bf16[64,768]{1,0:T(8,128)(2,1)}, u32[]{:S(2)}, u32[]{:S(2)}) collective-permute-start(bf16[64,768]{1,0:T(8,128)(2,1)S(1)} %get-tuple-element.25), channel_id=1, source_target_pairs={{0,384},{32,416},{64,448},{96,480},{128,0},{160,32},{192,64},{224,... | collective-permute-start | bytes 294920 | tf_op jit(solution)/shard_map/ppermute | solution.py:214
  164.0 0.1 reduce_sum.12
  164.2 0.1 copy.28
  164.3 0.6 add.56.slot
  164.9 0.0 collective-permute-done.3
  164.9 2.0 %collective-permute-done.4 = bf16[64,768]{1,0:T(8,128)(2,1)S(1)} collective-permute-done((bf16[64,768]{1,0:T(8,128)(2,1)S(1)}, bf16[64,768]{1,0:T(8,128)(2,1)S(1)}, u32[]{:S(2)}, u32[]{:S(2)}) %collective-permute-start.4) | collective-permute-done | bytes 98336 | tf_op jit(solution)/shard_map/ppermute | solution.py:214
  166.9 14.3 %collective-permute-done.5 = bf16[64,768]{1,0:T(8,128)(2,1)} collective-permute-done((bf16[64,768]{1,0:T(8,128)(2,1)S(1)}, bf16[64,768]{1,0:T(8,128)(2,1)}, u32[]{:S(2)}, u32[]{:S(2)}) %collective-permute-start.5) | collective-permute-done | bytes 98336 | tf_op jit(solution)/shard_map/ppermute | solution.py:214
  181.1 1.7 fusion.6
  182.9 0.0 all-to-all-done.2
  182.9 2.8 %finish.1 = (bf16[128,1024]{1,0:T(8,128)(2,1)}, bf16[128,1024]{1,0:T(8,128)(2,1)}, f32[2,128]{1,0:T(2,128)}) custom-call(s32[128,2]{1,0:T(8,128)} %add.56.slot, f32[128,2]{1,0:T(8,128)} %copy-done.1, bf16[128,1024]{1,0:T(8,128)(2,1)} %second_out.1, bf16[128,1024]{1,0:T(8,128)(2,1)} %first_grad.1, bf16[128,1024]{1,0:T(8,128)(2,1)} %second_grad.1, ...), custom_call_target="tpu_custom_call" | custom-call | tf_op jit(solution)/shard_map/finish/pallas_call | solution.py:191
  (11 shorter events, 0.1 us)
Async XLA Ops:
  7.2 84.2 %all-gather.2.cloned.1.call-start = ((), (), s32[]{:S(2)}) async-start(), calls=%async_computation.3 | async-start | bytes 5013504 | tf_op jit(solution)/shard_map/all_gather | solution.py:268
  20.0 3.8 %copy-start.1 = (f32[128,2]{1,0:T(8,128)}, f32[128,2]{1,0:T(8,128)S(1)}, u32[]{:S(2)}) copy-start(f32[128,2]{1,0:T(8,128)S(1)} %copy.31.gates) | copy-start | bytes 3076
  22.2 9.3 %copy-start.2 = (bf16[128,1024]{1,0:T(8,128)(2,1)S(1)}, bf16[128,1024]{1,0:T(8,128)(2,1)}, u32[]{:S(2)}) copy-start(bf16[128,1024]{1,0:T(8,128)(2,1)} %param.9) | copy-start | bytes 786436
  23.8 24.7 %all-to-all-start.1 = ((bf16[32,16,1024]{2,1,0:T(8,128)(2,1)}), bf16[32,16,1024]{2,1,0:T(8,128)(2,1)S(1)}, u32[]{:S(2)}, u32[]{:S(2)}) async-start(bf16[32,16,1024]{2,1,0:T(8,128)(2,1)} %bitcast.4), calls=%async_computation.1 | async-start | bytes 2097152 | tf_op jit(solution)/shard_map/all_to_all | solution.py:263
  48.5 20.8 %all-to-all-start = ((bf16[32,16,1024]{2,1,0:T(8,128)(2,1)}), bf16[32,16,1024]{2,1,0:T(8,128)(2,1)S(1)}, u32[]{:S(2)}, u32[]{:S(2)}) async-start(bf16[32,16,1024]{2,1,0:T(8,128)(2,1)} %bitcast.2), calls=%async_computation | async-start | bytes 2097152 | tf_op jit(solution)/shard_map/all_to_all | solution.py:262
  105.2 28.6 %copy-start = (f32[4,64,768]{2,1,0:T(8,128)S(1)}, f32[4,64,768]{2,1,0:T(8,128)}, u32[]{:S(2)}) copy-start(f32[4,64,768]{2,1,0:T(8,128)} %get-tuple-element.21) | copy-start | bytes 2359300
  105.2 77.7 %all-to-all-start.2 = ((bf16[32,16,2048]{2,1,0:T(8,128)(2,1)}), bf16[32,16,2048]{2,1,0:T(8,128)(2,1)S(1)}, u32[]{:S(2)}, u32[]{:S(2)}) async-start(bf16[32,16,2048]{2,1,0:T(8,128)(2,1)} %bitcast.52), calls=%async_computation.2 | async-start | bytes 4194304 | tf_op jit(solution)/shard_map/all_to_all | solution.py:276
  121.2 42.8 %copy-start.3 = (s32[128,2]{0,1:T(2,128)S(1)}, s32[128,2]{0,1:T(2,128)}, u32[]{:S(2)}) copy-start(s32[128,2]{0,1:T(2,128)} %param.13) | copy-start | bytes 3076
  121.2 12.5 %collective-permute-start = (bf16[4,64,768]{2,1,0:T(8,128)(2,1)}, bf16[4,64,768]{2,1,0:T(8,128)(2,1)S(1)}, u32[]{:S(2)}, u32[]{:S(2)}) collective-permute-start(bf16[4,64,768]{2,1,0:T(8,128)(2,1)} %get-tuple-element.20), channel_id=1, source_target_pairs={{0,480},{32,0},{64,32},{96,64},{128,96},{160,128},{192,160},{224,1... | collective-permute-start | bytes 1179656 | tf_op jit(solution)/shard_map/ppermute | solution.py:214
  123.1 12.8 %collective-permute-start.2 = (bf16[4,64,768]{2,1,0:T(8,128)(2,1)}, bf16[4,64,768]{2,1,0:T(8,128)(2,1)S(1)}, u32[]{:S(2)}, u32[]{:S(2)}) collective-permute-start(bf16[4,64,768]{2,1,0:T(8,128)(2,1)} %get-tuple-element.22), channel_id=1, source_target_pairs={{0,32},{32,64},{64,96},{96,128},{128,160},{160,192},{192,224},{224... | collective-permute-start | bytes 1179656 | tf_op jit(solution)/shard_map/ppermute | solution.py:214
  133.8 11.9 %collective-permute-start.1 = (bf16[4,64,768]{2,1,0:T(8,128)(2,1)S(1)}, bf16[4,64,768]{2,1,0:T(8,128)(2,1)S(1)}, u32[]{:S(2)}, u32[]{:S(2)}) collective-permute-start(bf16[4,64,768]{2,1,0:T(8,128)(2,1)S(1)} %add_convert_fusion), channel_id=1, source_target_pairs={{0,480},{32,0},{64,32},{96,64},{128,96},{160,128},{192,160},{224,1... | collective-permute-start | bytes 1179656 | tf_op jit(solution)/shard_map/ppermute | solution.py:214
  147.6 17.4 %collective-permute-start.3 = (bf16[64,768]{1,0:T(8,128)(2,1)}, bf16[64,768]{1,0:T(8,128)(2,1)S(1)}, u32[]{:S(2)}, u32[]{:S(2)}) collective-permute-start(bf16[64,768]{1,0:T(8,128)(2,1)} %get-tuple-element.24), channel_id=1, source_target_pairs={{0,128},{32,160},{64,192},{96,224},{128,256},{160,288},{192,320},{... | collective-permute-start | bytes 294920 | tf_op jit(solution)/shard_map/ppermute | solution.py:214
  152.4 14.5 %collective-permute-start.4 = (bf16[64,768]{1,0:T(8,128)(2,1)S(1)}, bf16[64,768]{1,0:T(8,128)(2,1)S(1)}, u32[]{:S(2)}, u32[]{:S(2)}) collective-permute-start(bf16[64,768]{1,0:T(8,128)(2,1)S(1)} %get-tuple-element.26), channel_id=1, source_target_pairs={{0,256},{32,288},{64,320},{96,352},{128,384},{160,416},{192,448},{... | collective-permute-start | bytes 294920 | tf_op jit(solution)/shard_map/ppermute | solution.py:214
  159.2 21.9 %collective-permute-start.5 = (bf16[64,768]{1,0:T(8,128)(2,1)S(1)}, bf16[64,768]{1,0:T(8,128)(2,1)}, u32[]{:S(2)}, u32[]{:S(2)}) collective-permute-start(bf16[64,768]{1,0:T(8,128)(2,1)S(1)} %get-tuple-element.25), channel_id=1, source_target_pairs={{0,384},{32,416},{64,448},{96,480},{128,0},{160,32},{192,64},{224,... | collective-permute-start | bytes 294920 | tf_op jit(solution)/shard_map/ppermute | solution.py:214
Sparse Core Ops, SparseCore 0:
  17.4 73.8 all-gather.1
